TPU v7x, 32 devices: a whole 2x2x4 slice. The times are simulated.
32 devices in a mesh: fsdp: 2 (over core), ctx: 4 (over z), tp: 4 (over y, x).
Axes of the slice: x: 2, y: 2, z: 4, core: 2. Of those that a mesh axis runs over, the one named last changes fastest.
Arguments:
- hidden_in: bfloat16 [8, 512, 2048], P('fsdp', 'ctx'), may hold values from -6 to 6
- seq_lengths: int32 [8], P('fsdp'), may hold values from 128 to 512, as said below
- mixer_gain: float32 [2048], replicated, may hold values from 0.5 to 1.5
- feed_gain: float32 [2048], replicated, may hold values from 0.5 to 1.5
- query_weight: bfloat16 [2048, 2048], P('fsdp', 'tp'), may hold values from -0.125 to 0.125
- key_weight: bfloat16 [2048, 2048], P('fsdp', 'tp'), may hold values from -0.125 to 0.125
- value_weight: bfloat16 [2048, 2048], P('fsdp', 'tp'), may hold values from -0.125 to 0.125
- rate_weight: bfloat16 [2048, 16], P('fsdp', 'tp'), may hold values from -0.125 to 0.125
- query_conv: float32 [4, 2048], P(None, 'tp'), may hold values from -3 to 3
- key_conv: float32 [4, 2048], P(None, 'tp'), may hold values from -3 to 3
- value_conv: float32 [4, 2048], P(None, 'tp'), may hold values from -3 to 3
- head_gain: float32 [128], replicated, may hold values from 0.5 to 1.5
- output_weight: bfloat16 [2048, 2048], P('tp', 'fsdp'), may hold values from -0.125 to 0.125
- gate_weight: bfloat16 [2048, 5632], P('fsdp', 'tp'), may hold values from -0.125 to 0.125
- up_weight: bfloat16 [2048, 5632], P('fsdp', 'tp'), may hold values from -0.125 to 0.125
- down_weight: bfloat16 [5632, 2048], P('tp', 'fsdp'), may hold values from -0.078125 to 0.078125
- query_left: bfloat16 [2048, 16], P(None, 'fsdp'), may hold values from -0.125 to 0.125
- query_right: bfloat16 [16, 2048], P('fsdp', 'tp'), may hold values from -1.5 to 1.5
- key_left: bfloat16 [2048, 16], P(None, 'fsdp'), may hold values from -0.125 to 0.125
- key_right: bfloat16 [16, 2048], P('fsdp', 'tp'), may hold values from -1.5 to 1.5
- value_left: bfloat16 [2048, 16], P(None, 'fsdp'), may hold values from -0.125 to 0.125
- value_right: bfloat16 [16, 2048], P('fsdp', 'tp'), may hold values from -1.5 to 1.5
- rate_left: bfloat16 [2048, 16], P(None, 'fsdp'), may hold values from -0.125 to 0.125
- rate_right: bfloat16 [16, 16], P('fsdp', 'tp'), may hold values from -1.5 to 1.5
- output_left: bfloat16 [2048, 16], P('tp', 'fsdp'), may hold values from -0.125 to 0.125
- output_right: bfloat16 [16, 2048], P('fsdp'), may hold values from -1.5 to 1.5
- gate_left: bfloat16 [2048, 16], P(None, 'fsdp'), may hold values from -0.125 to 0.125
- gate_right: bfloat16 [16, 5632], P('fsdp', 'tp'), may hold values from -1.5 to 1.5
- up_left: bfloat16 [2048, 16], P(None, 'fsdp'), may hold values from -0.125 to 0.125
- up_right: bfloat16 [16, 5632], P('fsdp', 'tp'), may hold values from -1.5 to 1.5
- down_left: bfloat16 [5632, 16], P('tp', 'fsdp'), may hold values from -0.078125 to 0.078125
- down_right: bfloat16 [16, 2048], P('fsdp'), may hold values from -1.5 to 1.5
- output_grad: bfloat16 [8, 512, 2048], P('fsdp', 'ctx'), may hold values from -6 to 6
Outputs:
- block_out: bfloat16 [8, 512, 2048], P('fsdp', 'ctx')
- input_grad: bfloat16 [8, 512, 2048], P('fsdp', 'ctx')
- query_left_grad: float32 [2048, 16], P(None, 'fsdp')
- query_right_grad: float32 [16, 2048], P('fsdp', 'tp')
- key_left_grad: float32 [2048, 16], P(None, 'fsdp')
- key_right_grad: float32 [16, 2048], P('fsdp', 'tp')
- value_left_grad: float32 [2048, 16], P(None, 'fsdp')
- value_right_grad: float32 [16, 2048], P('fsdp', 'tp')
- rate_left_grad: float32 [2048, 16], P(None, 'fsdp')
- rate_right_grad: float32 [16, 16], P('fsdp', 'tp')
- output_left_grad: float32 [2048, 16], P('tp', 'fsdp')
- output_right_grad: float32 [16, 2048], P('fsdp')
- gate_left_grad: float32 [2048, 16], P(None, 'fsdp')
- gate_right_grad: float32 [16, 5632], P('fsdp', 'tp')
- up_left_grad: float32 [2048, 16], P(None, 'fsdp')
- up_right_grad: float32 [16, 5632], P('fsdp', 'tp')
- down_left_grad: float32 [5632, 16], P('tp', 'fsdp')
- down_right_grad: float32 [16, 2048], P('fsdp')
Inputs may be any that keep to these rules, and one draw needn't show every extreme that they name: `seq_lengths`: valid positions of each sequence, the rest padding; some sequence in every draw has all 512.
All inputs are finite; a program needn't handle non-finite values.
Results may differ from a plain program's by a relative error of at most 0.025.
Values may be sent and summed in bfloat16 or wider, within the bound.
A program may use at most 256 MiB of HBM per device.

v0:
```python
from functools import partial

import jax
import jax.numpy as jnp
from jax import lax
from jax.sharding import PartitionSpec as P

CONV = 4
GROUP = 64


adapter_scale = 0.5
epsilon = 1e-06


def from_behind(block, axis, distance):
    devices = range(lax.axis_size(axis))
    route = [(i - distance, i) for i in devices if i - distance in devices]
    return lax.ppermute(block, axis, route)


def entering(value, axis, join, neutral):
    place = lax.axis_index(axis)
    gathered = jax.tree.map(
        lambda a, kind: lax.all_gather(a.astype(kind), axis), value, (jnp.bfloat16, jnp.bfloat16)
    )
    state = jax.tree.map(lambda a, e: jnp.zeros_like(a) + jnp.asarray(e, a.dtype), value, neutral)

    def one(step, state):
        return join(
            state,
            jax.tree.map(
                lambda a, own: lax.dynamic_index_in_dim(a, step, 0, False).astype(own.dtype),
                gathered,
                value,
            ),
        )

    return lax.fori_loop(0, place, one, state)


def entering_2(value, axis, combine, identity):
    size, place = (lax.axis_size(axis), lax.axis_index(axis))
    everything = jax.tree.map(
        lambda part, kind: lax.all_gather(part.astype(kind), axis),
        value,
        jax.tree.map(lambda a: jnp.bfloat16 if a.dtype == jnp.float32 else a.dtype, value),
    )
    start = jax.tree.map(
        lambda part, zero: jnp.broadcast_to(jnp.asarray(zero, part.dtype), part.shape),
        value,
        identity,
    )

    def step(k, before):
        at = size - 1 - k
        reached = at > place
        new = combine(
            before, jax.tree.map(lambda part, own: part[at].astype(own.dtype), everything, value)
        )
        return jax.tree.map(lambda a, b: jnp.where(reached, a, b), new, before)

    return lax.fori_loop(0, size, step, start)


def for_sending(value):

    def short(part):
        return part.astype(jnp.bfloat16) if part.dtype == jnp.float32 else part

    return jax.tree.map(short, value)


def precise(form, left_side, right_side):
    return jnp.einsum(form, left_side, right_side, precision=lax.Precision.HIGHEST)


def matmul(left_side, right_side):
    return jnp.dot(left_side, right_side, preferred_element_type=jnp.float32)


def times_transposed(left_side, right_side):
    return lax.dot_general(
        left_side, right_side, (((1,), (1,)), ((), ())), preferred_element_type=jnp.float32
    )


def transposed_times(left_side, right_side):
    return lax.dot_general(
        left_side, right_side, (((0,), (0,)), ((), ())), preferred_element_type=jnp.float32
    )


def scaled_norm(values_in, scale_gain):
    return (
        values_in
        * lax.rsqrt(jnp.mean(values_in * values_in, axis=-1, keepdims=True) + epsilon)
        * scale_gain
    )


def unit_norm(values_in):
    return values_in * lax.rsqrt(jnp.sum(values_in * values_in, axis=-1, keepdims=True) + epsilon)


def project(rows_low, frozen, into, back_out):
    inner = matmul(rows_low, into).astype(jnp.bfloat16)
    return (matmul(rows_low, frozen) + adapter_scale * matmul(inner, back_out), inner)


def split_blocks(stacked):
    return jnp.moveaxis(
        stacked.reshape((stacked.shape[0], stacked.shape[1] // GROUP, GROUP) + stacked.shape[2:]),
        1,
        0,
    )


def join_blocks(stacked):
    moved = jnp.moveaxis(stacked, 0, 1)
    return moved.reshape((moved.shape[0], moved.shape[1] * GROUP) + moved.shape[3:])


def block_solve(key_block, value_block, rate_block):
    strict = jnp.tril(jnp.ones((GROUP, GROUP), jnp.float32), -1)
    system = jnp.eye(GROUP, dtype=jnp.float32) + strict * rate_block[:, :, None] * precise(
        "bid,bjd->bij", key_block, key_block
    )
    weighted_keys = lax.linalg.triangular_solve(
        system, rate_block[:, :, None] * key_block, left_side=True, lower=True, unit_diagonal=True
    )
    weighted_values = lax.linalg.triangular_solve(
        system, rate_block[:, :, None] * value_block, left_side=True, lower=True, unit_diagonal=True
    )
    return (weighted_keys, weighted_values)


def block_summary(queries, key_rows, value_rows, rate_rows, eye_state, zero_state):
    causal = jnp.tril(jnp.ones((GROUP, GROUP), jnp.float32))

    def advance(carry, block):
        carry_state, carried_map = carry
        query_block, key_block, value_block, rate_block = block
        weighted_keys, weighted_values = block_solve(key_block, value_block, rate_block)
        fresh_values = weighted_values - precise("bid,bde->bie", weighted_keys, carry_state)
        scores = causal * precise("bid,bjd->bij", query_block, key_block)
        local_outs = precise("bid,bde->bie", query_block, carry_state) + precise(
            "bij,bje->bie", scores, fresh_values
        )
        reaching = query_block - precise("bij,bjd->bid", scores, weighted_keys)
        reaching = precise("bid,bde->bie", reaching, carried_map)
        step_map = eye_state - precise("bid,bie->bde", key_block, weighted_keys)
        carry_state = carry_state + precise("bid,bie->bde", key_block, fresh_values)
        carried_map = precise("bde,bef->bdf", step_map, carried_map)
        return ((carry_state, carried_map), (local_outs, reaching))

    blocked = (
        split_blocks(queries),
        split_blocks(key_rows),
        split_blocks(value_rows),
        split_blocks(rate_rows),
    )
    (end_state, end_map), (local_outs, reaching) = lax.scan(
        advance, (zero_state, eye_state), blocked
    )
    return (end_map, end_state, join_blocks(local_outs), join_blocks(reaching))


def block_run(queries, key_rows, value_rows, rate_rows, start_state):
    causal = jnp.tril(jnp.ones((GROUP, GROUP), jnp.float32))

    def advance(carry_state, block):
        query_block, key_block, value_block, rate_block = block
        weighted_keys, weighted_values = block_solve(key_block, value_block, rate_block)
        fresh_values = weighted_values - precise("bid,bde->bie", weighted_keys, carry_state)
        scores = causal * precise("bid,bjd->bij", query_block, key_block)
        block_outs = precise("bid,bde->bie", query_block, carry_state) + precise(
            "bij,bje->bie", scores, fresh_values
        )
        return (carry_state + precise("bid,bie->bde", key_block, fresh_values), block_outs)

    blocked = (
        split_blocks(queries),
        split_blocks(key_rows),
        split_blocks(value_rows),
        split_blocks(rate_rows),
    )
    end_state, block_outs = lax.scan(advance, start_state, blocked)
    return (join_blocks(block_outs), end_state)


def compose(earlier, later):
    return (
        precise("bde,bef->bdf", later[0], earlier[0]),
        precise("bde,bef->bdf", later[0], earlier[1]) + later[1],
    )


def local(
    hidden_in,
    seq_lengths,
    mixer_gain,
    feed_gain,
    query_weight,
    key_weight,
    value_weight,
    rate_weight,
    query_conv,
    key_conv,
    value_conv,
    head_gain,
    output_weight,
    gate_weight,
    up_weight,
    down_weight,
    query_left,
    query_right,
    key_left,
    key_right,
    value_left,
    value_right,
    rate_left,
    rate_right,
    output_left,
    output_right,
    gate_left,
    gate_right,
    up_left,
    up_right,
    down_left,
    down_right,
    output_grad,
):
    seq_count, slot_count, model_width = hidden_in.shape
    total_rows = seq_count * slot_count
    heads_here = rate_weight.shape[1]
    head_width = head_gain.shape[0]
    local_cols = heads_here * head_width
    state_batch = seq_count * heads_here
    fetched = (
        lax.all_gather(query_weight, "fsdp", axis=0, tiled=True),
        lax.all_gather(key_weight, "fsdp", axis=0, tiled=True),
        lax.all_gather(value_weight, "fsdp", axis=0, tiled=True),
        lax.all_gather(rate_weight, "fsdp", axis=0, tiled=True),
        lax.all_gather(output_weight, "fsdp", axis=1, tiled=True),
        lax.all_gather(gate_weight, "fsdp", axis=0, tiled=True),
        lax.all_gather(up_weight, "fsdp", axis=0, tiled=True),
        lax.all_gather(down_weight, "fsdp", axis=1, tiled=True),
        lax.all_gather(query_left, "fsdp", axis=1, tiled=True),
        lax.all_gather(query_right, "fsdp", axis=0, tiled=True),
        lax.all_gather(key_left, "fsdp", axis=1, tiled=True),
        lax.all_gather(key_right, "fsdp", axis=0, tiled=True),
        lax.all_gather(value_left, "fsdp", axis=1, tiled=True),
        lax.all_gather(value_right, "fsdp", axis=0, tiled=True),
        lax.all_gather(rate_left, "fsdp", axis=1, tiled=True),
        lax.all_gather(rate_right, "fsdp", axis=0, tiled=True),
        lax.all_gather(output_left, "fsdp", axis=1, tiled=True),
        lax.all_gather(output_right, "fsdp", axis=0, tiled=True),
        lax.all_gather(gate_left, "fsdp", axis=1, tiled=True),
        lax.all_gather(gate_right, "fsdp", axis=0, tiled=True),
        lax.all_gather(up_left, "fsdp", axis=1, tiled=True),
        lax.all_gather(up_right, "fsdp", axis=0, tiled=True),
        lax.all_gather(down_left, "fsdp", axis=1, tiled=True),
        lax.all_gather(down_right, "fsdp", axis=0, tiled=True),
    )
    (
        query_whole,
        key_whole,
        value_whole,
        rate_whole,
        output_whole,
        gate_whole,
        up_whole,
        down_whole,
        query_into,
        query_from,
        key_into,
        key_from,
        value_into,
        value_from,
        rate_into,
        rate_from,
        output_into,
        output_from,
        gate_into,
        gate_from,
        up_into,
        up_from,
        down_into,
        down_from,
    ) = fetched
    places = lax.axis_index("ctx") * slot_count + jnp.arange(slot_count)
    valid_mask = (places[None, :] < seq_lengths[:, None]).astype(jnp.float32)
    valid_rows = valid_mask.reshape(total_rows, 1)
    input_rows = hidden_in.reshape(total_rows, model_width).astype(jnp.float32)
    conv_taps = jnp.concatenate([query_conv, key_conv, value_conv], axis=1)
    eye_state = jnp.broadcast_to(
        jnp.eye(head_width, dtype=jnp.float32), (state_batch, head_width, head_width)
    )
    zero_state = jnp.zeros((state_batch, head_width, head_width), jnp.float32)
    first, first_back = jax.vjp(partial(scaled_norm, scale_gain=mixer_gain), input_rows)
    first_low = first.astype(jnp.bfloat16)
    pre_query, query_inner = project(first_low, query_whole, query_into, query_from)
    pre_key, key_inner = project(first_low, key_whole, key_into, key_from)
    pre_value, value_inner = project(first_low, value_whole, value_into, value_from)
    pre_rate, rate_inner = project(first_low, rate_whole, rate_into, rate_from)
    combined = jnp.concatenate([pre_query, pre_key, pre_value], axis=1).reshape(
        seq_count, slot_count, 3 * local_cols
    )
    before = from_behind(
        combined[:, slot_count - (CONV - 1) :, :].astype(jnp.bfloat16), "ctx", 1
    ).astype(jnp.float32)
    extended = jnp.concatenate([before, combined], axis=1)

    def heads_first(block):
        return (
            block.reshape(seq_count, slot_count, heads_here, head_width)
            .transpose(0, 2, 1, 3)
            .reshape(state_batch, slot_count, head_width)
        )

    def mixer_inputs(extended_rows, rate_pre):
        convolved = sum(
            (
                conv_taps[offset] * extended_rows[:, offset : offset + slot_count, :]
                for offset in range(CONV)
            )
        )
        active = jax.nn.silu(convolved)
        queries = unit_norm(heads_first(active[..., :local_cols]))
        key_rows = unit_norm(heads_first(active[..., local_cols : 2 * local_cols]))
        value_rows = heads_first(active[..., 2 * local_cols :])
        rate_rows = (
            jax.nn.sigmoid(rate_pre.reshape(seq_count, slot_count, heads_here))
            * valid_mask[..., None]
        )
        rate_rows = rate_rows.transpose(0, 2, 1).reshape(state_batch, slot_count)
        return (queries, key_rows, value_rows, rate_rows)

    (queries, key_rows, value_rows, rate_rows), mixer_back = jax.vjp(
        mixer_inputs, extended, pre_rate
    )
    end_map, end_state, local_outs, reaching = block_summary(
        queries, key_rows, value_rows, rate_rows, eye_state, zero_state
    )
    start_state = entering((end_map, end_state), "ctx", compose, (eye_state, zero_state))[1]
    mixed = local_outs + precise("bld,bde->ble", reaching, start_state)

    def head_norm(mixed_rows):
        normed_heads = scaled_norm(mixed_rows, head_gain)
        return (
            normed_heads.reshape(seq_count, heads_here, slot_count, head_width)
            .transpose(0, 2, 1, 3)
            .reshape(total_rows, local_cols)
        )

    heads_out, head_back = jax.vjp(head_norm, mixed)
    heads_low = heads_out.astype(jnp.bfloat16)
    summed_out, summed_out_inner = (
        lax.psum(matmul(heads_low, output_whole).astype(jnp.bfloat16), "tp").astype(jnp.float32),
        lax.psum(matmul(heads_low, output_into).astype(jnp.bfloat16), "tp").astype(jnp.float32),
    )
    out_inner = summed_out_inner.astype(jnp.bfloat16)
    residual = input_rows + summed_out + adapter_scale * matmul(out_inner, output_from)
    second, second_back = jax.vjp(partial(scaled_norm, scale_gain=feed_gain), residual)
    second_low = second.astype(jnp.bfloat16)
    pre_gate, gate_inner = project(second_low, gate_whole, gate_into, gate_from)
    pre_up, up_inner = project(second_low, up_whole, up_into, up_from)

    def swiglu(gate_rows, up_rows):
        return jax.nn.silu(gate_rows) * up_rows

    activated, act_back = jax.vjp(swiglu, pre_gate, pre_up)
    activated_low = activated.astype(jnp.bfloat16)
    summed_down, summed_down_inner = (
        lax.psum(matmul(activated_low, down_whole).astype(jnp.bfloat16), "tp").astype(jnp.float32),
        lax.psum(matmul(activated_low, down_into).astype(jnp.bfloat16), "tp").astype(jnp.float32),
    )
    down_inner = summed_down_inner.astype(jnp.bfloat16)
    final = residual + summed_down + adapter_scale * matmul(down_inner, down_from)
    block_out = (
        (valid_rows * final).astype(jnp.bfloat16).reshape(seq_count, slot_count, model_width)
    )
    later = (
        lax.all_gather(query_weight, "fsdp", axis=0, tiled=True),
        lax.all_gather(key_weight, "fsdp", axis=0, tiled=True),
        lax.all_gather(value_weight, "fsdp", axis=0, tiled=True),
        lax.all_gather(rate_weight, "fsdp", axis=0, tiled=True),
        lax.all_gather(output_weight, "fsdp", axis=1, tiled=True),
        lax.all_gather(gate_weight, "fsdp", axis=0, tiled=True),
        lax.all_gather(up_weight, "fsdp", axis=0, tiled=True),
        lax.all_gather(down_weight, "fsdp", axis=1, tiled=True),
        lax.all_gather(query_left, "fsdp", axis=1, tiled=True),
        lax.all_gather(query_right, "fsdp", axis=0, tiled=True),
        lax.all_gather(key_left, "fsdp", axis=1, tiled=True),
        lax.all_gather(key_right, "fsdp", axis=0, tiled=True),
        lax.all_gather(value_left, "fsdp", axis=1, tiled=True),
        lax.all_gather(value_right, "fsdp", axis=0, tiled=True),
        lax.all_gather(rate_left, "fsdp", axis=1, tiled=True),
        lax.all_gather(rate_right, "fsdp", axis=0, tiled=True),
        lax.all_gather(output_left, "fsdp", axis=1, tiled=True),
        lax.all_gather(output_right, "fsdp", axis=0, tiled=True),
        lax.all_gather(gate_left, "fsdp", axis=1, tiled=True),
        lax.all_gather(gate_right, "fsdp", axis=0, tiled=True),
        lax.all_gather(up_left, "fsdp", axis=1, tiled=True),
        lax.all_gather(up_right, "fsdp", axis=0, tiled=True),
        lax.all_gather(down_left, "fsdp", axis=1, tiled=True),
        lax.all_gather(down_right, "fsdp", axis=0, tiled=True),
    )
    (
        query_whole,
        key_whole,
        value_whole,
        rate_whole,
        output_whole,
        gate_whole,
        up_whole,
        down_whole,
        query_into,
        query_from,
        key_into,
        key_from,
        value_into,
        value_from,
        rate_into,
        rate_from,
        output_into,
        output_from,
        gate_into,
        gate_from,
        up_into,
        up_from,
        down_into,
        down_from,
    ) = later
    grad_rows = output_grad.reshape(total_rows, model_width).astype(jnp.float32) * valid_rows
    grad_low = grad_rows.astype(jnp.bfloat16)
    down_right_grad = adapter_scale * transposed_times(down_inner, grad_low)
    grad_down_inner = (adapter_scale * times_transposed(grad_low, down_from)).astype(jnp.bfloat16)
    down_left_grad = transposed_times(activated_low, grad_down_inner)
    grad_active = times_transposed(grad_low, down_whole) + times_transposed(
        grad_down_inner, down_into
    )
    grad_gate, grad_up = act_back(grad_active)
    grad_gate_low = grad_gate.astype(jnp.bfloat16)
    grad_up_low = grad_up.astype(jnp.bfloat16)
    gate_right_grad = adapter_scale * transposed_times(gate_inner, grad_gate_low)
    up_right_grad = adapter_scale * transposed_times(up_inner, grad_up_low)
    part_second = times_transposed(grad_gate_low, gate_whole) + times_transposed(
        grad_up_low, up_whole
    )
    sum_second, sum_gate_inner, sum_up_inner = (
        lax.psum(part_second.astype(jnp.bfloat16), "tp").astype(jnp.float32),
        lax.psum(
            (adapter_scale * times_transposed(grad_gate_low, gate_from)).astype(jnp.bfloat16), "tp"
        ).astype(jnp.float32),
        lax.psum(
            (adapter_scale * times_transposed(grad_up_low, up_from)).astype(jnp.bfloat16), "tp"
        ).astype(jnp.float32),
    )
    gate_inner_grad = sum_gate_inner.astype(jnp.bfloat16)
    up_inner_grad = sum_up_inner.astype(jnp.bfloat16)
    grad_second = (
        sum_second
        + times_transposed(gate_inner_grad, gate_into)
        + times_transposed(up_inner_grad, up_into)
    )
    grad_residual = grad_rows + second_back(grad_second)[0]
    resid_low = grad_residual.astype(jnp.bfloat16)
    gate_left_grad = transposed_times(second_low, gate_inner_grad)
    up_left_grad = transposed_times(second_low, up_inner_grad)
    output_right_grad = adapter_scale * transposed_times(out_inner, resid_low)
    grad_out_inner = (adapter_scale * times_transposed(resid_low, output_from)).astype(jnp.bfloat16)
    output_left_grad = transposed_times(heads_low, grad_out_inner)
    grad_heads = times_transposed(resid_low, output_whole) + times_transposed(
        grad_out_inner, output_into
    )
    grad_mixed = head_back(grad_heads)[0]
    collected = precise("bld,ble->bde", reaching, grad_mixed)
    flipped = jnp.swapaxes(end_map, 1, 2)
    end_grad = entering_2((flipped, collected), "ctx", compose, (eye_state, zero_state))[1]
    run_out, run_back = jax.vjp(block_run, queries, key_rows, value_rows, rate_rows, start_state)
    grad_queries, grad_keys, grad_values, grad_rates, unused_state = run_back(
        (grad_mixed, end_grad)
    )
    grad_extended, grad_rate_pre = mixer_back((grad_queries, grad_keys, grad_values, grad_rates))
    returned = from_behind(for_sending(grad_extended[:, : CONV - 1, :]), "ctx", -1)
    grad_combined = grad_extended[:, CONV - 1 :, :] + jnp.pad(
        returned, ((0, 0), (slot_count - (CONV - 1), 0), (0, 0))
    )
    grad_combined = grad_combined.reshape(total_rows, 3 * local_cols)
    grad_query_low = grad_combined[:, :local_cols].astype(jnp.bfloat16)
    grad_key_low = grad_combined[:, local_cols : 2 * local_cols].astype(jnp.bfloat16)
    grad_value_low = grad_combined[:, 2 * local_cols :].astype(jnp.bfloat16)
    grad_rate_low = grad_rate_pre.astype(jnp.bfloat16)
    query_right_grad = adapter_scale * transposed_times(query_inner, grad_query_low)
    key_right_grad = adapter_scale * transposed_times(key_inner, grad_key_low)
    value_right_grad = adapter_scale * transposed_times(value_inner, grad_value_low)
    rate_right_grad = adapter_scale * transposed_times(rate_inner, grad_rate_low)
    part_first = (
        times_transposed(grad_query_low, query_whole)
        + times_transposed(grad_key_low, key_whole)
        + times_transposed(grad_value_low, value_whole)
        + times_transposed(grad_rate_low, rate_whole)
    )
    sum_first, sum_query_inner, sum_key_inner, sum_value_inner, sum_rate_inner = (
        lax.psum(part_first.astype(jnp.bfloat16), "tp").astype(jnp.float32),
        lax.psum(
            (adapter_scale * times_transposed(grad_query_low, query_from)).astype(jnp.bfloat16),
            "tp",
        ).astype(jnp.float32),
        lax.psum(
            (adapter_scale * times_transposed(grad_key_low, key_from)).astype(jnp.bfloat16), "tp"
        ).astype(jnp.float32),
        lax.psum(
            (adapter_scale * times_transposed(grad_value_low, value_from)).astype(jnp.bfloat16),
            "tp",
        ).astype(jnp.float32),
        lax.psum(
            (adapter_scale * times_transposed(grad_rate_low, rate_from)).astype(jnp.bfloat16), "tp"
        ).astype(jnp.float32),
    )
    query_inner_grad = sum_query_inner.astype(jnp.bfloat16)
    key_inner_grad = sum_key_inner.astype(jnp.bfloat16)
    value_inner_grad = sum_value_inner.astype(jnp.bfloat16)
    rate_inner_grad = sum_rate_inner.astype(jnp.bfloat16)
    grad_first = (
        sum_first
        + times_transposed(query_inner_grad, query_into)
        + times_transposed(key_inner_grad, key_into)
        + times_transposed(value_inner_grad, value_into)
        + times_transposed(rate_inner_grad, rate_into)
    )
    input_grad = (
        (grad_residual + first_back(grad_first)[0])
        .astype(jnp.bfloat16)
        .reshape(seq_count, slot_count, model_width)
    )
    query_left_grad = transposed_times(first_low, query_inner_grad)
    key_left_grad = transposed_times(first_low, key_inner_grad)
    value_left_grad = transposed_times(first_low, value_inner_grad)
    rate_left_grad = transposed_times(first_low, rate_inner_grad)
    shared = (
        lax.psum_scatter(
            query_left_grad.astype(jnp.bfloat16), "fsdp", scatter_dimension=1, tiled=True
        ).astype(jnp.float32),
        lax.psum_scatter(
            query_right_grad.astype(jnp.bfloat16), "fsdp", scatter_dimension=0, tiled=True
        ).astype(jnp.float32),
        lax.psum_scatter(
            key_left_grad.astype(jnp.bfloat16), "fsdp", scatter_dimension=1, tiled=True
        ).astype(jnp.float32),
        lax.psum_scatter(
            key_right_grad.astype(jnp.bfloat16), "fsdp", scatter_dimension=0, tiled=True
        ).astype(jnp.float32),
        lax.psum_scatter(
            value_left_grad.astype(jnp.bfloat16), "fsdp", scatter_dimension=1, tiled=True
        ).astype(jnp.float32),
        lax.psum_scatter(
            value_right_grad.astype(jnp.bfloat16), "fsdp", scatter_dimension=0, tiled=True
        ).astype(jnp.float32),
        lax.psum_scatter(
            rate_left_grad.astype(jnp.bfloat16), "fsdp", scatter_dimension=1, tiled=True
        ).astype(jnp.float32),
        lax.psum_scatter(
            rate_right_grad.astype(jnp.bfloat16), "fsdp", scatter_dimension=0, tiled=True
        ).astype(jnp.float32),
        lax.psum_scatter(
            output_left_grad.astype(jnp.bfloat16), "fsdp", scatter_dimension=1, tiled=True
        ).astype(jnp.float32),
        lax.psum_scatter(
            output_right_grad.astype(jnp.bfloat16), "fsdp", scatter_dimension=0, tiled=True
        ).astype(jnp.float32),
        lax.psum_scatter(
            gate_left_grad.astype(jnp.bfloat16), "fsdp", scatter_dimension=1, tiled=True
        ).astype(jnp.float32),
        lax.psum_scatter(
            gate_right_grad.astype(jnp.bfloat16), "fsdp", scatter_dimension=0, tiled=True
        ).astype(jnp.float32),
        lax.psum_scatter(
            up_left_grad.astype(jnp.bfloat16), "fsdp", scatter_dimension=1, tiled=True
        ).astype(jnp.float32),
        lax.psum_scatter(
            up_right_grad.astype(jnp.bfloat16), "fsdp", scatter_dimension=0, tiled=True
        ).astype(jnp.float32),
        lax.psum_scatter(
            down_left_grad.astype(jnp.bfloat16), "fsdp", scatter_dimension=1, tiled=True
        ).astype(jnp.float32),
        lax.psum_scatter(
            down_right_grad.astype(jnp.bfloat16), "fsdp", scatter_dimension=0, tiled=True
        ).astype(jnp.float32),
    )
    (
        query_left_share,
        query_right_share,
        key_left_share,
        key_right_share,
        value_left_share,
        value_right_share,
        rate_left_share,
        rate_right_share,
        output_left_share,
        output_right_share,
        gate_left_share,
        gate_right_share,
        up_left_share,
        up_right_share,
        down_left_share,
        down_right_share,
    ) = shared
    summed = (
        lax.psum(query_left_share.astype(jnp.bfloat16), "ctx").astype(jnp.float32),
        lax.psum(query_right_share.astype(jnp.bfloat16), "ctx").astype(jnp.float32),
        lax.psum(key_left_share.astype(jnp.bfloat16), "ctx").astype(jnp.float32),
        lax.psum(key_right_share.astype(jnp.bfloat16), "ctx").astype(jnp.float32),
        lax.psum(value_left_share.astype(jnp.bfloat16), "ctx").astype(jnp.float32),
        lax.psum(value_right_share.astype(jnp.bfloat16), "ctx").astype(jnp.float32),
        lax.psum(rate_left_share.astype(jnp.bfloat16), "ctx").astype(jnp.float32),
        lax.psum(rate_right_share.astype(jnp.bfloat16), "ctx").astype(jnp.float32),
        lax.psum(output_left_share.astype(jnp.bfloat16), "ctx").astype(jnp.float32),
        lax.psum(output_right_share.astype(jnp.bfloat16), "ctx").astype(jnp.float32),
        lax.psum(gate_left_share.astype(jnp.bfloat16), "ctx").astype(jnp.float32),
        lax.psum(gate_right_share.astype(jnp.bfloat16), "ctx").astype(jnp.float32),
        lax.psum(up_left_share.astype(jnp.bfloat16), "ctx").astype(jnp.float32),
        lax.psum(up_right_share.astype(jnp.bfloat16), "ctx").astype(jnp.float32),
        lax.psum(down_left_share.astype(jnp.bfloat16), "ctx").astype(jnp.float32),
        lax.psum(down_right_share.astype(jnp.bfloat16), "ctx").astype(jnp.float32),
    )
    return (block_out, input_grad) + tuple(summed)


def solution(mesh):
    placed = (
        P("fsdp", "ctx", None),
        P("fsdp"),
        P(),
        P(),
        P("fsdp", "tp"),
        P("fsdp", "tp"),
        P("fsdp", "tp"),
        P("fsdp", "tp"),
        P(None, "tp"),
        P(None, "tp"),
        P(None, "tp"),
        P(),
        P("tp", "fsdp"),
        P("fsdp", "tp"),
        P("fsdp", "tp"),
        P("tp", "fsdp"),
        P(None, "fsdp"),
        P("fsdp", "tp"),
        P(None, "fsdp"),
        P("fsdp", "tp"),
        P(None, "fsdp"),
        P("fsdp", "tp"),
        P(None, "fsdp"),
        P("fsdp", "tp"),
        P("tp", "fsdp"),
        P("fsdp", None),
        P(None, "fsdp"),
        P("fsdp", "tp"),
        P(None, "fsdp"),
        P("fsdp", "tp"),
        P("tp", "fsdp"),
        P("fsdp", None),
        P("fsdp", "ctx", None),
    )
    return jax.shard_map(
        local,
        mesh=mesh,
        in_specs=placed,
        out_specs=(
            P("fsdp", "ctx", None),
            P("fsdp", "ctx", None),
            P(None, "fsdp"),
            P("fsdp", "tp"),
            P(None, "fsdp"),
            P("fsdp", "tp"),
            P(None, "fsdp"),
            P("fsdp", "tp"),
            P(None, "fsdp"),
            P("fsdp", "tp"),
            P("tp", "fsdp"),
            P("fsdp", None),
            P(None, "fsdp"),
            P("fsdp", "tp"),
            P(None, "fsdp"),
            P("fsdp", "tp"),
            P("tp", "fsdp"),
            P("fsdp", None),
        ),
        check_vma=False,
    )
```

profile of v0, /device:TPU:0, one launch (start us, length us, event | category | flops | bytes accessed | tf_op | source)
XLA Modules:
  0.0 1506.7 jit_solution(17824678491742909967)
XLA Ops:
  32.3 3.1 fusion.272
  40.5 9.1 all-gather.17.cloned.1.call-done
  57.4 4.1 collective-permute-start
  62.8 7.7 fusion.198
  80.9 206.8 %while.106 = (s32[]{:T(128)}, f32[16,128,128]{2,1,0:T(8,128)S(1)}, f32[16,128,128]{2,1,0:T(8,128)}, f32[2,16,64,128]{3,2,1,0:T(8,128)}, f32[2,16,64,128]{3,2,0,1...) while((s32[]{:T(128)}, f32[16,128,128]{2,1,0:T(8,128)S(1)}, ...), condition=%wide.region_4.6_spmd.clone, body=%wide.region_3.5_spmd.clone.sunk | while | flops 2015662080 | bytes 48016976 | solution.py:163
  84.9 79.4 %custom-call.37 = f32[16,1,64,64]{2,3,1,0:T(8,128)S(1)} custom-call(f32[16,1,64,64]{3,2,1,0:T(8,128)} %fusion.589), custom_call_target="InvertDiagBlocksLowerTriangular" | custom-call | tf_op jit(solution)/shard_map/while/body/eval_jaxpr/triangular_solve/custom-call.1 | solution.py:132
  188.2 79.4 %custom-call.37 = f32[16,1,64,64]{2,3,1,0:T(8,128)S(1)} custom-call(f32[16,1,64,64]{3,2,1,0:T(8,128)} %fusion.589), custom_call_target="InvertDiagBlocksLowerTriangular" | custom-call | tf_op jit(solution)/shard_map/while/body/eval_jaxpr/triangular_solve/custom-call.1 | solution.py:132
  293.3 44.4 %all-gather.31.cloned.1.call-done = bf16[64,128,128]{2,1,0:T(8,128)(2,1)} async-done(((bf16[16,128,128]{2,1,0:T(8,128)(2,1)}), bf16[64,128,128]{2,1,0:T(8,128)(2,1)}) %all-gather.31.cloned.1.call-update) | async-done | bytes 2097168 | tf_op jit(solution)/shard_map/all_gather | solution.py:25
  337.7 46.1 %all-gather.33.cloned.1.call-done = bf16[64,128,128]{2,1,0:T(8,128)(2,1)} async-done(((bf16[16,128,128]{2,1,0:T(8,128)(2,1)}), bf16[64,128,128]{2,1,0:T(8,128)(2,1)}) %all-gather.33.cloned.1.call-update) | async-done | bytes 2097168 | tf_op jit(solution)/shard_map/all_gather | solution.py:25
  388.5 6.0 all-gather.23.cloned.1.call-done
  394.5 4.3 convolution_convert_fusion
  419.5 16.7 %psum.197 = bf16[512,16]{0,1:T(8,128)(2,1)S(1)} all-reduce(bf16[512,16]{0,1:T(8,128)(2,1)S(1)} %convolution_convert_fusion.18), channel_id=1, replica_groups=mesh['fsdp'=2,'ctx'=4,'tp'=4] {'tp'}, use_global_device_ids=true, to_apply=%region_9.11 | all-reduce | flops 8192 | bytes 32768 | tf_op jit(solution)/shard_map/psum | solution.py:361
  436.2 8.5 fusion.276
  444.7 43.5 %all-reduce.24.cloned.1.call-done = bf16[512,2048]{1,0:T(8,128)(2,1)} async-done(((bf16[512,2048]{1,0:T(8,128)(2,1)}), bf16[512,2048]{1,0:T(8,128)(2,1)}) %all-reduce.24.cloned.1.call-update) | async-done | bytes 2097168 | tf_op jit(solution)/shard_map/psum | solution.py:360
  488.2 3.4 multiply_reduce_fusion.1
  495.5 10.3 all-gather.25.cloned.1.call-done
  505.8 6.4 fusion.274
  514.3 10.1 all-gather.27.cloned.1.call-done
  524.5 6.5 fusion.275
  532.8 3.2 multiply_convert_fusion.2
  536.4 3.4 fusion.277
  539.9 4.7 add_convert_fusion.1
  556.4 16.8 %all-reduce.13 = (bf16[512,16]{0,1:T(8,128)(2,1)S(1)}, bf16[512,16]{0,1:T(8,128)(2,1)S(1)}) all-reduce(bf16[512,16]{0,1:T(8,128)(2,1)S(1)} %fusion.210, bf16[512,16]{0,1:T(8,128)(2,1)S(1)} %fusion.211), channel_id=1, replica_groups=mesh['fsdp'=2,'ctx'=4,'tp'=4] {'tp'}, use_global_device_ids=true, to_apply=%region_14.16 | all-reduce | flops 16384 | bytes 65536 | tf_op jit(solution)/shard_map/psum | solution.py:454
  576.0 40.0 %all-reduce.26.cloned.1.call-done = bf16[512,2048]{1,0:T(8,128)(2,1)} async-done(((bf16[512,2048]{1,0:T(8,128)(2,1)}), bf16[512,2048]{1,0:T(8,128)(2,1)}) %all-reduce.26.cloned.1.call-update) | async-done | bytes 2097168 | tf_op jit(solution)/shard_map/psum | solution.py:453
  616.1 5.3 multiply_reduce_fusion
  642.5 195.8 %while.104 = (s32[]{:T(128)}, f32[16,128,128]{2,1,0:T(8,128)S(1)}, f32[2,16,64,64]{3,2,1,0:T(8,128)}, f32[2,16,64,64]{3,2,1,0:T(8,128)}, f32[2,16,64,1]{2,1,3,0:...) while((s32[]{:T(128)}, f32[16,128,128]{2,1,0:T(8,128)S(1)}, ...), condition=%wide.region_21.23_spmd.clone.clone, body=%wide.region_20.22_spmd.clone.clone.sunk | while | flops 806654016 | bytes 17356216 | solution.py:188
  647.7 80.0 %custom-call.35 = f32[16,1,64,64]{2,3,1,0:T(8,128)} custom-call(f32[16,1,64,64]{3,2,1,0:T(8,128)} %add_bitcast_fusion.2), custom_call_target="InvertDiagBlocksLowerTriangular" | custom-call | tf_op jit(solution)/shard_map/jvp()/while/body/eval_jaxpr/triangular_solve/custom-call.1 | solution.py:132
  727.8 3.2 bitcast_dynamic-update-slice_fusion.18
  745.6 80.0 %custom-call.35 = f32[16,1,64,64]{2,3,1,0:T(8,128)} custom-call(f32[16,1,64,64]{3,2,1,0:T(8,128)} %add_bitcast_fusion.2), custom_call_target="InvertDiagBlocksLowerTriangular" | custom-call | tf_op jit(solution)/shard_map/jvp()/while/body/eval_jaxpr/triangular_solve/custom-call.1 | solution.py:132
  825.6 3.2 bitcast_dynamic-update-slice_fusion.18
  846.2 8.8 while.107
  858.3 251.1 %while.105 = (s32[]{:T(128)}, f32[16,128,128]{2,1,0:T(8,128)S(1)}, f32[2,16,64,128]{3,2,0,1:T(8,128)}, f32[2,16,64,128]{3,2,0,1:T(8,128)}, f32[2,16,64,128]{3,2,...) while((s32[]{:T(128)}, f32[16,128,128]{2,1,0:T(8,128)S(1)}, ...), condition=%wide.region_26.30_spmd.clone.clone, body=%wide.region_22.29_spmd.clone.clone.sunk | while | flops 2318494720 | bytes 99539992 | solution.py:188
  860.9 3.1 fusion.556
  871.3 79.4 %custom-call.36 = f32[16,1,64,64]{2,3,1,0:T(8,128)S(1)} custom-call(f32[16,1,64,64]{3,2,1,0:T(8,128)} %fusion.558), custom_call_target="InvertDiagBlocksLowerTriangular" | custom-call | tf_op jit(solution)/shard_map/transpose(jvp())/while/body/eval_jaxpr/triangular_solve/custom-call.0 | solution.py:129
  952.5 4.2 fusion.560
  962.4 3.2 fusion.555
  996.6 79.4 %custom-call.36 = f32[16,1,64,64]{2,3,1,0:T(8,128)S(1)} custom-call(f32[16,1,64,64]{3,2,1,0:T(8,128)} %fusion.558), custom_call_target="InvertDiagBlocksLowerTriangular" | custom-call | tf_op jit(solution)/shard_map/transpose(jvp())/while/body/eval_jaxpr/triangular_solve/custom-call.0 | solution.py:129
  1077.8 4.2 fusion.560
  1087.7 3.2 fusion.555
  1125.3 3.7 collective-permute-done.1
  1140.3 7.3 convolution_convert_fusion.1
  1148.4 3.2 fusion.203
  1154.4 5.0 fusion.240
  1159.4 3.2 fusion.248
  1162.6 3.3 fusion.244
  1165.9 10.8 all-reduce.28.cloned.1.call-done
  1185.5 14.0 all-reduce.34.cloned.1.call-done
  1204.8 5.6 reduce-scatter.32.cloned.1.call-done
  1210.4 10.8 reduce-scatter.34.cloned.1.call-done
  1221.1 10.7 reduce-scatter.28.cloned.1.call-done
  1231.8 11.5 reduce-scatter.30.cloned.1.call-done
  1243.3 10.7 reduce-scatter.16.cloned.1.call-done
  1254.0 10.9 reduce-scatter.20.cloned.1.call-done
  1264.9 10.9 reduce-scatter.24.cloned.1.call-done
  1275.8 11.5 reduce-scatter.14.cloned.1.call-done
  1287.2 11.3 reduce-scatter.18.cloned.1.call-done
  1298.6 11.5 reduce-scatter.22.cloned.1.call-done
  1310.1 11.3 reduce-scatter.26.cloned.1.call-done
  1321.4 10.8 reduce-scatter.36.cloned.1.call-done
  1332.3 6.8 add_convert_fusion
  1348.1 29.8 %all-reduce.32.cloned.1.call-done = (bf16[2048,8]{0,1:T(8,128)(2,1)}, bf16[8,512]{1,0:T(8,128)(2,1)}, bf16[2048,8]{0,1:T(8,128)(2,1)}, bf16[8,512]{1,0:T(8,128)(...) async-done(((bf16[2048,8]{0,1:T(8,128)(2,1)}, ...) | async-done | bytes 362576 | tf_op jit(solution)/shard_map/psum | solution.py:612
  1399.6 86.5 %all-reduce.30.cloned.1.call-done = (bf16[512,2048]{1,0:T(8,128)(2,1)}, bf16[512,2048]{1,0:T(8,128)(2,1)}) async-done(((bf16[512,2048]{1,0:T(8,128)(2,1)}, bf16[512,2048]{1,0:T(8,128)(2,1)}), (bf16[512,2048]{1,0:T(8,128)(2,1)}, bf16[512,2048]{1,0:T(8,128)(2,1)})) %all-reduce.30.cloned.1.call-update) | async-done | bytes 4194320 | tf_op jit(solution)/shard_map/psum | solution.py:376
  1486.2 5.2 multiply_convert_fusion
  1492.2 5.4 fusion.184
  (759 shorter events, 370.4 us)
Async XLA Ops:
  7.2 25.1 %all-gather.21.cloned.1.call-start = ((), (), s32[]{:S(2)}) async-start(), calls=%async_computation.14 | async-start | bytes 3145728 | tf_op jit(solution)/shard_map/all_gather | solution.py:243
  8.0 28.3 %all-gather.19.cloned.1.call-start = ((), (), s32[]{:S(2)}) async-start(), calls=%async_computation.13 | async-start | bytes 3145728 | tf_op jit(solution)/shard_map/all_gather | solution.py:242
  8.7 40.9 %all-gather.17.cloned.1.call-start = ((), (), s32[]{:S(2)}) async-start(), calls=%async_computation.12 | async-start | bytes 3145728 | tf_op jit(solution)/shard_map/all_gather | solution.py:241
  9.5 328.3 %all-gather.31.cloned.1.call-start = ((), (), s32[]{:S(2)}) async-start(), calls=%async_computation.33 | async-start | bytes 2621440 | tf_op jit(solution)/shard_map/all_gather | solution.py:25
  14.6 35.0 %copy-start = (bf16[512,2048]{1,0:T(8,128)(2,1)}, bf16[512,2048]{1,0:T(8,128)(2,1)S(1)}, u32[]{:S(2)}) copy-start(bf16[512,2048]{1,0:T(8,128)(2,1)S(1)} %fusion.182) | copy-start | bytes 6291460
  14.7 8.9 copy-start.150
  14.7 10.7 copy-start.151
  14.7 12.5 copy-start.121
  15.4 20.1 %copy-start.80 = (bf16[512,16]{0,1:T(8,128)(2,1)}, bf16[512,16]{0,1:T(8,128)(2,1)S(1)}, u32[]{:S(2)}) copy-start(bf16[512,16]{0,1:T(8,128)(2,1)S(1)} %convolution_convert_fusion.14) | copy-start | bytes 49156
  15.4 13.6 copy-start.122
  21.2 394.0 %copy-start.116 = (f32[512]{0:T(512)}, f32[512]{0:T(512)S(1)}, u32[]{:S(2)}) copy-start(f32[512]{0:T(512)S(1)} %get-tuple-element.1548) | copy-start | bytes 6148
  23.5 11.9 copy-start.107
  25.3 13.8 copy-start.106
  27.2 25.4 %copy-start.104 = (bf16[16,512]{1,0:T(8,128)(2,1)}, bf16[16,512]{1,0:T(8,128)(2,1)S(1)}, u32[]{:S(2)}) copy-start(bf16[16,512]{1,0:T(8,128)(2,1)S(1)} %all_gather.122) | copy-start | bytes 49156
  30.9 31.8 %copy-start.89 = (f32[1536]{0:T(1024)}, f32[1536]{0:T(1024)S(1)}, u32[]{:S(2)}) copy-start(f32[1536]{0:T(1024)S(1)} %get-tuple-element.1347) | copy-start | bytes 18436
  31.0 31.8 %copy-start.91 = (f32[1536]{0:T(1024)}, f32[1536]{0:T(1024)S(1)}, u32[]{:S(2)}) copy-start(f32[1536]{0:T(1024)S(1)} %get-tuple-element.1349) | copy-start | bytes 18436
  31.0 31.8 %copy-start.93 = (f32[1536]{0:T(1024)}, f32[1536]{0:T(1024)S(1)}, u32[]{:S(2)}) copy-start(f32[1536]{0:T(1024)S(1)} %get-tuple-element.1350) | copy-start | bytes 18436
  31.0 31.8 %copy-start.95 = (f32[1536]{0:T(1024)}, f32[1536]{0:T(1024)S(1)}, u32[]{:S(2)}) copy-start(f32[1536]{0:T(1024)S(1)} %get-tuple-element.1348) | copy-start | bytes 18436
  32.3 20.3 %copy-start.84 = (bf16[512,16]{0,1:T(8,128)(2,1)}, bf16[512,16]{0,1:T(8,128)(2,1)S(1)}, u32[]{:S(2)}) copy-start(bf16[512,16]{0,1:T(8,128)(2,1)S(1)} %convolution_convert_fusion.16) | copy-start | bytes 49156
  57.4 5.4 collective-permute-start
  289.9 94.0 %all-gather.33.cloned.1.call-start = ((), (), s32[]{:S(2)}) async-start(), calls=%async_computation.34 | async-start | bytes 2621440 | tf_op jit(solution)/shard_map/all_gather | solution.py:25
  290.9 103.7 %all-gather.23.cloned.1.call-start = ((), (), s32[]{:S(2)}) async-start(), calls=%async_computation.15 | async-start | bytes 3145728 | tf_op jit(solution)/shard_map/all_gather | solution.py:245
  291.4 144.7 %all-gather.29.cloned.1.call-start = ((), (), s32[]{:S(2)}) async-start(), calls=%async_computation.19 | async-start | bytes 8650752 | tf_op jit(solution)/shard_map/all_gather | solution.py:248
  292.2 196.0 %all-reduce.24.cloned.1.call-start = ((), (), s32[]{:S(2)}) async-start(), calls=%async_computation.16 | async-start | bytes 4194304 | tf_op jit(solution)/shard_map/psum | solution.py:360
  386.9 12.0 copy-start.32
  399.0 10.6 copy-start.124
  399.0 12.5 copy-start.125
  399.0 14.3 copy-start.126
  399.0 106.8 %all-gather.25.cloned.1.call-start = ((), (), s32[]{:S(2)}) async-start(), calls=%async_computation.17 | async-start | bytes 8650752 | tf_op jit(solution)/shard_map/all_gather | solution.py:246
  399.8 124.7 %all-gather.27.cloned.1.call-start = ((), (), s32[]{:S(2)}) async-start(), calls=%async_computation.18 | async-start | bytes 8650752 | tf_op jit(solution)/shard_map/all_gather | solution.py:247
  400.3 215.7 %all-reduce.26.cloned.1.call-start = ((), (), s32[]{:S(2)}) async-start(), calls=%async_computation.20 | async-start | bytes 4194304 | tf_op jit(solution)/shard_map/psum | solution.py:453
  402.2 17.0 %copy-start.109 = (bf16[512,16]{0,1:T(8,128)(2,1)}, bf16[512,16]{0,1:T(8,128)(2,1)S(1)}, u32[]{:S(2)}) copy-start(bf16[512,16]{0,1:T(8,128)(2,1)S(1)} %all_gather.137) | copy-start | bytes 49156
  407.7 123.9 %copy-start.78 = (bf16[1408,16]{0,1:T(8,128)(2,1)}, bf16[1408,16]{0,1:T(8,128)(2,1)S(1)}, u32[]{:S(2)}) copy-start(bf16[1408,16]{0,1:T(8,128)(2,1)S(1)} %all_gather.146) | copy-start | bytes 135172
  419.3 112.4 %copy-start.99 = (bf16[512,16]{0,1:T(8,128)(2,1)}, bf16[512,16]{0,1:T(8,128)(2,1)S(1)}, u32[]{:S(2)}) copy-start(bf16[512,16]{0,1:T(8,128)(2,1)S(1)} %fusion.213) | copy-start | bytes 49156
  436.2 52.0 %copy-start.88 = (bf16[512,16]{0,1:T(8,128)(2,1)}, bf16[512,16]{0,1:T(8,128)(2,1)S(1)}, u32[]{:S(2)}) copy-start(bf16[512,16]{0,1:T(8,128)(2,1)S(1)} %psum.197) | copy-start | bytes 49156
  444.7 46.9 %copy-start.113 = (f32[2048]{0:T(1024)S(1)}, f32[2048]{0:T(1024)}, u32[]{:S(2)}) copy-start(f32[2048]{0:T(1024)} %param.52) | copy-start | bytes 24580
  544.7 301.5 %all-gather.35.cloned.1.call-start = ((), (), s32[]{:S(2)}) async-start(), calls=%async_computation.35 | async-start | bytes 2621440 | tf_op jit(solution)/shard_map/all_gather | solution.py:45
  552.6 293.6 %all-gather.37.cloned.1.call-start = ((), (), s32[]{:S(2)}) async-start(), calls=%async_computation.36 | async-start | bytes 2621440 | tf_op jit(solution)/shard_map/all_gather | solution.py:45
  573.2 48.1 %copy-start.97 = (bf16[512,16]{0,1:T(8,128)(2,1)}, bf16[512,16]{0,1:T(8,128)(2,1)S(1)}, u32[]{:S(2)}) copy-start(bf16[512,16]{0,1:T(8,128)(2,1)S(1)} %get-tuple-element.1470) | copy-start | bytes 49156
  573.2 48.1 %copy-start.111 = (bf16[512,16]{0,1:T(8,128)(2,1)}, bf16[512,16]{0,1:T(8,128)(2,1)S(1)}, u32[]{:S(2)}) copy-start(bf16[512,16]{0,1:T(8,128)(2,1)S(1)} %get-tuple-element.1471) | copy-start | bytes 49156
  639.1 537.7 %all-reduce.28.cloned.1.call-start = ((), (), s32[]{:S(2)}) async-start(), calls=%async_computation.37 | async-start | bytes 163840 | tf_op jit(solution)/shard_map/psum | solution.py:377
  1123.0 6.0 collective-permute-start.1
  1125.3 8.9 copy-start.105
  1125.3 11.3 copy-start.17
  1135.1 64.4 %all-reduce.34.cloned.1.call-start = ((), (), s32[]{:S(2)}) async-start(), calls=%async_computation.40 | async-start | bytes 272384
  1136.6 73.8 %reduce-scatter.32.cloned.1.call-start = ((), (), s32[]{:S(2)}) async-start(), calls=%async_computation.30 | async-start | bytes 98304 | tf_op jit(solution)/shard_map/reduce_scatter | solution.py:574
  1138.4 82.8 %reduce-scatter.34.cloned.1.call-start = ((), (), s32[]{:S(2)}) async-start(), calls=%async_computation.31 | async-start | bytes 98304 | tf_op jit(solution)/shard_map/reduce_scatter | solution.py:580
  1140.2 91.6 %reduce-scatter.28.cloned.1.call-start = ((), (), s32[]{:S(2)}) async-start(), calls=%async_computation.28 | async-start | bytes 24576 | tf_op jit(solution)/shard_map/reduce_scatter | solution.py:568
  1148.4 95.0 %reduce-scatter.30.cloned.1.call-start = ((), (), s32[]{:S(2)}) async-start(), calls=%async_computation.29 | async-start | bytes 98304 | tf_op jit(solution)/shard_map/reduce_scatter | solution.py:571
  1151.7 102.3 %reduce-scatter.16.cloned.1.call-start = ((), (), s32[]{:S(2)}) async-start(), calls=%async_computation.22 | async-start | bytes 24576 | tf_op jit(solution)/shard_map/reduce_scatter | solution.py:547
  1152.6 112.3 %reduce-scatter.20.cloned.1.call-start = ((), (), s32[]{:S(2)}) async-start(), calls=%async_computation.24 | async-start | bytes 24576 | tf_op jit(solution)/shard_map/reduce_scatter | solution.py:553
  1153.4 122.3 %reduce-scatter.24.cloned.1.call-start = ((), (), s32[]{:S(2)}) async-start(), calls=%async_computation.26 | async-start | bytes 24576 | tf_op jit(solution)/shard_map/reduce_scatter | solution.py:559
  1154.3 133.0 %reduce-scatter.14.cloned.1.call-start = ((), (), s32[]{:S(2)}) async-start(), calls=%async_computation.21 | async-start | bytes 98304 | tf_op jit(solution)/shard_map/reduce_scatter | solution.py:544
  1162.6 14.1 copy-start.1
  1178.5 120.1 %reduce-scatter.18.cloned.1.call-start = ((), (), s32[]{:S(2)}) async-start(), calls=%async_computation.23 | async-start | bytes 98304 | tf_op jit(solution)/shard_map/reduce_scatter | solution.py:550
  1180.4 129.7 %reduce-scatter.22.cloned.1.call-start = ((), (), s32[]{:S(2)}) async-start(), calls=%async_computation.25 | async-start | bytes 98304 | tf_op jit(solution)/shard_map/reduce_scatter | solution.py:556
  1181.6 150.6 %copy-start.87 = (bf16[2048,4]{0,1:T(4,128)(2,1)S(1)}, bf16[2048,4]{0,1:T(4,128)(2,1)}, u32[]{:S(2)}) copy-start(bf16[2048,4]{0,1:T(4,128)(2,1)} %copy-done.86) | copy-start | bytes 49156
  1181.6 150.6 %copy-start.147 = (bf16[512,4]{0,1:T(4,128)(2,1)S(1)}, bf16[512,4]{0,1:T(4,128)(2,1)}, u32[]{:S(2)}) copy-start(bf16[512,4]{0,1:T(4,128)(2,1)} %copy-done.146) | copy-start | bytes 12292
  1181.7 139.7 %reduce-scatter.26.cloned.1.call-start = ((), (), s32[]{:S(2)}) async-start(), calls=%async_computation.27 | async-start | bytes 98304 | tf_op jit(solution)/shard_map/reduce_scatter | solution.py:562
  1182.8 149.4 %reduce-scatter.36.cloned.1.call-start = ((), (), s32[]{:S(2)}) async-start(), calls=%async_computation.32 | async-start | bytes 98304 | tf_op jit(solution)/shard_map/reduce_scatter | solution.py:589
  1185.5 192.5 %all-reduce.32.cloned.1.call-start = ((), (), s32[]{:S(2)}) async-start(), calls=%async_computation.39 | async-start | bytes 727040 | tf_op jit(solution)/shard_map/psum | solution.py:612
  1332.2 153.9 %all-reduce.30.cloned.1.call-start = ((), (), s32[]{:S(2)}) async-start(), calls=%async_computation.38 | async-start | bytes 8388608 | tf_op jit(solution)/shard_map/psum | solution.py:376
  1345.4 140.8 %copy-start.77 = (bf16[16,2048]{1,0:T(8,128)(2,1)S(1)}, bf16[16,2048]{1,0:T(8,128)(2,1)}, u32[]{:S(2)}) copy-start(bf16[16,2048]{1,0:T(8,128)(2,1)} %copy-done.76) | copy-start | bytes 196612
  1345.4 140.8 %copy-start.118 = (f32[512]{0:T(512)S(1)}, f32[512]{0:T(512)}, u32[]{:S(2)}) copy-start(f32[512]{0:T(512)} %copy-done.116) | copy-start | bytes 6148
  (160 other events, 644.8 us)
Sparse Core Ops, SparseCore 0:
  9.6 13.2 all-gather.20
  24.5 11.7 all-gather.18
  37.8 11.7 all-gather.16
  290.0 47.6 all-gather.30
  339.1 44.6 all-gather.32
  385.2 9.2 all-gather.22
  396.1 17.2 all-gather.28
  417.0 71.1 all-reduce.23
  489.8 15.9 all-gather.24
  507.3 17.1 all-gather.26
  544.8 71.1 all-reduce.25
  617.5 45.9 all-gather.34
  665.0 45.0 all-gather.36
  1135.2 41.4 all-reduce.27
  1180.4 19.0 all-reduce.33
  1201.6 8.7 reduce-scatter.31
  1212.5 8.5 reduce-scatter.33
  1223.3 8.5 reduce-scatter.27
  1234.7 8.5 reduce-scatter.29
  1245.4 8.5 reduce-scatter.15
  1256.3 8.5 reduce-scatter.19
  1267.1 8.5 reduce-scatter.23
  1278.6 8.5 reduce-scatter.13
  1289.9 8.5 reduce-scatter.17
  1301.4 8.5 reduce-scatter.21
  1312.8 8.5 reduce-scatter.25
  1323.5 8.5 reduce-scatter.35
  1337.2 40.6 all-reduce.31
  1382.0 104.0 all-reduce.29
where the time goes:
time: 1520 us; the launch traced here: 1510 us
  other arithmetic  547 us (36%)
  waiting for transfers between devices  488 us (32%)
  matrix products  312 us (21%)
  local copies, waits for them, and re-layouts  69 us (5%)
  blocking collectives  65 us (4%)
  between operations  16.8 us (1%)
    another operation x16, other arithmetic, block_solve(): lax.linalg.triangular_solve(system, rate_block[:, :, None] * value_block,...  321 us
    another operation x8, other arithmetic, block_solve(): lax.linalg.triangular_solve(system, rate_block[:, :, None] * key_block, l...  161 us
    dot_general x58, matrix products, precise(): jnp.einsum(form, left_side, right_side, precision=lax.Precision.HIGHEST)  123 us
    all_gather x2, waiting for transfers between devices, entering(): lax.all_gather(a.astype(kind), axis)  90.5 us
    psum x1, waiting for transfers between devices, local(): lax.psum(matmul(activated_low, down_whole).astype(jnp.bfloat16), 'tp')  86.5 us
    dot_general x24, matrix products, times_transposed(): lax.dot_general(left_side, right_side, (((1,), (1,)), ((), ())), preferre...  71.9 us
    dot_general x24, matrix products, matmul(): return jnp.dot(left_side, right_side, preferred_element_type=jnp.float32)  52.8 us
    psum x1, waiting for transfers between devices, local(): lax.psum(matmul(heads_low, output_whole).astype(jnp.bfloat16), 'tp')  43.5 us
  transfers between devices with their start and end apart: 31, of which 27 were waited for; matrix products, arithmetic and copies ran while one was open for 24% of the time, Pallas kernels for 0%

commit v1 on v0

v1 whole, which is shorter than its diff:
```python
import functools

import jax
import jax.numpy as jnp
from jax import lax
from jax.experimental import pallas as pl
from jax.experimental.pallas import tpu as pltpu
from jax.sharding import PartitionSpec as P

MESH = pl.DeviceIdType.MESH
ANY = pl.BlockSpec(memory_space=pl.ANY)
VMEM = pl.BlockSpec(memory_space=pltpu.VMEM)
DMA = pltpu.SemaphoreType.DMA
f32, bf16 = jnp.float32, jnp.bfloat16

CONV = 4
SCALE = 0.5
EPS = 1e-06
LANES = 128
RATE_AT = 64
HALO = 8


def shape(dims, kind):
    return jax.ShapeDtypeStruct(tuple(dims), kind)


def product(left, right, dims):
    return lax.dot_general(
        left.astype(bf16), right.astype(bf16), (dims, ((), ())), preferred_element_type=f32
    )


def mm(left, right):
    return product(left, right, ((1,), (0,)))


def mt(left, right):
    return product(left, right, ((1,), (1,)))


def tm(left, right):
    return product(left, right, ((0,), (0,)))


def params(collective, limit=58 << 20):
    return pltpu.CompilerParams(
        collective_id=collective, has_side_effects=True, vmem_limit_bytes=limit
    )


def grid_of(size):
    rows = lax.broadcasted_iota(jnp.int32, (size, size), 0)
    cols = lax.broadcasted_iota(jnp.int32, (size, size), 1)
    return rows, cols


def halves(values):
    high = values.astype(bf16)
    return high, (values - high.astype(f32)).astype(bf16)


def finer(left, right, dims):
    lhigh, llow = halves(left)
    rhigh, rlow = halves(right)
    (la,), (ra,) = dims
    return lax.dot_general(
        jnp.concatenate([lhigh, llow, lhigh], axis=la),
        jnp.concatenate([rhigh, rhigh, rlow], axis=ra),
        (dims, ((), ())),
        preferred_element_type=f32,
    )


def unit_inverses(stricts):
    size = stricts[0].shape[0]
    rows, cols = grid_of(size)
    eye = jnp.where(rows == cols, 1.0, 0.0)
    found = [eye - jnp.where((rows >> 1) == (cols >> 1), item, 0.0) for item in stricts]
    level = 1
    while (1 << level) < size:
        joined = ((rows >> (level + 1)) == (cols >> (level + 1))) & ((rows >> level) != (cols >> level))
        lows = [item.astype(bf16) for item in found]
        inner = [mm(jnp.where(joined, item, 0.0), low) for item, low in zip(stricts, lows)]
        found = [item - mm(low, part) for item, low, part in zip(found, lows, inner)]
        level += 1
    lows = [item.astype(bf16) for item in found]
    errors = []
    for item, low in zip(stricts, lows):
        pair = jnp.concatenate(halves(item), axis=1)
        errors.append(eye - low.astype(f32) - mm(pair, jnp.concatenate([low, low], axis=0)))
    return [low.astype(f32) + mm(low, error) for low, error in zip(lows, errors)]


def normed(values, gain):
    return values * lax.rsqrt(jnp.mean(values * values, axis=-1, keepdims=True) + EPS) * gain


def norm_back(values, gain, grad):
    scale = lax.rsqrt(jnp.mean(values * values, axis=-1, keepdims=True) + EPS)
    weighted = gain * grad
    return scale * weighted - values * (scale * scale * scale) * jnp.mean(
        values * weighted, axis=-1, keepdims=True
    )


def greet(barrier, peers):
    count = 0
    for peer, condition in peers:

        def tell(peer=peer):
            pl.semaphore_signal(barrier, inc=1, device_id=peer, device_id_type=MESH)

        if condition is None:
            tell()
            count = count + 1
        else:
            pl.when(condition)(tell)
            count = count + jnp.where(condition, 1, 0)
    pl.semaphore_wait(barrier, count)


def remote(source, target, send_sem, recv_sem, peer):
    return pltpu.make_async_remote_copy(
        src_ref=source,
        dst_ref=target,
        send_sem=send_sem,
        recv_sem=recv_sem,
        device_id=peer,
        device_id_type=MESH,
    )


def column(block, lane):
    return block[:, lane : lane + 1]


def convolved(ext_ref, taps, s, length, at, width):
    total = None
    for i in range(CONV):
        rows = ext_ref[s, pl.ds(HALO - (CONV - 1) + i, length), pl.ds(at, width)]
        term = taps[i : i + 1, at : at + width] * rows
        total = term if total is None else total + term
    return total


def kept(lens_ref, s, c, length):
    place = c * length + lax.broadcasted_iota(jnp.int32, (length, 1), 0)
    return jnp.where(place < lens_ref[s], 1.0, 0.0)


def part_of(at, size):
    return pl.ds(pl.multiple_of(at * size, size), size)


class Cube:
    def __init__(self, t, src, out, first, second, held, send_sem, recv_sem, chunks):
        self.y, self.x = t // 2, lax.rem(t, 2)
        self.t, self.src, self.out = t, src, out
        self.first, self.second, self.held = first, second, held
        self.send_sem, self.recv_sem = send_sem, recv_sem
        self.chunks = chunks
        self.block = src.shape[0] // 4
        self.half_width = src.shape[1] // 2
        self.width = self.half_width // chunks
        self.beside = self.y * 2 + (1 - self.x)
        self.above = (1 - self.y) * 2 + self.x

    def peer(self, side):
        return {"tp": self.beside * (1 - side) + self.above * side}

    def columns(self, half, chunk):
        return pl.ds(
            pl.multiple_of(half * self.half_width + chunk * self.width, self.width), self.width
        )

    def copy(self, stage, half, chunk, j):
        wide = self.columns(half, chunk)
        slim = part_of(chunk, self.width)
        send, recv = self.send_sem.at[stage, half, chunk, j], self.recv_sem.at[stage, half, chunk, j]
        across = self.above * (1 - half) + self.beside * half
        if stage == 0:
            g = (1 - half) * (2 * j + 1 - self.x) + half * (2 * (1 - self.y) + j)
            source, target = self.src.at[part_of(g, self.block), wide], self.first.at[half, j, :, slim]
            side = half
        elif stage == 1:
            source, target = self.held.at[half, :, slim], self.second.at[half, :, slim]
            side = 1 - half
        else:
            g = self.t if j == 0 else across
            source = target = self.out.at[part_of(g, self.block), wide]
            side = 1 - half if stage == 2 else half
        return remote(source, target, send, recv, self.peer(side))

    def each(self, body):
        @pl.loop(0, 2 * self.chunks)
        def _(k):
            body(lax.rem(k, 2), k // 2)

    def start(self, half, chunk):
        self.copy(0, half, chunk, 0).start()
        self.copy(0, half, chunk, 1).start()

    def middle(self):
        def body(half, chunk):
            wide = self.columns(half, chunk)
            slim = part_of(chunk, self.width)
            for j in range(2):
                self.copy(0, half, chunk, j).wait_recv()
            across = self.above * (1 - half) + self.beside * half
            other = (1 - half) * (1 - self.y) + half * (1 - self.x)
            self.held[half, :, slim] = (
                self.src[part_of(across, self.block), wide].astype(f32)
                + self.first[half, other, :, slim].astype(f32)
            ).astype(bf16)
            self.copy(1, half, chunk, 0).start()

        self.each(body)

    def finish(self, total_ref):
        def body(half, chunk):
            wide = self.columns(half, chunk)
            slim = part_of(chunk, self.width)
            self.copy(1, half, chunk, 0).wait_recv()
            mine = (1 - half) * self.y + half * self.x
            total_ref[:, wide] = (
                self.src[part_of(self.t, self.block), wide].astype(f32)
                + self.first[half, mine, :, slim].astype(f32)
                + self.second[half, :, slim].astype(f32)
            )

        self.each(body)

    def spread(self):
        def body(half, chunk):
            self.copy(2, half, chunk, 0).start()
            self.copy(3, half, chunk, 0).start()

        self.each(body)

    def relay(self):
        def body(half, chunk):
            self.copy(2, half, chunk, 0).wait_recv()
            self.copy(3, half, chunk, 1).start()

        self.each(body)

    def done(self):
        def body(half, chunk):
            for j in range(2):
                self.copy(3, half, chunk, j).wait_recv()
            for stage in range(4):
                for j in range(2 if stage in (0, 3) else 1):
                    self.copy(stage, half, chunk, j).wait_send()

        self.each(body)


class Tail:
    def __init__(self, t, src, out, got, send_sem, recv_sem, size):
        self.t, self.src, self.out, self.got, self.size = t, src, out, got, size
        self.send_sem, self.recv_sem = send_sem, recv_sem
        self.block = src.shape[0] // size

    def copies(self, stage):
        found = []
        for i in range(self.size - 1):
            g = lax.rem(self.t + 1 + i, self.size)
            if stage == 0:
                source, target = self.src.at[part_of(g, self.block)], self.got.at[self.size - 2 - i]
            else:
                source = target = self.out.at[part_of(self.t, self.block)]
            found.append(
                remote(
                    source,
                    target,
                    self.send_sem.at[stage, i],
                    self.recv_sem.at[stage, self.size - 2 - i],
                    {"tp": g},
                )
            )
        return found

    def start(self, stage):
        for copy in self.copies(stage):
            copy.start()

    def wait(self, stage):
        for copy in self.copies(stage):
            copy.wait_recv()

    def total(self):
        self.wait(0)
        total = self.src[part_of(self.t, self.block), :].astype(f32)
        for i in range(self.size - 1):
            total = total + self.got[i].astype(f32)
        return total

    def done(self):
        for stage in range(2):
            for copy in self.copies(stage):
                copy.wait_send()


CHUNKS = 4


def cube_scratch(rows, model):
    block = rows // 4
    return [
        pltpu.VMEM((rows, model), bf16),
        pltpu.VMEM((2, 2, block, model // 2), bf16),
        pltpu.VMEM((2, block, model // 2), bf16),
        pltpu.VMEM((2, block, model // 2), bf16),
        pltpu.VMEM((block, model), f32),
        DMA((4, 2, CHUNKS, 2)),
        DMA((4, 2, CHUNKS, 2)),
    ]


def tail_scratch(rows, size):
    return [
        pltpu.VMEM((rows, LANES), bf16),
        pltpu.VMEM((size - 1, rows // size, LANES), bf16),
        DMA((2, size - 1)),
        DMA((2, size - 1)),
    ]


def tp_peers(t, size):
    return [({"tp": lax.rem(t + 1 + i, size)}, None) for i in range(size - 1)]


def stacked(pieces):
    rows = sum(piece.shape[0] for piece in pieces)
    fill = jnp.zeros((LANES - rows, pieces[0].shape[1]), f32)
    return jnp.concatenate([piece.astype(f32) for piece in pieces] + [fill], axis=0).astype(bf16)


def slot_loads(pairs, f, sems):
    loads = []
    for i, (own, other, scratch) in enumerate(pairs):
        loads.append(pltpu.make_async_copy(own, scratch.at[f], sems.at[i, 0]))
        loads.append(pltpu.make_async_copy(other, scratch.at[1 - f], sems.at[i, 1]))
    for load in loads:
        load.start()
    return loads


def unit_steps(units, body):
    step = 2 * LANES
    whole = units // step

    @pl.loop(0, whole)
    def _(k):
        body(part_of(k, step))

    if units % step:
        body(pl.ds(whole * step, units % step))


def mixer_kernel(
    sizes,
    lens_ref,
    x_ref,
    gain_ref,
    qtaps_ref,
    ktaps_ref,
    vtaps_ref,
    wq_ref,
    wk_ref,
    wv_ref,
    wr_ref,
    wide0,
    wide1,
    wide2,
    wide3,
    wide4,
    wide5,
    wide6,
    wide7,
    slim0,
    slim1,
    slim2,
    slim3,
    slim4,
    slim5,
    slim6,
    slim7,
    wo_ref,
    wg_ref,
    wu_ref,
    wd_ref,
    n1_ref,
    wqkv_out,
    wo_out,
    wg_out,
    wu_out,
    wd_out,
    wide_out,
    slim_out,
    into_ref,
    back_ref,
    ext_ref,
    inner_ref,
    rates_ref,
    inv_ref,
    wkey_ref,
    wval_ref,
    reach_ref,
    local_ref,
    map_ref,
    end_ref,
    w_ref,
    wr_all,
    halo_out,
    halo_in,
    back_f32,
    into_f32,
    send_sem,
    recv_sem,
    local_sem,
    store_sem,
    halo_send,
    halo_recv,
):
    seqs, length, heads, width, ctx_size = sizes
    cols = heads * width
    rows = seqs * length
    half = wq_ref.shape[0]
    model = 2 * half
    f = lax.axis_index("fsdp")
    c = lax.axis_index("ctx")
    mate = {"fsdp": 1 - f}
    greet(
        pltpu.get_barrier_semaphore(),
        [(mate, None), ({"ctx": c - 1}, c > 0), ({"ctx": c + 1}, c < ctx_size - 1)],
    )
    top = pl.ds(pl.multiple_of(f * half, half), half)
    moves = []
    for i, ref in enumerate((wide0, wide1, wide2, wide3, wide4, wide5, wide6, wide7)):
        moves.append((ref, wide_out.at[f, i]))
    at = 0
    for ref in (slim0, slim1, slim2, slim3, slim4, slim5, slim6, slim7):
        moves.append((ref, slim_out.at[f, :, at : at + ref.shape[1]]))
        at += ref.shape[1]
    moves += [
        (wr_ref, wr_all.at[:, top]),
        (wq_ref, w_ref.at[0, top]),
        (wk_ref, w_ref.at[1, top]),
        (wv_ref, w_ref.at[2, top]),
    ]
    near = [pltpu.make_async_copy(src, dst, local_sem.at[i]) for i, (src, dst) in enumerate(moves)]
    local_count = len(moves)
    moves += [(wo_ref, wo_out), (wg_ref, wg_out), (wu_ref, wu_out), (wd_ref, wd_out)]
    across = [
        remote(src, dst, send_sem.at[i], recv_sem.at[i], mate) for i, (src, dst) in enumerate(moves)
    ]
    for copy in across[:local_count] + near + across[local_count:]:
        copy.start()

    @pl.loop(0, seqs)
    def _(s):
        here = pl.ds(pl.multiple_of(s * length, length), length)
        n1_ref[here, :] = normed(x_ref[here, :].astype(f32), gain_ref[...]).astype(bf16)

    for i in range(local_count):
        near[i].wait()
        across[i].wait_recv()
    kinds = 4
    into_f32[...] = jnp.zeros_like(into_f32)
    back_f32[...] = jnp.zeros_like(back_f32)
    for core in range(2):
        for kind in range(kinds):
            spot = core * 32 + kind * 8
            into_f32[spot : spot + 8, :] = wide_out[core, kind].astype(f32)
        for kind in range(kinds):
            at = kind * cols
            wide = cols if kind < 3 else LANES
            back_f32[core * 32 + kind * 8 : core * 32 + kind * 8 + 8, at : at + wide] = slim_out[
                core, :, at : at + wide
            ].astype(f32)
    into_f32[RATE_AT : RATE_AT + 8, :] = wr_all[...].astype(f32)
    into_ref[...] = into_f32[...].astype(bf16)
    back_ref[...] = back_f32[...].astype(bf16)
    keep_w = [
        pltpu.make_async_copy(w_ref.at[i], wqkv_out.at[i], store_sem.at[i]) for i in range(3)
    ]
    for copy in keep_w:
        copy.start()

    @pl.loop(0, seqs)
    def _(s):
        here = pl.ds(pl.multiple_of(s * length, length), length)
        block = n1_ref[here, :]
        tail = mt(block, into_ref[...])
        inner = tail.astype(bf16)
        inner_ref[here, :] = inner
        for i in range(3):
            pre = mm(block, w_ref[i]) + SCALE * mm(inner, back_ref[:, i * cols : (i + 1) * cols])
            ext_ref[s, HALO : HALO + length, i * cols : (i + 1) * cols] = pre
            halo_out[s, :, i * cols : (i + 1) * cols] = pre[length - HALO :, :].astype(bf16)
        pre_rate = tail + SCALE * mm(inner, back_ref[:, 3 * cols :])
        rates_ref[here, :] = jax.nn.sigmoid(pre_rate) * kept(lens_ref, s, c, length)

    halo = remote(halo_out, halo_in, halo_send, halo_recv, {"ctx": c + 1})

    @pl.when(c < ctx_size - 1)
    def _():
        halo.start()

    @pl.when(c > 0)
    def _():
        halo.wait_recv()
        ext_ref[:, 0:HALO, :] = halo_in[...].astype(f32)

    @pl.when(c == 0)
    def _():
        ext_ref[:, 0:HALO, :] = jnp.zeros((seqs, HALO, 3 * cols), f32)

    taps = jnp.concatenate([qtaps_ref[...], ktaps_ref[...], vtaps_ref[...]], axis=1)
    row_at, col_at = grid_of(length)

    @pl.loop(0, seqs)
    def _(s):
        here = pl.ds(pl.multiple_of(s * length, length), length)
        rate_block = rates_ref[here, :]
        queries, keys, values, rates, stricts = [], [], [], [], []
        for h in range(heads):
            at = h * width
            parts = [
                jax.nn.silu(convolved(ext_ref, taps, s, length, i * cols + at, width))
                for i in range(3)
            ]
            query, key = [
                a * lax.rsqrt(jnp.sum(a * a, axis=-1, keepdims=True) + EPS) for a in parts[:2]
            ]
            rate = column(rate_block, RATE_AT + h)
            queries.append(query)
            keys.append(key)
            values.append(parts[2])
            rates.append(rate)
            stricts.append(
                jnp.where(row_at > col_at, rate * finer(key, key, ((1,), (1,))), 0.0)
            )
        inverses = unit_inverses(stricts)
        for h in range(heads):
            pair = s * heads + h
            query, key, value, rate, inverse = queries[h], keys[h], values[h], rates[h], inverses[h]
            wkey = mm(inverse, rate * key)
            wval = mm(inverse, rate * value)
            scores = jnp.where(row_at >= col_at, mt(query, key), 0.0)
            inv_ref[pair] = inverse.astype(bf16)
            wkey_ref[pair] = wkey.astype(bf16)
            wval_ref[pair] = wval
            reach_ref[pair] = (query - mm(scores, wkey)).astype(bf16)
            local_ref[pair] = mm(scores, wval)
            map_ref[pair] = (jnp.where(row_at == col_at, 1.0, 0.0) - tm(key, wkey)).astype(bf16)
            end_ref[pair] = tm(key, wval)

    for copy in across[local_count:]:
        copy.wait_recv()
    for copy in keep_w:
        copy.wait()
    for copy in across:
        copy.wait_send()

    @pl.when(c < ctx_size - 1)
    def _():
        halo.wait_send()


def attend_kernel(
    sizes,
    lens_ref,
    x_ref,
    gain_ref,
    head_gain_ref,
    map_ref,
    end_ref,
    reach_ref,
    local_ref,
    wide_ref,
    slim_ref,
    grad_ref,
    wo_own,
    wo_other,
    wd_own,
    wd_other,
    n2_ref,
    out_inner_ref,
    resid_ref,
    heads_ref,
    start_ref,
    active_ref,
    down_inner_ref,
    chain_out,
    wo_ref,
    wd_ref,
    load_sem,
    chain_send,
    chain_recv,
    *scratch,
):
    seqs, length, heads, width, ctx_size, tp_size = sizes
    cols = heads * width
    model = x_ref.shape[1]
    half_model = model // 2
    units = active_ref.shape[1]
    left_at = 3 * cols + LANES
    down_at = left_at + cols + 2 * units
    f = lax.axis_index("fsdp")
    c = lax.axis_index("ctx")
    t = lax.axis_index("tp")
    loads = slot_loads([(wo_own, wo_other, wo_ref), (wd_own, wd_other, wd_ref)], f, load_sem)
    greet(
        pltpu.get_barrier_semaphore(),
        [({"ctx": c - 1}, c > 0), ({"ctx": c + 1}, c < ctx_size - 1)] + tp_peers(t, tp_size),
    )
    src, first, second, held, total_ref, send_sem, recv_sem = scratch[:7]
    tail_src, tail_got, tail_send, tail_recv = scratch[7:]
    cube = Cube(t, src, n2_ref, first, second, held, send_sem, recv_sem, CHUNKS)
    tail = Tail(t, tail_src, out_inner_ref, tail_got, tail_send, tail_recv, tp_size)
    gain = head_gain_ref[...]

    @pl.loop(0, seqs)
    def _(s):
        pairs = pl.ds(s * heads, heads)
        hop = remote(
            chain_out.at[s], start_ref.at[pairs], chain_send.at[s], chain_recv.at[s], {"ctx": c + 1}
        )

        @pl.when(c > 0)
        def _():
            hop.wait_recv()

        @pl.when(c == 0)
        def _():
            start_ref[pairs] = jnp.zeros((heads, width, width), bf16)

        @pl.when(c < ctx_size - 1)
        def _():
            for h in range(heads):
                pair = s * heads + h
                chain_out[s, h] = (mm(map_ref[pair], start_ref[pair]) + end_ref[pair]).astype(bf16)
            hop.start()

        here = part_of(s, length)
        for h in range(heads):
            pair = s * heads + h
            mixed = mm(reach_ref[pair], start_ref[pair]) + local_ref[pair]
            heads_ref[here, h * width : (h + 1) * width] = normed(mixed, gain).astype(bf16)

    into = stacked([slim_ref[core, :, left_at : left_at + cols] for core in range(2)])
    low = heads_ref[...]
    tail_src[...] = mt(low, into).astype(bf16)
    tail.start(0)
    loads[0].wait()
    loads[1].wait()

    def project(half, chunk):
        src[:, cube.columns(half, chunk)] = mm(
            heads_ref[...], wo_ref[half, :, part_of(chunk, cube.width)]
        ).astype(bf16)
        cube.start(half, chunk)

    cube.each(project)
    down_from = stacked([wide_ref[core, 7] for core in range(2)])
    for s in range(seqs):
        here = pl.ds(s * length, length)
        down_inner_ref[here, :] = (
            kept(lens_ref, s, c, length) * (SCALE * mt(grad_ref[here, :], down_from))
        ).astype(bf16)
    loads[2].wait()
    loads[3].wait()

    def activate(at):
        into_down = stacked([slim_ref[core, :, pl.ds(down_at + at.start, at.size)] for core in range(2)])
        part = mt(grad_ref[:, :half_model], wd_ref[0, at, :])
        part = part + mt(grad_ref[:, half_model:], wd_ref[1, at, :])
        part = part + mm(down_inner_ref[...], into_down)
        for s in range(seqs):
            active_ref[s * length : (s + 1) * length, at] = (
                kept(lens_ref, s, c, length) * part[s * length : (s + 1) * length]
            )

    unit_steps(units, activate)
    cube.middle()
    cube.finish(total_ref)
    inner = tail.total().astype(bf16)
    here = part_of(t, length)
    right = stacked([wide_ref[core, 6] for core in range(2)])
    resid = x_ref[here, :].astype(f32) + total_ref[...] + SCALE * mm(inner, right)
    resid_ref[...] = resid
    out_inner_ref[here, :] = inner
    n2_ref[here, :] = normed(resid, gain_ref[...]).astype(bf16)
    cube.spread()
    tail.start(1)
    cube.relay()
    tail.wait(1)
    cube.done()
    tail.done()

    @pl.when(c < ctx_size - 1)
    def _():
        @pl.loop(0, seqs)
        def _(s):
            remote(
                chain_out.at[s],
                start_ref.at[pl.ds(0, heads)],
                chain_send.at[s],
                chain_recv.at[s],
                {"ctx": c + 1},
            ).wait_send()


def feed_kernel(
    sizes,
    lens_ref,
    n2_ref,
    active_ref,
    resid_ref,
    gain_ref,
    wide_ref,
    slim_ref,
    down_grad_ref,
    grad_ref,
    wg_own,
    wg_other,
    wu_own,
    wu_other,
    wd_own,
    wd_other,
    low_ref,
    inner_grad_ref,
    gresid_ref,
    down_ref,
    down_tail_ref,
    gate_right_ref,
    up_right_ref,
    down_left_ref,
    wg_ref,
    wu_ref,
    wd_ref,
    act_ref,
    dgate_ref,
    dup_ref,
    inner_ref,
    back_gate,
    back_up,
    own_grad,
    load_sem,
    grad_sem,
    *scratch,
):
    seqs, length, cols, ctx_size, tp_size = sizes
    model = n2_ref.shape[1]
    half_model = model // 2
    units = active_ref.shape[1]
    gate_at = 4 * cols + LANES
    up_at = gate_at + units
    down_at = up_at + units
    f = lax.axis_index("fsdp")
    c = lax.axis_index("ctx")
    t = lax.axis_index("tp")
    loads = slot_loads(
        [(wg_own, wg_other, wg_ref), (wu_own, wu_other, wu_ref), (wd_own, wd_other, wd_ref)],
        f,
        load_sem,
    )
    here = part_of(t, length)
    own_load = pltpu.make_async_copy(grad_ref.at[here], own_grad, grad_sem)
    own_load.start()
    greet(pltpu.get_barrier_semaphore(), tp_peers(t, tp_size))
    src, first, second, held, total_ref, send_sem, recv_sem = scratch[:7]
    tail_src, tail_got, tail_send, tail_recv = scratch[7:]
    cube = Cube(t, src, low_ref, first, second, held, send_sem, recv_sem, CHUNKS)
    tail = Tail(t, tail_src, inner_grad_ref, tail_got, tail_send, tail_recv, tp_size)
    into = stacked([wide_ref[core, 4 + kind] for core in range(2) for kind in range(2)])
    blank = jnp.zeros((8, units), bf16)
    gates = [slim_ref[core, :, gate_at : gate_at + units] for core in range(2)]
    ups = [slim_ref[core, :, up_at : up_at + units] for core in range(2)]
    back_gate[...] = stacked([gates[0], blank, gates[1], blank])
    back_up[...] = stacked([blank, ups[0], blank, ups[1]])
    inner_ref[...] = mt(n2_ref[...], into).astype(bf16)
    for load in loads[:4]:
        load.wait()

    def forward(at):
        pre = []
        for weight, back in ((wg_ref, back_gate), (wu_ref, back_up)):
            part = mm(n2_ref[:, :half_model], weight[0, :, at])
            part = part + mm(n2_ref[:, half_model:], weight[1, :, at])
            pre.append(part + SCALE * mm(inner_ref[...], back[:, at]))
        gate, up = pre
        sigma = jax.nn.sigmoid(gate)
        silu = gate * sigma
        active = active_ref[:, at]
        act_ref[:, at] = (silu * up).astype(bf16)
        dgate_ref[:, at] = (active * up * (sigma * (1.0 + gate * (1.0 - sigma)))).astype(bf16)
        dup_ref[:, at] = (active * silu).astype(bf16)

    unit_steps(units, forward)
    tail_src[...] = (
        SCALE * (mt(dgate_ref[...], back_gate[...]) + mt(dup_ref[...], back_up[...]))
    ).astype(bf16)
    tail.start(0)

    def project(half, chunk):
        rows = part_of(chunk, cube.width)
        src[:, cube.columns(half, chunk)] = (
            mt(dgate_ref[...], wg_ref[half, rows, :]) + mt(dup_ref[...], wu_ref[half, rows, :])
        ).astype(bf16)
        cube.start(half, chunk)

    cube.each(project)
    cube.middle()
    for load in loads[4:]:
        load.wait()

    def descend(half, chunk):
        down_ref[:, cube.columns(half, chunk)] = mm(
            act_ref[...], wd_ref[half, :, part_of(chunk, cube.width)]
        ).astype(bf16)

    cube.each(descend)
    cube.finish(total_ref)
    own_load.wait()
    inner = tail.total().astype(bf16)
    grad_second = total_ref[...] + mm(inner, into)
    grad = own_grad[...].astype(f32) * kept(lens_ref, t, c, length) + norm_back(
        resid_ref[...], gain_ref[...], grad_second
    )
    gresid_ref[...] = grad
    low_ref[here, :] = grad.astype(bf16)
    inner_grad_ref[here, :] = inner
    cube.spread()
    tail.start(1)
    into_down = stacked([slim_ref[core, :, down_at : down_at + units] for core in range(2)])
    down_tail_ref[...] = mt(act_ref[...], into_down).astype(bf16)
    gate_right_ref[...] = SCALE * tm(inner_ref[...], dgate_ref[...])
    cube.relay()
    up_right_ref[...] = SCALE * tm(inner_ref[...], dup_ref[...])
    down_left_ref[...] = tm(down_grad_ref[...], act_ref[...])
    tail.wait(1)
    cube.done()
    tail.done()


def back_kernel(
    sizes,
    lens_ref,
    low_ref,
    head_gain_ref,
    start_ref,
    map_ref,
    reach_ref,
    local_ref,
    inv_ref,
    wkey_ref,
    wval_ref,
    ext_ref,
    qtaps_ref,
    ktaps_ref,
    vtaps_ref,
    rates_ref,
    wide_ref,
    slim_ref,
    wo_own,
    wo_other,
    heads_ref,
    out_inner_ref,
    src,
    tail_src,
    resid_ref,
    grad_ref,
    n2_ref,
    feed_grad_ref,
    pre_ref,
    block_ref,
    out_left_ref,
    out_right_ref,
    down_right_ref,
    feed_left_ref,
    wo_ref,
    dheads_ref,
    dmix_ref,
    after_ref,
    chain_out,
    gconv_ref,
    halo_out,
    halo_in,
    down_inner_ref,
    load_sem,
    chain_send,
    chain_recv,
    halo_send,
    halo_recv,
    *scratch,
):
    seqs, length, heads, width, ctx_size, tp_size = sizes
    cols = heads * width
    model = low_ref.shape[1]
    half_model = model // 2
    left_at = 3 * cols + LANES
    f = lax.axis_index("fsdp")
    c = lax.axis_index("ctx")
    t = lax.axis_index("tp")
    loads = slot_loads([(wo_own, wo_other, wo_ref)], f, load_sem)
    greet(
        pltpu.get_barrier_semaphore(),
        [({"ctx": c - 1}, c > 0), ({"ctx": c + 1}, c < ctx_size - 1)] + tp_peers(t, tp_size),
    )
    first, second, held, total_ref, send_sem, recv_sem = scratch[:6]
    tail_got, tail_send, tail_recv = scratch[6:]
    cube = Cube(t, src, block_ref, first, second, held, send_sem, recv_sem, CHUNKS)
    tail = Tail(t, tail_src, down_inner_ref, tail_got, tail_send, tail_recv, tp_size)
    cube.each(cube.start)
    tail.start(0)
    mine = part_of(t, length)
    gain = head_gain_ref[...]
    taps = jnp.concatenate([qtaps_ref[...], ktaps_ref[...], vtaps_ref[...]], axis=1)
    row_at, col_at = grid_of(length)
    gconv_ref[...] = jnp.zeros_like(gconv_ref)
    from_out = stacked([wide_ref[core, 6] for core in range(2)])
    into_out = stacked([slim_ref[core, :, left_at : left_at + cols] for core in range(2)])
    inner_grad = (SCALE * mt(low_ref[...], from_out)).astype(bf16)
    for load in loads:
        load.wait()
    dheads_ref[...] = (
        mt(low_ref[:, :half_model], wo_ref[0])
        + mt(low_ref[:, half_model:], wo_ref[1])
        + mm(inner_grad, into_out)
    )
    out_left_ref[...] = tm(inner_grad, heads_ref[...])

    @pl.loop(0, seqs)
    def _(s):
        here = part_of(s, length)
        pairs = pl.ds(s * heads, heads)
        hop = remote(
            chain_out.at[s], after_ref.at[pairs], chain_send.at[s], chain_recv.at[s], {"ctx": c - 1}
        )
        for h in range(heads):
            pair = s * heads + h
            mixed = mm(reach_ref[pair], start_ref[pair]) + local_ref[pair]
            dmix_ref[pair] = norm_back(mixed, gain, dheads_ref[here, h * width : (h + 1) * width])

        @pl.when(c < ctx_size - 1)
        def _():
            hop.wait_recv()

        @pl.when(c == ctx_size - 1)
        def _():
            after_ref[pairs] = jnp.zeros((heads, width, width), bf16)

        @pl.when(c > 0)
        def _():
            for h in range(heads):
                pair = s * heads + h
                chain_out[s, h] = (
                    tm(map_ref[pair], after_ref[pair]) + tm(reach_ref[pair], dmix_ref[pair])
                ).astype(bf16)
            hop.start()

    cube.middle()

    @pl.loop(0, seqs)
    def _(s):
        here = part_of(s, length)
        rate_block = rates_ref[here, :]
        rate_grads = jnp.zeros((length, LANES), f32)
        lane = lax.broadcasted_iota(jnp.int32, (length, LANES), 1)
        for h in range(heads):
            pair = s * heads + h
            at = h * width
            convs = [convolved(ext_ref, taps, s, length, i * cols + at, width) for i in range(3)]
            sigmas = [jax.nn.sigmoid(a) for a in convs]
            acts = [a * b for a, b in zip(convs, sigmas)]
            scales = [
                lax.rsqrt(jnp.sum(a * a, axis=-1, keepdims=True) + EPS) for a in acts[:2]
            ]
            query, key = [a * b for a, b in zip(acts, scales)]
            value = acts[2]
            rate = column(rate_block, RATE_AT + h)
            start, after = start_ref[pair], after_ref[pair]
            dmix = dmix_ref[pair]
            inverse = inv_ref[pair]
            fresh = wval_ref[pair] - mm(wkey_ref[pair], start)
            products = mt(key, key)
            scores = jnp.where(row_at >= col_at, mt(query, key), 0.0)
            dfresh = tm(scores, dmix) + mm(key, after)
            dvalue = tm(inverse, dfresh)
            dkey_in = -mt(dvalue, start)
            dscores = jnp.where(row_at >= col_at, mt(dmix, fresh), 0.0)
            dquery = mt(dmix, start) + mm(dscores, key)
            dstrict = jnp.where(row_at > col_at, -mt(dvalue, fresh), 0.0)
            dprod = rate * dstrict
            dkey = (
                tm(dscores, query)
                + mt(fresh, after)
                + rate * dkey_in
                + mm(dprod, key)
                + tm(dprod, key)
            )
            drate = jnp.sum(dstrict * products + dvalue * value + dkey_in * key, axis=-1, keepdims=True)
            grads = [
                scale * grad - act * (scale * scale * scale) * jnp.sum(act * grad, axis=-1, keepdims=True)
                for act, scale, grad in zip(acts, scales, (dquery, dkey))
            ] + [rate * dvalue]
            for i in range(3):
                slope = sigmas[i] * (1.0 + convs[i] * (1.0 - sigmas[i]))
                gconv_ref[pl.ds(HALO, length), pl.ds(i * cols + at, width)] = grads[i] * slope
            rate_grads = rate_grads + jnp.where(
                lane == RATE_AT + h, drate * rate * (1.0 - rate), 0.0
            )
        for i in range(3 * heads):
            at = i * width
            total = None
            spill = None
            for j in range(CONV):
                tap = taps[j : j + 1, at : at + width]
                term = tap * gconv_ref[pl.ds(HALO + CONV - 1 - j, length), pl.ds(at, width)]
                edge = tap * gconv_ref[pl.ds(CONV - 1 - j, HALO), pl.ds(at, width)]
                total = term if total is None else total + term
                spill = edge if spill is None else spill + edge
            pre_ref[here, at : at + width] = total.astype(bf16)
            halo_out[0, s, :, at : at + width] = total[length - HALO :, :]
            halo_out[1, s, :, at : at + width] = spill
        pre_ref[here, 3 * cols :] = rate_grads.astype(bf16)

        @pl.when(s == 1)
        def _():
            cube.finish(total_ref)
            inner = tail.total().astype(bf16)
            right = stacked([wide_ref[core, 7] for core in range(2)])
            final = resid_ref[...] + total_ref[...] + SCALE * mm(inner, right)
            block_ref[mine, :] = (kept(lens_ref, t, c, length) * final).astype(bf16)
            down_inner_ref[mine, :] = inner
            cube.spread()
            tail.start(1)

        @pl.when(s == 2)
        def _():
            cube.relay()

    halo_in[1] = halo_out[1].astype(bf16)
    halo = remote(halo_in.at[1], halo_in.at[0], halo_send, halo_recv, {"ctx": c - 1})

    @pl.when(c > 0)
    def _():
        halo.start()

    @pl.when(c < ctx_size - 1)
    def _():
        halo.wait_recv()
        for s in range(seqs):
            last = s * length + length - 16
            block = pre_ref[last : last + 16, : 3 * cols].astype(f32)
            edge = (halo_out[0, s] + halo_in[0, s].astype(f32))
            pre_ref[last : last + 16, : 3 * cols] = jnp.concatenate(
                [block[:HALO], edge], axis=0
            ).astype(bf16)

    @pl.when(c > 0)
    def _():
        halo.wait_send()

        @pl.loop(0, seqs)
        def _(s):
            remote(
                chain_out.at[s], after_ref.at[pl.ds(0, heads)], chain_send.at[s], chain_recv.at[s],
                {"ctx": c - 1},
            ).wait_send()
    out_right_ref[...] = SCALE * tm(out_inner_ref[...], low_ref[...])
    feed_left_ref[...] = tm(feed_grad_ref[...], n2_ref[...])
    tail.wait(1)
    masked = jnp.concatenate(
        [
            kept(lens_ref, s, c, length) * down_inner_ref[s * length : (s + 1) * length, :].astype(f32)
            for s in range(seqs)
        ],
        axis=0,
    )
    down_right_ref[...] = SCALE * tm(masked, grad_ref[...])
    cube.done()
    tail.done()


def first_kernel(
    sizes,
    pre_ref,
    w_ref,
    back_ref,
    into_ref,
    x_ref,
    gain_ref,
    gresid_ref,
    n1_ref,
    inner_ref,
    grad_ref,
    left_ref,
    right_ref,
    inner_grad_ref,
    *scratch,
):
    (tp_size,) = sizes
    t = lax.axis_index("tp")
    block = x_ref.shape[0] // tp_size
    half_model = x_ref.shape[1] // 2
    cols = w_ref.shape[2]
    greet(pltpu.get_barrier_semaphore(), tp_peers(t, tp_size))
    src, first, second, held, total_ref, send_sem, recv_sem = scratch[:7]
    tail_src, tail_got, tail_send, tail_recv = scratch[7:]
    cube = Cube(t, src, grad_ref, first, second, held, send_sem, recv_sem, CHUNKS)
    tail = Tail(t, tail_src, inner_grad_ref, tail_got, tail_send, tail_recv, tp_size)
    tail_src[...] = (SCALE * mt(pre_ref[...], back_ref[...])).astype(bf16)
    tail.start(0)

    def project(half, chunk):
        rows = cube.columns(half, chunk)
        part = mm(pre_ref[:, 3 * cols :], into_ref[:, rows])
        for i in range(3):
            part = part + mt(pre_ref[:, i * cols : (i + 1) * cols], w_ref[i, rows, :])
        src[:, rows] = part.astype(bf16)
        cube.start(half, chunk)

    cube.each(project)
    inner = tail.total().astype(bf16)
    here = part_of(t, block)
    inner_grad_ref[here, :] = inner
    tail.start(1)
    cube.middle()
    right_ref[...] = SCALE * tm(inner_ref[...], pre_ref[...])
    tail.wait(1)
    left_ref[...] = tm(inner_grad_ref[...], n1_ref[...])
    cube.finish(total_ref)
    grad_first = total_ref[...] + mm(inner, into_ref[...])
    grad = gresid_ref[...] + norm_back(x_ref[here, :].astype(f32), gain_ref[...], grad_first)
    grad_ref[here, :] = grad.astype(bf16)
    cube.spread()
    cube.relay()
    cube.done()
    tail.done()


def share_kernel(sizes, strips, *refs):
    ctx_size, wide = sizes
    count = len(refs) - 10
    ins, outs, (pack, mate_in, mine, recv, summed, send_sem, recv_sem, part_send, part_recv) = (
        refs[:count],
        refs[count : count + 1],
        refs[count + 1 :],
    )
    f = lax.axis_index("fsdp")
    c = lax.axis_index("ctx")
    mate = {"fsdp": 1 - f}
    others = [({"ctx": lax.rem(c + 1 + i, ctx_size)}, None) for i in range(ctx_size - 1)]
    greet(pltpu.get_barrier_semaphore(), [(mate, None)] + others)
    part = wide // ctx_size
    used = sum(strip[4] for strip in strips)
    for core in range(2):
        at = 0
        for index, row, step, col, width in strips:
            rows = row + core * step
            pack[core, :, at : at + width] = ins[index][rows : rows + 8, col : col + width].astype(bf16)
            at += width
        pack[core, :, used:] = jnp.zeros((8, wide - used), bf16)
    swap = remote(pack.at[1 - f], mate_in, send_sem, recv_sem, mate)
    swap.start()
    swap.wait()
    both = (pack[f].astype(f32) + mate_in[...].astype(f32)).astype(bf16)
    for j in range(ctx_size):
        mine[j] = both[:, j * part : (j + 1) * part]
    sends = []
    for i in range(ctx_size - 1):
        j = lax.rem(c + 1 + i, ctx_size)
        sends.append(
            remote(
                mine.at[j],
                recv.at[ctx_size - 2 - i],
                part_send.at[0, i],
                part_recv.at[0, ctx_size - 2 - i],
                {"ctx": j},
            )
        )
    for copy in sends:
        copy.start()
    for copy in sends:
        copy.wait_recv()
    total = mine[c].astype(f32)
    for i in range(ctx_size - 1):
        total = total + recv[i].astype(f32)
    summed[c] = total.astype(bf16)
    spreads = []
    for i in range(ctx_size - 1):
        j = lax.rem(c + 1 + i, ctx_size)
        spreads.append(
            remote(
                summed.at[c],
                summed.at[c],
                part_send.at[1, i],
                part_recv.at[1, ctx_size - 2 - i],
                {"ctx": j},
            )
        )
    for copy in spreads:
        copy.start()
    for copy in spreads:
        copy.wait_recv()
    for j in range(ctx_size):
        outs[0][:, j * part : (j + 1) * part] = summed[j].astype(f32)
    for copy in sends + spreads:
        copy.wait_send()


def deal_kernel(strips, packed_ref, *outs):
    at = 0
    for out, strip in zip(outs, strips):
        out[...] = packed_ref[:, at : at + strip[4]]
        at += strip[4]


def local(ctx_size, tp_size, *arguments):
    (
        hidden_in,
        seq_lengths,
        mixer_gain,
        feed_gain,
        query_weight,
        key_weight,
        value_weight,
        rate_weight,
        query_conv,
        key_conv,
        value_conv,
        head_gain,
        output_weight,
        gate_weight,
        up_weight,
        down_weight,
        query_left,
        query_right,
        key_left,
        key_right,
        value_left,
        value_right,
        rate_left,
        rate_right,
        output_left,
        output_right,
        gate_left,
        gate_right,
        up_left,
        up_right,
        down_left,
        down_right,
        output_grad,
    ) = arguments
    seqs, length, model = hidden_in.shape
    heads = rate_weight.shape[1]
    width = head_gain.shape[0]
    cols = heads * width
    rows = seqs * length
    units = gate_weight.shape[1]
    half = query_weight.shape[0]
    pairs = seqs * heads
    x = hidden_in.reshape(rows, model)
    grad_rows = output_grad.reshape(rows, model)
    rate_from = jnp.pad(rate_right, ((0, 0), (RATE_AT, LANES - RATE_AT - heads)))
    rate_rows = jnp.pad(rate_weight.T, ((0, 8 - heads), (0, 0)))
    wides = (
        query_left.T,
        key_left.T,
        value_left.T,
        rate_left.T,
        gate_left.T,
        up_left.T,
        output_right,
        down_right,
    )
    slims = (
        query_right,
        key_right,
        value_right,
        rate_from,
        output_left.T,
        gate_right,
        up_right,
        down_left.T,
    )
    slim_wide = sum(item.shape[1] for item in slims)
    gain1, gain2, gain3 = mixer_gain[None, :], feed_gain[None, :], head_gain[None, :]
    ext = length + HALO
    square = (pairs, width, width)
    tall = (pairs, length, width)
    block = rows // tp_size
    smem = pl.BlockSpec(memory_space=pltpu.SMEM)
    (
        n1,
        wqkv,
        wo,
        wg,
        wu,
        wd,
        wide_all,
        slim_all,
        into,
        back,
        pre_ext,
        inner,
        rates,
        inverse,
        wkey,
        wval,
        reach,
        local_out,
        step_map,
        end_state,
    ) = pl.pallas_call(
        functools.partial(mixer_kernel, (seqs, length, heads, width, ctx_size)),
        out_shape=(
            shape((rows, model), bf16),
            shape((3, model, cols), bf16),
            shape(output_weight.shape, bf16),
            shape(gate_weight.shape, bf16),
            shape(up_weight.shape, bf16),
            shape(down_weight.shape, bf16),
            shape((2, 8, 8, model), bf16),
            shape((2, 8, slim_wide), bf16),
            shape((LANES, model), bf16),
            shape((LANES, 3 * cols + LANES), bf16),
            shape((seqs, ext, 3 * cols), f32),
            shape((rows, LANES), bf16),
            shape((rows, LANES), f32),
            shape((pairs, length, length), bf16),
            shape(tall, bf16),
            shape(tall, f32),
            shape(tall, bf16),
            shape(tall, f32),
            shape(square, bf16),
            shape(square, f32),
        ),
        in_specs=[smem] + [VMEM] * 5 + [ANY] * 24,
        out_specs=(VMEM,) + (ANY,) * 5 + (VMEM,) * 14,
        scratch_shapes=[
            pltpu.VMEM((3, model, cols), bf16),
            pltpu.VMEM((8, model), bf16),
            pltpu.VMEM((seqs, HALO, 3 * cols), bf16),
            pltpu.VMEM((seqs, HALO, 3 * cols), bf16),
            pltpu.VMEM((LANES, 3 * cols + LANES), f32),
            pltpu.VMEM((LANES, model), f32),
            DMA((24,)),
            DMA((24,)),
            DMA((20,)),
            DMA((3,)),
            DMA,
            DMA,
        ],
        compiler_params=params(0),
        name="mixer",
    )(
        seq_lengths,
        x,
        gain1,
        query_conv,
        key_conv,
        value_conv,
        query_weight,
        key_weight,
        value_weight,
        rate_rows,
        *wides,
        *slims,
        output_weight,
        gate_weight,
        up_weight,
        down_weight,
    )
    mixer_sizes = (seqs, length, heads, width, ctx_size, tp_size)
    second, out_inner, residual, heads_low, start, active, down_grad = pl.pallas_call(
        functools.partial(attend_kernel, mixer_sizes),
        out_shape=(
            shape((rows, model), bf16),
            shape((rows, LANES), bf16),
            shape((block, model), f32),
            shape((rows, cols), bf16),
            shape(square, bf16),
            shape((rows, units), f32),
            shape((rows, LANES), bf16),
        ),
        in_specs=[smem] + [VMEM] * 10 + [ANY] * 4,
        out_specs=(VMEM,) * 7,
        scratch_shapes=[
            pltpu.VMEM((seqs, heads, width, width), bf16),
            pltpu.VMEM((2,) + output_weight.shape, bf16),
            pltpu.VMEM((2,) + down_weight.shape, bf16),
            DMA((2, 2)),
            DMA((seqs,)),
            DMA((seqs,)),
        ]
        + cube_scratch(rows, model)
        + tail_scratch(rows, tp_size),
        compiler_params=params(1),
        name="attend",
    )(
        seq_lengths,
        x,
        gain2,
        gain3,
        step_map,
        end_state,
        reach,
        local_out,
        wide_all,
        slim_all,
        grad_rows,
        output_weight,
        wo,
        down_weight,
        wd,
    )
    (
        resid_low,
        feed_grad,
        grad_residual,
        down_part,
        down_tail,
        gate_right_grad,
        up_right_grad,
        down_left_grad,
    ) = pl.pallas_call(
        functools.partial(feed_kernel, (seqs, length, cols, ctx_size, tp_size)),
        out_shape=(
            shape((rows, model), bf16),
            shape((rows, LANES), bf16),
            shape((block, model), f32),
            shape((rows, model), bf16),
            shape((rows, LANES), bf16),
            shape((LANES, units), f32),
            shape((LANES, units), f32),
            shape((LANES, units), f32),
        ),
        in_specs=[smem] + [VMEM] * 7 + [ANY] * 7,
        out_specs=(VMEM,) * 8,
        scratch_shapes=[
            pltpu.VMEM((2,) + gate_weight.shape, bf16),
            pltpu.VMEM((2,) + up_weight.shape, bf16),
            pltpu.VMEM((2,) + down_weight.shape, bf16),
            pltpu.VMEM((rows, units), bf16),
            pltpu.VMEM((rows, units), bf16),
            pltpu.VMEM((rows, units), bf16),
            pltpu.VMEM((rows, LANES), bf16),
            pltpu.VMEM((LANES, units), bf16),
            pltpu.VMEM((LANES, units), bf16),
            pltpu.VMEM((block, model), bf16),
            DMA((3, 2)),
            DMA,
        ]
        + cube_scratch(rows, model)
        + tail_scratch(rows, tp_size),
        compiler_params=params(2),
        name="feed",
    )(
        seq_lengths,
        second,
        active,
        residual,
        gain2,
        wide_all,
        slim_all,
        down_grad,
        grad_rows,
        gate_weight,
        wg,
        up_weight,
        wu,
        down_weight,
        wd,
    )
    grad_pre, block_out, out_left, out_right, down_right_grad, feed_left = pl.pallas_call(
        functools.partial(back_kernel, mixer_sizes),
        out_shape=(
            shape((rows, 3 * cols + LANES), bf16),
            shape((rows, model), bf16),
            shape((LANES, cols), f32),
            shape((LANES, model), f32),
            shape((LANES, model), f32),
            shape((LANES, model), f32),
        ),
        in_specs=[smem] + [VMEM] * 16 + [ANY] * 2 + [VMEM] * 8,
        out_specs=(VMEM,) * 6,
        scratch_shapes=[
            pltpu.VMEM((2,) + output_weight.shape, bf16),
            pltpu.VMEM((rows, cols), f32),
            pltpu.VMEM(tall, f32),
            pltpu.VMEM(square, bf16),
            pltpu.VMEM((seqs, heads, width, width), bf16),
            pltpu.VMEM((HALO + length + HALO, 3 * cols), f32),
            pltpu.VMEM((2, seqs, HALO, 3 * cols), f32),
            pltpu.VMEM((2, seqs, HALO, 3 * cols), bf16),
            pltpu.VMEM((rows, LANES), bf16),
            DMA((1, 2)),
            DMA((seqs,)),
            DMA((seqs,)),
            DMA,
            DMA,
        ]
        + cube_scratch(rows, model)[1:]
        + tail_scratch(rows, tp_size)[1:],
        compiler_params=params(3),
        name="back",
    )(
        seq_lengths,
        resid_low,
        gain3,
        start,
        step_map,
        reach,
        local_out,
        inverse,
        wkey,
        wval,
        pre_ext,
        query_conv,
        key_conv,
        value_conv,
        rates,
        wide_all,
        slim_all,
        output_weight,
        wo,
        heads_low,
        out_inner,
        down_part,
        down_tail,
        residual,
        grad_rows,
        second,
        feed_grad,
    )
    input_grad, mixer_left, mixer_right = pl.pallas_call(
        functools.partial(first_kernel, (tp_size,)),
        out_shape=(
            shape((rows, model), bf16),
            shape((LANES, model), f32),
            shape((LANES, 3 * cols + LANES), f32),
        ),
        in_specs=[VMEM] * 9,
        out_specs=(VMEM,) * 3,
        scratch_shapes=[pltpu.VMEM((rows, LANES), bf16)]
        + cube_scratch(rows, model)
        + tail_scratch(rows, tp_size),
        compiler_params=params(4),
        name="first",
    )(grad_pre, wqkv, back, into, x, gain1, grad_residual, n1, inner)
    sources = [
        mixer_left,
        mixer_right,
        feed_left,
        gate_right_grad,
        up_right_grad,
        out_left,
        out_right,
        down_left_grad,
        down_right_grad,
    ]
    strips = []
    for kind in range(4):
        strips.append((0, kind * 8, 32, 0, model))
        strips.append((1, kind * 8, 32, kind * cols, cols if kind < 3 else LANES))
    strips += [
        (5, 0, 8, 0, cols),
        (6, 0, 8, 0, model),
        (2, 0, 16, 0, model),
        (3, 0, 16, 0, units),
        (2, 8, 16, 0, model),
        (4, 8, 16, 0, units),
        (7, 0, 8, 0, units),
        (8, 0, 8, 0, model),
    ]
    strips = tuple(strips)
    used = sum(item[4] for item in strips)
    grain = LANES * ctx_size
    total_wide = -(-used // grain) * grain
    packed = pl.pallas_call(
        functools.partial(share_kernel, (ctx_size, total_wide), strips),
        out_shape=(shape((8, total_wide), f32),),
        in_specs=[VMEM] * len(sources),
        out_specs=(VMEM,),
        scratch_shapes=[
            pltpu.VMEM((2, 8, total_wide), bf16),
            pltpu.VMEM((8, total_wide), bf16),
            pltpu.VMEM((ctx_size, 8, total_wide // ctx_size), bf16),
            pltpu.VMEM((ctx_size - 1, 8, total_wide // ctx_size), bf16),
            pltpu.VMEM((ctx_size, 8, total_wide // ctx_size), bf16),
            DMA,
            DMA,
            DMA((2, ctx_size - 1)),
            DMA((2, ctx_size - 1)),
        ],
        compiler_params=params(5),
        name="share",
    )(*sources)[0]
    shares = list(
        pl.pallas_call(
            functools.partial(deal_kernel, strips),
            out_shape=tuple(shape((8, item[4]), f32) for item in strips),
            in_specs=[VMEM],
            out_specs=(VMEM,) * len(strips),
            name="deal",
        )(packed)
    )
    shares[7] = shares[7][:, RATE_AT : RATE_AT + heads]
    lefts = (0, 2, 4, 6, 8, 10, 12, 14)
    shares = [item.T if i in lefts else item for i, item in enumerate(shares)]
    return (
        block_out.reshape(seqs, length, model),
        input_grad.reshape(seqs, length, model),
    ) + tuple(shares)


def solution(mesh):
    placed = (
        P("fsdp", "ctx", None),
        P("fsdp"),
        P(),
        P(),
        P("fsdp", "tp"),
        P("fsdp", "tp"),
        P("fsdp", "tp"),
        P("fsdp", "tp"),
        P(None, "tp"),
        P(None, "tp"),
        P(None, "tp"),
        P(),
        P("tp", "fsdp"),
        P("fsdp", "tp"),
        P("fsdp", "tp"),
        P("tp", "fsdp"),
    )
    left_in, left_over, right_over, right_in = (
        P(None, "fsdp"),
        P("tp", "fsdp"),
        P("fsdp", None),
        P("fsdp", "tp"),
    )
    adapters = (left_in, right_in) * 4 + (left_over, right_over) + (left_in, right_in) * 2 + (
        left_over,
        right_over,
    )
    rows = P("fsdp", "ctx", None)
    return jax.shard_map(
        functools.partial(local, mesh.shape["ctx"], mesh.shape["tp"]),
        mesh=mesh,
        in_specs=placed + adapters + (rows,),
        out_specs=(rows, rows) + adapters,
        check_vma=False,
    )
```

time: 1520 us -> 318 us (0.21)
  other arithmetic: 547 us -> 0 us
  waiting for transfers between devices: 488 us -> 0 us
  matrix products: 312 us -> 0 us
  Pallas kernels: 0 us -> 309 us
  blocking collectives: 65 us -> 0 us
  local copies, waits for them, and re-layouts: 69 us -> 7.81 us
  between operations: 16.8 us -> 0.72 us
    another operation x30 -> x0, other arithmetic: 484 us -> none  [the longest x16 321 us: block_solve(): lax.linalg.triangular_solve(system, rate_block[:, :, None] * value_block,...]
    pallas_call x0 -> x7, Pallas kernels: none -> 309 us  [the longest x1 81 us: local(): pl.pallas_call(functools.partial(back_kernel, mixer_sizes), out_shape=(sh...]
    dot_general x126 -> x0, matrix products: 279 us -> none  [the longest x58 123 us: precise(): jnp.einsum(form, left_side, right_side, precision=lax.Precision.HIGHEST)]
    psum x5 -> x0, waiting for transfers between devices: 211 us -> none  [the longest x1 86.5 us: local(): lax.psum(matmul(activated_low, down_whole).astype(jnp.bfloat16), 'tp')]
    reduce_scatter x12 -> x0, waiting for transfers between devices: 127 us -> none  [the longest x1 11.5 us: local(): lax.psum_scatter(query_left_grad.astype(jnp.bfloat16), 'fsdp', scatter_di...]
    all_gather x11 -> x0, waiting for transfers between devices: 127 us -> none  [the longest x2 90.5 us: entering(): lax.all_gather(a.astype(kind), axis)]
    psum x2 -> x0, blocking collectives: 33.5 us -> none  [the longest x1 16.8 us: local(): lax.psum((adapter_scale * times_transposed(grad_gate_low, gate_from)).ast...]
    another operation x16 -> x0, matrix products: 33.2 us -> none  [the longest x8 17.6 us: block_solve(): lax.linalg.triangular_solve(system, rate_block[:, :, None] * key_block, l...]
  transfers between devices with their start and end apart: 31 -> 0, of which waited for: 27 -> 0; matrix products, arithmetic and copies ran while one was open for 24% -> 0% of each run, Pallas kernels for 0% -> 0%
where the time goes in v1:
time: 318 us
  Pallas kernels  309 us (97%)
  local copies, waits for them, and re-layouts  7.81 us (2%)
    pallas_call x1, Pallas kernels, local(): pl.pallas_call(functools.partial(back_kernel, mixer_sizes), out_shape=(sh...  81 us
    pallas_call x1, Pallas kernels, local(): pl.pallas_call(functools.partial(feed_kernel, (seqs, length, cols, ctx_si...  61 us
    pallas_call x1, Pallas kernels, local(): pl.pallas_call(functools.partial(attend_kernel, mixer_sizes), out_shape=(...  57.1 us
    pallas_call x1, Pallas kernels, local(): pl.pallas_call(functools.partial(first_kernel, (tp_size,)), out_shape=(sh...  42.7 us
    pallas_call x1, Pallas kernels, local(): pl.pallas_call(functools.partial(mixer_kernel, (seqs, length, heads, widt...  40.5 us
    pallas_call x1, Pallas kernels, local(): pl.pallas_call(functools.partial(share_kernel, (ctx_size, total_wide), st...  25 us

profile of v1, /device:TPU:0, one launch (start us, length us, event | category | flops | bytes accessed | tf_op | source)
XLA Modules:
  0.0 317.7 jit_solution(17453669880633448774)
XLA Ops:
  0.7 0.8 copy.51
  1.4 0.7 pad.9.slim3
  2.1 1.3 pad.8.wr_ref
  3.4 40.5 %mixer.1 = (bf16[512,2048]{1,0:T(8,128)(2,1)}, bf16[3,2048,512]{2,1,0:T(8,128)(2,1)}, bf16[512,1024]{1,0:T(8,128)(2,1)}, bf16[1024,1408]{1,0:T(8,128)(2,1)}, bf1...) custom-call(s32[4]{0:T(128)} %lens_ref.7, ...), custom_call_target="tpu_custom_call" | custom-call | tf_op jit(solution)/shard_map/mixer/pallas_call | solution.py:1320
  43.9 57.1 %attend.1 = (bf16[512,2048]{1,0:T(8,128)(2,1)}, bf16[512,128]{1,0:T(8,128)(2,1)}, f32[128,2048]{1,0:T(8,128)}, bf16[512,512]{1,0:T(8,128)(2,1)}, bf16[16,128,128...) custom-call(s32[4]{0:T(128)} %lens_ref.7, bf16[512,2048]{1,0:T(8,128)(2,1)} %bitcast.25, ...), custom_call_target="tpu_custom_call" | custom-call | tf_op jit(solution)/shard_map/attend/pallas_call | solution.py:1381
  101.0 61.0 %feed.1 = (bf16[512,2048]{1,0:T(8,128)(2,1)}, bf16[512,128]{1,0:T(8,128)(2,1)}, f32[128,2048]{1,0:T(8,128)}, bf16[512,2048]{1,0:T(8,128)(2,1)}, bf16[512,128]{1,...) custom-call(s32[4]{0:T(128)} %lens_ref.7, ...), custom_call_target="tpu_custom_call" | custom-call | tf_op jit(solution)/shard_map/feed/pallas_call | solution.py:1432
  162.0 81.0 %back.1 = (bf16[512,1664]{1,0:T(8,128)(2,1)}, bf16[512,2048]{1,0:T(8,128)(2,1)}, f32[128,512]{1,0:T(8,128)}, f32[128,2048]{1,0:T(8,128)}, f32[128,2048]{1,0:T(8,128)}, /*index=5*/f32[128,2048]{1,0:T(8,128)}) custom-call(s32[4]{0:T(128)} %lens_ref.7, bf16[512,2048]{1,0:T(8,128)(2,1)} %get-tuple-element.92.low_ref, f32[1,128]{1,0:T(1,128)} %bitcast.46, ...), custom_call_target="tpu_custom_call" | custom-call | tf_op jit(solution)/shard_map/back/pallas_call | solution.py:1481
  243.0 42.7 %first.1 = (bf16[512,2048]{1,0:T(8,128)(2,1)}, f32[128,2048]{1,0:T(8,128)}, f32[128,1664]{1,0:T(8,128)}) custom-call(bf16[512,1664]{1,0:T(8,128)(2,1)} %get-tuple-element.105.pre_ref, bf16[3,2048,512]{2,1,0:T(8,128)(2,1)} %get-tuple-element.106.w_ref, bf16[128,1664]{1,0:T(8,128)(2,1)} %get-tuple-element.107.back_ref, ...), custom_call_target="tpu_custom_call" | custom-call | tf_op jit(solution)/shard_map/first/pallas_call | solution.py:1542
  285.7 0.0 copy-start
  285.7 25.0 %share.1.packed_ref = f32[8,23040]{1,0:T(8,128)} custom-call(f32[128,2048]{1,0:T(8,128)} %get-tuple-element.113.refs_0_, f32[128,1664]{1,0:T(8,128)} %get-tuple-element.114.refs_1_, f32[128,2048]{1,0:T(8,128)} %get-tuple-element.115.refs_2_, f32[128,1408]{1,0:T(8,128)} %get-tuple-element.116.refs_3_, f32[128,1408]{1,0:T(8,128)} %get-tuple-element.117.refs_4_, ...), custom_call_target="tpu_custom_call" | custom-call | tf_op jit(solution)/shard_map/share/pallas_call | solution.py:1586
  310.6 2.0 deal.1
  312.6 0.8 slice.3
  313.4 0.7 copy.52
  314.0 0.0 copy-done
  314.0 0.0 copy-start.1
  314.0 1.3 copy.55
  315.4 1.0 copy-done.1
  316.4 1.3 copy.56
Async XLA Ops:
  285.7 28.4 %copy-start = (bf16[512,2048]{1,0:T(8,128)(2,1)S(1)}, bf16[512,2048]{1,0:T(8,128)(2,1)}, u32[]{:S(2)}) copy-start(bf16[512,2048]{1,0:T(8,128)(2,1)} %get-tuple-element.104) | copy-start | bytes 6291460
  314.0 2.3 copy-start.1

commit v2 on v1

--- a/solution.py
+++ b/solution.py
@@ -364,6 +364,8 @@
     lens_ref,
     x_ref,
     gain_ref,
+    gain2_ref,
+    head_gain_ref,
     qtaps_ref,
     ktaps_ref,
     vtaps_ref,
@@ -387,16 +389,38 @@
     slim5,
     slim6,
     slim7,
-    wo_ref,
-    wg_ref,
-    wu_ref,
-    wd_ref,
+    wo_own,
+    wg_own,
+    wu_own,
+    wd_own,
+    grad_hbm,
+    n2_ref,
+    out_inner_ref,
+    resid_ref,
+    wo_other,
+    wg_other,
+    wu_other,
+    wd_other,
+    wqkv_out,
+    n1_out,
+    wide_hbm,
+    slim_hbm,
+    into_out,
+    back_out,
+    ext_out,
+    inner_out,
+    rates_out,
+    inv_out,
+    wkey_out,
+    wval_out,
+    reach_out,
+    local_out,
+    map_out,
+    heads_out,
+    start_out,
+    active_out,
+    down_inner_out,
     n1_ref,
-    wqkv_out,
-    wo_out,
-    wg_out,
-    wu_out,
-    wd_out,
     wide_out,
     slim_out,
     into_ref,
@@ -410,6 +434,10 @@
     reach_ref,
     local_ref,
     map_ref,
+    heads_ref,
+    start_ref,
+    active_ref,
+    down_inner_ref,
     end_ref,
     w_ref,
     wr_all,
@@ -417,25 +445,51 @@
     halo_in,
     back_f32,
     into_f32,
+    chain_out,
+    wo_ref,
+    wd_ref,
+    grad_ref,
     send_sem,
     recv_sem,
     local_sem,
     store_sem,
     halo_send,
     halo_recv,
+    load_sem,
+    grad_sem,
+    chain_send,
+    chain_recv,
+    *scratch,
 ):
-    seqs, length, heads, width, ctx_size = sizes
+    seqs, length, heads, width, ctx_size, tp_size = sizes
     cols = heads * width
-    rows = seqs * length
     half = wq_ref.shape[0]
     model = 2 * half
+    half_model = half
+    units = active_ref.shape[1]
+    left_at = 3 * cols + LANES
+    down_at = left_at + cols + 2 * units
     f = lax.axis_index("fsdp")
     c = lax.axis_index("ctx")
+    t = lax.axis_index("tp")
     mate = {"fsdp": 1 - f}
     greet(
         pltpu.get_barrier_semaphore(),
-        [(mate, None), ({"ctx": c - 1}, c > 0), ({"ctx": c + 1}, c < ctx_size - 1)],
-    )
+        [(mate, None), ({"ctx": c - 1}, c > 0), ({"ctx": c + 1}, c < ctx_size - 1)]
+        + tp_peers(t, tp_size),
+    )
+    src, first, second, held, total_ref, cube_send, cube_recv = scratch[:7]
+    tail_src, tail_got, tail_send, tail_recv = scratch[7:]
+    cube = Cube(t, src, n2_ref, first, second, held, cube_send, cube_recv, CHUNKS)
+    tail = Tail(t, tail_src, out_inner_ref, tail_got, tail_send, tail_recv, tp_size)
+    stores = []
+
+    def store(pairs):
+        for source, target in pairs:
+            copy = pltpu.make_async_copy(source, target, store_sem.at[len(stores)])
+            copy.start()
+            stores.append(copy)
+
     top = pl.ds(pl.multiple_of(f * half, half), half)
     moves = []
     for i, ref in enumerate((wide0, wide1, wide2, wide3, wide4, wide5, wide6, wide7)):
@@ -452,12 +506,17 @@
     ]
     near = [pltpu.make_async_copy(src, dst, local_sem.at[i]) for i, (src, dst) in enumerate(moves)]
     local_count = len(moves)
-    moves += [(wo_ref, wo_out), (wg_ref, wg_out), (wu_ref, wu_out), (wd_ref, wd_out)]
+    moves += [(wo_own, wo_other), (wg_own, wg_other), (wu_own, wu_other), (wd_own, wd_other)]
     across = [
         remote(src, dst, send_sem.at[i], recv_sem.at[i], mate) for i, (src, dst) in enumerate(moves)
     ]
-    for copy in across[:local_count] + near + across[local_count:]:
+    for copy in across[:local_count] + near:
         copy.start()
+    own_loads = [
+        pltpu.make_async_copy(wo_own, wo_ref.at[f], load_sem.at[0]),
+        pltpu.make_async_copy(wd_own, wd_ref.at[f], load_sem.at[2]),
+        pltpu.make_async_copy(grad_hbm, grad_ref, grad_sem),
+    ]
 
     @pl.loop(0, seqs)
     def _(s):
@@ -467,6 +526,8 @@
     for i in range(local_count):
         near[i].wait()
         across[i].wait_recv()
+    for copy in across[local_count:] + own_loads:
+        copy.start()
     kinds = 4
     into_f32[...] = jnp.zeros_like(into_f32)
     back_f32[...] = jnp.zeros_like(back_f32)
@@ -483,11 +544,8 @@
     into_f32[RATE_AT : RATE_AT + 8, :] = wr_all[...].astype(f32)
     into_ref[...] = into_f32[...].astype(bf16)
     back_ref[...] = back_f32[...].astype(bf16)
-    keep_w = [
-        pltpu.make_async_copy(w_ref.at[i], wqkv_out.at[i], store_sem.at[i]) for i in range(3)
-    ]
-    for copy in keep_w:
-        copy.start()
+    store([(w_ref, wqkv_out), (n1_ref, n1_out), (wide_out, wide_hbm), (slim_out, slim_hbm)])
+    store([(into_ref, into_out), (back_ref, back_out)])
 
     @pl.loop(0, seqs)
     def _(s):
@@ -521,8 +579,7 @@
     taps = jnp.concatenate([qtaps_ref[...], ktaps_ref[...], vtaps_ref[...]], axis=1)
     row_at, col_at = grid_of(length)
 
-    @pl.loop(0, seqs)
-    def _(s):
+    def solve(s):
         here = pl.ds(pl.multiple_of(s * length, length), length)
         rate_block = rates_ref[here, :]
         queries, keys, values, rates, stricts = [], [], [], [], []
@@ -549,82 +606,18 @@
             query, key, value, rate, inverse = queries[h], keys[h], values[h], rates[h], inverses[h]
             wkey = mm(inverse, rate * key)
             wval = mm(inverse, rate * value)
-            scores = jnp.where(row_at >= col_at, mt(query, key), 0.0)
+            scores = jnp.where(row_at >= col_at, finer(query, key, ((1,), (1,))), 0.0)
             inv_ref[pair] = inverse.astype(bf16)
             wkey_ref[pair] = wkey.astype(bf16)
             wval_ref[pair] = wval
             reach_ref[pair] = (query - mm(scores, wkey)).astype(bf16)
-            local_ref[pair] = mm(scores, wval)
+            local_ref[pair] = finer(scores, wval, ((1,), (0,)))
             map_ref[pair] = (jnp.where(row_at == col_at, 1.0, 0.0) - tm(key, wkey)).astype(bf16)
             end_ref[pair] = tm(key, wval)
 
-    for copy in across[local_count:]:
-        copy.wait_recv()
-    for copy in keep_w:
-        copy.wait()
-    for copy in across:
-        copy.wait_send()
-
-    @pl.when(c < ctx_size - 1)
-    def _():
-        halo.wait_send()
-
-
-def attend_kernel(
-    sizes,
-    lens_ref,
-    x_ref,
-    gain_ref,
-    head_gain_ref,
-    map_ref,
-    end_ref,
-    reach_ref,
-    local_ref,
-    wide_ref,
-    slim_ref,
-    grad_ref,
-    wo_own,
-    wo_other,
-    wd_own,
-    wd_other,
-    n2_ref,
-    out_inner_ref,
-    resid_ref,
-    heads_ref,
-    start_ref,
-    active_ref,
-    down_inner_ref,
-    chain_out,
-    wo_ref,
-    wd_ref,
-    load_sem,
-    chain_send,
-    chain_recv,
-    *scratch,
-):
-    seqs, length, heads, width, ctx_size, tp_size = sizes
-    cols = heads * width
-    model = x_ref.shape[1]
-    half_model = model // 2
-    units = active_ref.shape[1]
-    left_at = 3 * cols + LANES
-    down_at = left_at + cols + 2 * units
-    f = lax.axis_index("fsdp")
-    c = lax.axis_index("ctx")
-    t = lax.axis_index("tp")
-    loads = slot_loads([(wo_own, wo_other, wo_ref), (wd_own, wd_other, wd_ref)], f, load_sem)
-    greet(
-        pltpu.get_barrier_semaphore(),
-        [({"ctx": c - 1}, c > 0), ({"ctx": c + 1}, c < ctx_size - 1)] + tp_peers(t, tp_size),
-    )
-    src, first, second, held, total_ref, send_sem, recv_sem = scratch[:7]
-    tail_src, tail_got, tail_send, tail_recv = scratch[7:]
-    cube = Cube(t, src, n2_ref, first, second, held, send_sem, recv_sem, CHUNKS)
-    tail = Tail(t, tail_src, out_inner_ref, tail_got, tail_send, tail_recv, tp_size)
     gain = head_gain_ref[...]
 
-    @pl.loop(0, seqs)
-    def _(s):
+    def link(s):
         pairs = pl.ds(s * heads, heads)
         hop = remote(
             chain_out.at[s], start_ref.at[pairs], chain_send.at[s], chain_recv.at[s], {"ctx": c + 1}
@@ -651,12 +644,40 @@
             mixed = mm(reach_ref[pair], start_ref[pair]) + local_ref[pair]
             heads_ref[here, h * width : (h + 1) * width] = normed(mixed, gain).astype(bf16)
 
-    into = stacked([slim_ref[core, :, left_at : left_at + cols] for core in range(2)])
+    @pl.loop(0, seqs + ctx_size - 1)
+    def _(k):
+        @pl.when(k < seqs)
+        def _():
+            solve(k)
+
+        @pl.when((k >= c) & (k < c + seqs))
+        def _():
+            link(k - c)
+
+    store(
+        [
+            (ext_ref, ext_out),
+            (inner_ref, inner_out),
+            (rates_ref, rates_out),
+            (inv_ref, inv_out),
+            (wkey_ref, wkey_out),
+            (wval_ref, wval_out),
+            (reach_ref, reach_out),
+            (local_ref, local_out),
+            (map_ref, map_out),
+            (heads_ref, heads_out),
+            (start_ref, start_out),
+        ]
+    )
+    into = stacked([slim_out[core, :, left_at : left_at + cols] for core in range(2)])
     low = heads_ref[...]
     tail_src[...] = mt(low, into).astype(bf16)
     tail.start(0)
-    loads[0].wait()
-    loads[1].wait()
+    across[local_count].wait_recv()
+    wo_load = pltpu.make_async_copy(wo_other, wo_ref.at[1 - f], load_sem.at[1])
+    wo_load.start()
+    own_loads[0].wait()
+    wo_load.wait()
 
     def project(half, chunk):
         src[:, cube.columns(half, chunk)] = mm(
@@ -665,17 +686,22 @@
         cube.start(half, chunk)
 
     cube.each(project)
-    down_from = stacked([wide_ref[core, 7] for core in range(2)])
+    for copy in across[local_count + 1 :]:
+        copy.wait_recv()
+    wd_load = pltpu.make_async_copy(wd_other, wd_ref.at[1 - f], load_sem.at[3])
+    wd_load.start()
+    own_loads[2].wait()
+    down_from = stacked([wide_out[core, 7] for core in range(2)])
     for s in range(seqs):
         here = pl.ds(s * length, length)
         down_inner_ref[here, :] = (
             kept(lens_ref, s, c, length) * (SCALE * mt(grad_ref[here, :], down_from))
         ).astype(bf16)
-    loads[2].wait()
-    loads[3].wait()
+    own_loads[1].wait()
+    wd_load.wait()
 
     def activate(at):
-        into_down = stacked([slim_ref[core, :, pl.ds(down_at + at.start, at.size)] for core in range(2)])
+        into_down = stacked([slim_out[core, :, pl.ds(down_at + at.start, at.size)] for core in range(2)])
         part = mt(grad_ref[:, :half_model], wd_ref[0, at, :])
         part = part + mt(grad_ref[:, half_model:], wd_ref[1, at, :])
         part = part + mm(down_inner_ref[...], into_down)
@@ -685,24 +711,31 @@
             )
 
     unit_steps(units, activate)
+    store([(active_ref, active_out), (down_inner_ref, down_inner_out)])
     cube.middle()
     cube.finish(total_ref)
     inner = tail.total().astype(bf16)
     here = part_of(t, length)
-    right = stacked([wide_ref[core, 6] for core in range(2)])
+    right = stacked([wide_out[core, 6] for core in range(2)])
     resid = x_ref[here, :].astype(f32) + total_ref[...] + SCALE * mm(inner, right)
     resid_ref[...] = resid
     out_inner_ref[here, :] = inner
-    n2_ref[here, :] = normed(resid, gain_ref[...]).astype(bf16)
+    n2_ref[here, :] = normed(resid, gain2_ref[...]).astype(bf16)
     cube.spread()
     tail.start(1)
     cube.relay()
     tail.wait(1)
     cube.done()
     tail.done()
+    for copy in across:
+        copy.wait_send()
+    for copy in stores:
+        copy.wait()
 
     @pl.when(c < ctx_size - 1)
     def _():
+        halo.wait_send()
+
         @pl.loop(0, seqs)
         def _(s):
             remote(
@@ -838,13 +871,29 @@
     tail.start(1)
     into_down = stacked([slim_ref[core, :, down_at : down_at + units] for core in range(2)])
     down_tail_ref[...] = mt(act_ref[...], into_down).astype(bf16)
-    gate_right_ref[...] = SCALE * tm(inner_ref[...], dgate_ref[...])
+    gate_right_ref[...] = SCALE * tm(inner_ref[...], dgate_ref[...])[:32]
     cube.relay()
-    up_right_ref[...] = SCALE * tm(inner_ref[...], dup_ref[...])
-    down_left_ref[...] = tm(down_grad_ref[...], act_ref[...])
+    up_right_ref[...] = SCALE * tm(inner_ref[...], dup_ref[...])[:32]
+    down_left_ref[...] = tm(down_grad_ref[...], act_ref[...])[:32]
     tail.wait(1)
     cube.done()
     tail.done()
+
+
+def strip_plan(cols, model, units):
+    widths = (
+        ("ql", model), ("qr", cols), ("kl", model), ("kr", cols), ("vl", model), ("vr", cols),
+        ("rl", model), ("rr", LANES), ("ol", cols), ("or", model), ("gl", model), ("gr", units),
+        ("ul", model), ("ur", units), ("dl", units), ("dr", model),
+    )
+    plan, at = {}, 0
+    for name, wide in widths:
+        plan[name] = (at, wide)
+        at += wide
+    return plan, at
+
+
+BACK_LOADS = 24
 
 
 def back_kernel(
@@ -852,6 +901,44 @@
     lens_ref,
     low_ref,
     head_gain_ref,
+    gain_ref,
+    qtaps_ref,
+    ktaps_ref,
+    vtaps_ref,
+    wide_ref,
+    slim_ref,
+    tail_src,
+    feed_grad_ref,
+    out_inner_ref,
+    inner_ref,
+    gate_right_ref,
+    up_right_ref,
+    down_left_ref,
+    start_hbm,
+    map_hbm,
+    reach_hbm,
+    local_hbm,
+    inv_hbm,
+    wkey_hbm,
+    wval_hbm,
+    ext_hbm,
+    rates_hbm,
+    heads_hbm,
+    down_hbm,
+    resid_hbm,
+    grad_hbm,
+    n2_hbm,
+    n1_hbm,
+    x_hbm,
+    gresid_hbm,
+    w_hbm,
+    back_hbm,
+    into_hbm,
+    wo_own,
+    wo_other,
+    block_hbm,
+    input_grad_hbm,
+    packed_ref,
     start_ref,
     map_ref,
     reach_ref,
@@ -860,30 +947,20 @@
     wkey_ref,
     wval_ref,
     ext_ref,
-    qtaps_ref,
-    ktaps_ref,
-    vtaps_ref,
     rates_ref,
-    wide_ref,
-    slim_ref,
-    wo_own,
-    wo_other,
     heads_ref,
-    out_inner_ref,
     src,
-    tail_src,
     resid_ref,
     grad_ref,
-    n2_ref,
-    feed_grad_ref,
+    normed_ref,
+    x_ref,
+    gresid_ref,
+    w_ref,
+    back_ref,
+    into_ref,
+    wo_ref,
+    out_ref,
     pre_ref,
-    block_ref,
-    out_left_ref,
-    out_right_ref,
-    down_right_ref,
-    feed_left_ref,
-    wo_ref,
-    dheads_ref,
     dmix_ref,
     after_ref,
     chain_out,
@@ -891,64 +968,146 @@
     halo_out,
     halo_in,
     down_inner_ref,
+    keys_ref,
+    slopes_ref,
+    values_ref,
+    vslopes_ref,
+    dfresh_ref,
+    dkeys_ref,
+    fresh_ref,
+    tail2_src,
+    inner_grad_ref,
+    pack,
+    mate_in,
+    mine_ref,
+    got,
+    summed,
     load_sem,
+    store_sem,
     chain_send,
     chain_recv,
     halo_send,
     halo_recv,
-    *scratch,
+    swap_send,
+    swap_recv,
+    part_send,
+    part_recv,
+    first,
+    second,
+    held,
+    total_ref,
+    cube_send,
+    cube_recv,
+    cube2_send,
+    cube2_recv,
+    tail_got,
+    tail_send,
+    tail_recv,
+    tail2_got,
+    tail2_send,
+    tail2_recv,
 ):
     seqs, length, heads, width, ctx_size, tp_size = sizes
     cols = heads * width
     model = low_ref.shape[1]
     half_model = model // 2
+    units = gate_right_ref.shape[1]
     left_at = 3 * cols + LANES
+    plan, used = strip_plan(cols, model, units)
     f = lax.axis_index("fsdp")
     c = lax.axis_index("ctx")
     t = lax.axis_index("tp")
-    loads = slot_loads([(wo_own, wo_other, wo_ref)], f, load_sem)
+    mate = {"fsdp": 1 - f}
+    mine = part_of(t, length)
+    loads = {}
+
+    def fetch(name, source, target):
+        loads[name] = pltpu.make_async_copy(source, target, load_sem.at[len(loads)])
+        loads[name].start()
+
+    fetch("wo_own", wo_own, wo_ref.at[f])
+    fetch("wo_other", wo_other, wo_ref.at[1 - f])
+    fetch("src", down_hbm, src)
+    fetch("reach", reach_hbm, reach_ref)
+    fetch("start", start_hbm, start_ref)
+    fetch("local", local_hbm, local_ref)
+    fetch("map", map_hbm, map_ref)
+    fetch("ext", ext_hbm, ext_ref)
+    fetch("rates", rates_hbm, rates_ref)
+    fetch("wkey", wkey_hbm, wkey_ref)
+    fetch("wval", wval_hbm, wval_ref)
+    fetch("inv", inv_hbm, inv_ref)
+    fetch("heads", heads_hbm, heads_ref)
+    fetch("resid", resid_hbm, resid_ref)
+    fetch("n2", n2_hbm, normed_ref)
+    fetch("grad", grad_hbm, grad_ref)
     greet(
         pltpu.get_barrier_semaphore(),
-        [({"ctx": c - 1}, c > 0), ({"ctx": c + 1}, c < ctx_size - 1)] + tp_peers(t, tp_size),
-    )
-    first, second, held, total_ref, send_sem, recv_sem = scratch[:6]
-    tail_got, tail_send, tail_recv = scratch[6:]
-    cube = Cube(t, src, block_ref, first, second, held, send_sem, recv_sem, CHUNKS)
+        [(mate, None)]
+        + [({"ctx": lax.rem(c + 1 + i, ctx_size)}, None) for i in range(ctx_size - 1)]
+        + tp_peers(t, tp_size),
+    )
+    cube = Cube(t, src, out_ref, first, second, held, cube_send, cube_recv, CHUNKS)
     tail = Tail(t, tail_src, down_inner_ref, tail_got, tail_send, tail_recv, tp_size)
-    cube.each(cube.start)
+    cube2 = Cube(t, src, out_ref, first, second, held, cube2_send, cube2_recv, CHUNKS)
+    tail2 = Tail(t, tail2_src, inner_grad_ref, tail2_got, tail2_send, tail2_recv, tp_size)
+
+    def put(name, core, rows):
+        at, wide = plan[name]
+        pack[core, :, at : at + wide] = rows.astype(bf16)
+
     tail.start(0)
-    mine = part_of(t, length)
     gain = head_gain_ref[...]
     taps = jnp.concatenate([qtaps_ref[...], ktaps_ref[...], vtaps_ref[...]], axis=1)
     row_at, col_at = grid_of(length)
     gconv_ref[...] = jnp.zeros_like(gconv_ref)
     from_out = stacked([wide_ref[core, 6] for core in range(2)])
     into_out = stacked([slim_ref[core, :, left_at : left_at + cols] for core in range(2)])
-    inner_grad = (SCALE * mt(low_ref[...], from_out)).astype(bf16)
-    for load in loads:
-        load.wait()
-    dheads_ref[...] = (
+    out_grad = (SCALE * mt(low_ref[...], from_out)).astype(bf16)
+    loads["wo_own"].wait()
+    loads["wo_other"].wait()
+    dheads = (
         mt(low_ref[:, :half_model], wo_ref[0])
         + mt(low_ref[:, half_model:], wo_ref[1])
-        + mm(inner_grad, into_out)
-    )
-    out_left_ref[...] = tm(inner_grad, heads_ref[...])
+        + mm(out_grad, into_out)
+    )
+    for s in range(seqs):
+        for h in range(heads):
+            dmix_ref[s * heads + h] = dheads[
+                s * length : (s + 1) * length, h * width : (h + 1) * width
+            ]
+    loads["src"].wait()
+    cube.each(cube.start)
+    for name in ("reach", "start", "local", "map"):
+        loads[name].wait()
 
     @pl.loop(0, seqs)
     def _(s):
-        here = part_of(s, length)
-        pairs = pl.ds(s * heads, heads)
-        hop = remote(
-            chain_out.at[s], after_ref.at[pairs], chain_send.at[s], chain_recv.at[s], {"ctx": c - 1}
-        )
         for h in range(heads):
             pair = s * heads + h
             mixed = mm(reach_ref[pair], start_ref[pair]) + local_ref[pair]
-            dmix_ref[pair] = norm_back(mixed, gain, dheads_ref[here, h * width : (h + 1) * width])
+            dmix_ref[pair] = norm_back(mixed, gain, dmix_ref[pair])
+
+    for name in ("ext", "rates", "wkey", "wval", "inv"):
+        loads[name].wait()
+    fetch("w", w_hbm, w_ref)
+    fetch("back", back_hbm, back_ref)
+    fetch("into", into_hbm, into_ref)
+    fetch("x", x_hbm.at[mine], x_ref)
+    fetch("gresid", gresid_hbm, gresid_ref)
+
+    def hop_of(s):
+        pairs = pl.ds(s * heads, heads)
+        return remote(
+            chain_out.at[s], after_ref.at[pairs], chain_send.at[s], chain_recv.at[s], {"ctx": c - 1}
+        )
+
+    def link(s):
+        pairs = pl.ds(s * heads, heads)
 
         @pl.when(c < ctx_size - 1)
         def _():
-            hop.wait_recv()
+            hop_of(s).wait_recv()
 
         @pl.when(c == ctx_size - 1)
         def _():
@@ -961,61 +1120,12 @@
                 chain_out[s, h] = (
                     tm(map_ref[pair], after_ref[pair]) + tm(reach_ref[pair], dmix_ref[pair])
                 ).astype(bf16)
-            hop.start()
-
-    cube.middle()
-
-    @pl.loop(0, seqs)
-    def _(s):
+            hop_of(s).start()
+
+    def unconvolve(s, kind):
         here = part_of(s, length)
-        rate_block = rates_ref[here, :]
-        rate_grads = jnp.zeros((length, LANES), f32)
-        lane = lax.broadcasted_iota(jnp.int32, (length, LANES), 1)
         for h in range(heads):
-            pair = s * heads + h
-            at = h * width
-            convs = [convolved(ext_ref, taps, s, length, i * cols + at, width) for i in range(3)]
-            sigmas = [jax.nn.sigmoid(a) for a in convs]
-            acts = [a * b for a, b in zip(convs, sigmas)]
-            scales = [
-                lax.rsqrt(jnp.sum(a * a, axis=-1, keepdims=True) + EPS) for a in acts[:2]
-            ]
-            query, key = [a * b for a, b in zip(acts, scales)]
-            value = acts[2]
-            rate = column(rate_block, RATE_AT + h)
-            start, after = start_ref[pair], after_ref[pair]
-            dmix = dmix_ref[pair]
-            inverse = inv_ref[pair]
-            fresh = wval_ref[pair] - mm(wkey_ref[pair], start)
-            products = mt(key, key)
-            scores = jnp.where(row_at >= col_at, mt(query, key), 0.0)
-            dfresh = tm(scores, dmix) + mm(key, after)
-            dvalue = tm(inverse, dfresh)
-            dkey_in = -mt(dvalue, start)
-            dscores = jnp.where(row_at >= col_at, mt(dmix, fresh), 0.0)
-            dquery = mt(dmix, start) + mm(dscores, key)
-            dstrict = jnp.where(row_at > col_at, -mt(dvalue, fresh), 0.0)
-            dprod = rate * dstrict
-            dkey = (
-                tm(dscores, query)
-                + mt(fresh, after)
-                + rate * dkey_in
-                + mm(dprod, key)
-                + tm(dprod, key)
-            )
-            drate = jnp.sum(dstrict * products + dvalue * value + dkey_in * key, axis=-1, keepdims=True)
-            grads = [
-                scale * grad - act * (scale * scale * scale) * jnp.sum(act * grad, axis=-1, keepdims=True)
-                for act, scale, grad in zip(acts, scales, (dquery, dkey))
-            ] + [rate * dvalue]
-            for i in range(3):
-                slope = sigmas[i] * (1.0 + convs[i] * (1.0 - sigmas[i]))
-                gconv_ref[pl.ds(HALO, length), pl.ds(i * cols + at, width)] = grads[i] * slope
-            rate_grads = rate_grads + jnp.where(
-                lane == RATE_AT + h, drate * rate * (1.0 - rate), 0.0
-            )
-        for i in range(3 * heads):
-            at = i * width
+            at = kind * cols + h * width
             total = None
             spill = None
             for j in range(CONV):
@@ -1027,22 +1137,117 @@
             pre_ref[here, at : at + width] = total.astype(bf16)
             halo_out[0, s, :, at : at + width] = total[length - HALO :, :]
             halo_out[1, s, :, at : at + width] = spill
+
+    def early(s):
+        for h in range(heads):
+            pair = s * heads + h
+            at = h * width
+            convs = [convolved(ext_ref, taps, s, length, i * cols + at, width) for i in range(3)]
+            sigmas = [jax.nn.sigmoid(a) for a in convs]
+            slopes = [b * (1.0 + a * (1.0 - b)) for a, b in zip(convs, sigmas)]
+            acts = [a * b for a, b in zip(convs, sigmas)]
+            scales = [lax.rsqrt(jnp.sum(a * a, axis=-1, keepdims=True) + EPS) for a in acts[:2]]
+            query, key = [a * b for a, b in zip(acts, scales)]
+            start, dmix = start_ref[pair], dmix_ref[pair]
+            fresh = wval_ref[pair] - mm(wkey_ref[pair], start)
+            scores = jnp.where(row_at >= col_at, finer(query, key, ((1,), (1,))), 0.0)
+            dscores = jnp.where(row_at >= col_at, finer(dmix, fresh, ((1,), (1,))), 0.0)
+            dquery = mt(dmix, start) + mm(dscores, key)
+            keys_ref[pair] = key
+            slopes_ref[pair] = slopes[1] * scales[1]
+            values_ref[pair] = acts[2]
+            vslopes_ref[pair] = slopes[2]
+            dfresh_ref[pair] = tm(scores, dmix)
+            dkeys_ref[pair] = tm(dscores, query)
+            fresh_ref[pair] = fresh.astype(bf16)
+            along = jnp.sum(query * dquery, axis=-1, keepdims=True)
+            gconv_ref[pl.ds(HALO, length), pl.ds(at, width)] = (
+                slopes[0] * scales[0] * (dquery - query * along)
+            )
+        unconvolve(s, 0)
+
+    def late(s):
+        here = part_of(s, length)
+        rate_block = rates_ref[here, :]
+        rate_grads = jnp.zeros((length, LANES), f32)
+        lane = lax.broadcasted_iota(jnp.int32, (length, LANES), 1)
+        for h in range(heads):
+            pair = s * heads + h
+            at = h * width
+            rate = column(rate_block, RATE_AT + h)
+            start, after, key, fresh = start_ref[pair], after_ref[pair], keys_ref[pair], fresh_ref[pair]
+            dfresh = dfresh_ref[pair] + mm(key, after)
+            dvalue = tm(inv_ref[pair], dfresh)
+            dkey_in = -mt(dvalue, start)
+            dstrict = jnp.where(row_at > col_at, -mt(dvalue, fresh), 0.0)
+            dprod = rate * dstrict
+            dkey = (
+                dkeys_ref[pair] + mt(fresh, after) + rate * dkey_in + mm(dprod, key) + tm(dprod, key)
+            )
+            drate = jnp.sum(
+                dstrict * mt(key, key) + dvalue * values_ref[pair] + dkey_in * key,
+                axis=-1,
+                keepdims=True,
+            )
+            along = jnp.sum(key * dkey, axis=-1, keepdims=True)
+            gconv_ref[pl.ds(HALO, length), pl.ds(cols + at, width)] = slopes_ref[pair] * (
+                dkey - key * along
+            )
+            gconv_ref[pl.ds(HALO, length), pl.ds(2 * cols + at, width)] = (
+                rate * dvalue * vslopes_ref[pair]
+            )
+            rate_grads = rate_grads + jnp.where(
+                lane == RATE_AT + h, drate * rate * (1.0 - rate), 0.0
+            )
+        unconvolve(s, 1)
+        unconvolve(s, 2)
         pre_ref[here, 3 * cols :] = rate_grads.astype(bf16)
 
-        @pl.when(s == 1)
+    ends = c == ctx_size - 1
+    starts = c == 0
+    inside = (c > 0) & (c < ctx_size - 1)
+    begins = (ctx_size - 1 - c) // (ctx_size - 1)
+
+    final = c // (ctx_size - 1)
+
+    @pl.loop(0, 3 * seqs)
+    def _(k):
+        part = k // seqs
+        s = lax.rem(k, seqs)
+        odd = lax.rem(k, 2) == seqs % 2
+        later = (1 - begins) * s + begins * lax.rem((k + seqs) // 2, seqs)
+
+        @pl.when(k == 2 + 3 * final)
+        def _():
+            cube.middle()
+
+        @pl.when(k == 4 + 4 * final)
         def _():
             cube.finish(total_ref)
+            loads["resid"].wait()
             inner = tail.total().astype(bf16)
             right = stacked([wide_ref[core, 7] for core in range(2)])
-            final = resid_ref[...] + total_ref[...] + SCALE * mm(inner, right)
-            block_ref[mine, :] = (kept(lens_ref, t, c, length) * final).astype(bf16)
+            rows = resid_ref[...] + total_ref[...] + SCALE * mm(inner, right)
+            out_ref[mine, :] = (kept(lens_ref, t, c, length) * rows).astype(bf16)
             down_inner_ref[mine, :] = inner
             cube.spread()
             tail.start(1)
 
-        @pl.when(s == 2)
+        @pl.when(k == 6 + 4 * final)
         def _():
             cube.relay()
+
+        @pl.when((ends & (part == 1)) | ((starts | inside) & (part == 0)))
+        def _():
+            early(s)
+
+        @pl.when((ends & (part == 0)) | (inside & (part == 1)) | (starts & (part > 0) & odd))
+        def _():
+            link(later)
+
+        @pl.when(((ends | inside) & (part == 2)) | (starts & (part > 0) & jnp.logical_not(odd)))
+        def _():
+            late(later)
 
     halo_in[1] = halo_out[1].astype(bf16)
     halo = remote(halo_in.at[1], halo_in.at[0], halo_send, halo_recv, {"ctx": c - 1})
@@ -1072,8 +1277,35 @@
                 chain_out.at[s], after_ref.at[pl.ds(0, heads)], chain_send.at[s], chain_recv.at[s],
                 {"ctx": c - 1},
             ).wait_send()
-    out_right_ref[...] = SCALE * tm(out_inner_ref[...], low_ref[...])
-    feed_left_ref[...] = tm(feed_grad_ref[...], n2_ref[...])
+
+    for name in ("w", "back", "into"):
+        loads[name].wait()
+    cube.done()
+    block_store = pltpu.make_async_copy(out_ref, block_hbm, store_sem.at[0])
+    block_store.start()
+    tail2_src[...] = (SCALE * mt(pre_ref[...], back_ref[...])).astype(bf16)
+    tail2.start(0)
+
+    def project(half, chunk):
+        rows = cube2.columns(half, chunk)
+        part = mm(pre_ref[:, 3 * cols :], into_ref[:, rows])
+        for i in range(3):
+            part = part + mt(pre_ref[:, i * cols : (i + 1) * cols], w_ref[i, rows, :])
+        src[:, rows] = part.astype(bf16)
+        cube2.start(half, chunk)
+
+    cube2.each(project)
+    inner = tail2.total().astype(bf16)
+    inner_grad_ref[mine, :] = inner
+    tail2.start(1)
+    loads["n2"].wait()
+    feed_left = tm(feed_grad_ref[...], normed_ref[...])
+    fetch("n1", n1_hbm, normed_ref)
+    pack[:, :, used:] = jnp.zeros((2, 8, pack.shape[2] - used), bf16)
+    loads["heads"].wait()
+    out_left = tm(out_grad, heads_ref[...])
+    out_right = SCALE * tm(out_inner_ref[...], low_ref[...])
+    right = SCALE * tm(inner_ref[...], pre_ref[...])
     tail.wait(1)
     masked = jnp.concatenate(
         [
@@ -1082,143 +1314,91 @@
         ],
         axis=0,
     )
-    down_right_ref[...] = SCALE * tm(masked, grad_ref[...])
-    cube.done()
-    tail.done()
-
-
-def first_kernel(
-    sizes,
-    pre_ref,
-    w_ref,
-    back_ref,
-    into_ref,
-    x_ref,
-    gain_ref,
-    gresid_ref,
-    n1_ref,
-    inner_ref,
-    grad_ref,
-    left_ref,
-    right_ref,
-    inner_grad_ref,
-    *scratch,
-):
-    (tp_size,) = sizes
-    t = lax.axis_index("tp")
-    block = x_ref.shape[0] // tp_size
-    half_model = x_ref.shape[1] // 2
-    cols = w_ref.shape[2]
-    greet(pltpu.get_barrier_semaphore(), tp_peers(t, tp_size))
-    src, first, second, held, total_ref, send_sem, recv_sem = scratch[:7]
-    tail_src, tail_got, tail_send, tail_recv = scratch[7:]
-    cube = Cube(t, src, grad_ref, first, second, held, send_sem, recv_sem, CHUNKS)
-    tail = Tail(t, tail_src, inner_grad_ref, tail_got, tail_send, tail_recv, tp_size)
-    tail_src[...] = (SCALE * mt(pre_ref[...], back_ref[...])).astype(bf16)
-    tail.start(0)
-
-    def project(half, chunk):
-        rows = cube.columns(half, chunk)
-        part = mm(pre_ref[:, 3 * cols :], into_ref[:, rows])
-        for i in range(3):
-            part = part + mt(pre_ref[:, i * cols : (i + 1) * cols], w_ref[i, rows, :])
-        src[:, rows] = part.astype(bf16)
-        cube.start(half, chunk)
-
-    cube.each(project)
-    inner = tail.total().astype(bf16)
-    here = part_of(t, block)
-    inner_grad_ref[here, :] = inner
-    tail.start(1)
-    cube.middle()
-    right_ref[...] = SCALE * tm(inner_ref[...], pre_ref[...])
-    tail.wait(1)
-    left_ref[...] = tm(inner_grad_ref[...], n1_ref[...])
-    cube.finish(total_ref)
-    grad_first = total_ref[...] + mm(inner, into_ref[...])
-    grad = gresid_ref[...] + norm_back(x_ref[here, :].astype(f32), gain_ref[...], grad_first)
-    grad_ref[here, :] = grad.astype(bf16)
-    cube.spread()
-    cube.relay()
-    cube.done()
-    tail.done()
-
-
-def share_kernel(sizes, strips, *refs):
-    ctx_size, wide = sizes
-    count = len(refs) - 10
-    ins, outs, (pack, mate_in, mine, recv, summed, send_sem, recv_sem, part_send, part_recv) = (
-        refs[:count],
-        refs[count : count + 1],
-        refs[count + 1 :],
-    )
-    f = lax.axis_index("fsdp")
-    c = lax.axis_index("ctx")
-    mate = {"fsdp": 1 - f}
-    others = [({"ctx": lax.rem(c + 1 + i, ctx_size)}, None) for i in range(ctx_size - 1)]
-    greet(pltpu.get_barrier_semaphore(), [(mate, None)] + others)
-    part = wide // ctx_size
-    used = sum(strip[4] for strip in strips)
+    loads["grad"].wait()
+    down_right = SCALE * tm(masked, grad_ref[...])
     for core in range(2):
-        at = 0
-        for index, row, step, col, width in strips:
-            rows = row + core * step
-            pack[core, :, at : at + width] = ins[index][rows : rows + 8, col : col + width].astype(bf16)
-            at += width
-        pack[core, :, used:] = jnp.zeros((8, wide - used), bf16)
-    swap = remote(pack.at[1 - f], mate_in, send_sem, recv_sem, mate)
+        at = core * 8
+        put("ol", core, out_left[at : at + 8])
+        put("or", core, out_right[at : at + 8])
+        put("dr", core, down_right[at : at + 8])
+        put("dl", core, down_left_ref[at : at + 8, :])
+        at = core * 16
+        put("gl", core, feed_left[at : at + 8])
+        put("ul", core, feed_left[at + 8 : at + 16])
+        put("gr", core, gate_right_ref[at : at + 8, :])
+        put("ur", core, up_right_ref[at + 8 : at + 16, :])
+        for kind, name in enumerate(("qr", "kr", "vr", "rr")):
+            at = core * 32 + kind * 8
+            put(name, core, right[at : at + 8, kind * cols : kind * cols + plan[name][1]])
+    block_store.wait()
+    cube2.middle()
+    loads["n1"].wait()
+    tail2.wait(1)
+    left = tm(inner_grad_ref[...], normed_ref[...])
+    for core in range(2):
+        for kind, name in enumerate(("ql", "kl", "vl", "rl")):
+            at = core * 32 + kind * 8
+            put(name, core, left[at : at + 8])
+    swap = remote(pack.at[1 - f], mate_in, swap_send, swap_recv, mate)
     swap.start()
-    swap.wait()
+    cube2.finish(total_ref)
+    swap.wait_recv()
     both = (pack[f].astype(f32) + mate_in[...].astype(f32)).astype(bf16)
+    piece = both.shape[1] // ctx_size
     for j in range(ctx_size):
-        mine[j] = both[:, j * part : (j + 1) * part]
+        mine_ref[j] = both[:, j * piece : (j + 1) * piece]
     sends = []
+    spreads = []
     for i in range(ctx_size - 1):
-        j = lax.rem(c + 1 + i, ctx_size)
+        peer = {"ctx": lax.rem(c + 1 + i, ctx_size)}
+        back = ctx_size - 2 - i
         sends.append(
             remote(
-                mine.at[j],
-                recv.at[ctx_size - 2 - i],
+                mine_ref.at[lax.rem(c + 1 + i, ctx_size)],
+                got.at[back],
                 part_send.at[0, i],
-                part_recv.at[0, ctx_size - 2 - i],
-                {"ctx": j},
+                part_recv.at[0, back],
+                peer,
             )
+        )
+        spreads.append(
+            remote(summed.at[c], summed.at[c], part_send.at[1, i], part_recv.at[1, back], peer)
         )
     for copy in sends:
         copy.start()
+    loads["x"].wait()
+    loads["gresid"].wait()
+    grad_first = total_ref[...] + mm(inner, into_ref[...])
+    grad = gresid_ref[...] + norm_back(x_ref[...].astype(f32), gain_ref[...], grad_first)
+    out_ref[mine, :] = grad.astype(bf16)
+    cube2.spread()
     for copy in sends:
         copy.wait_recv()
-    total = mine[c].astype(f32)
+    total = mine_ref[c].astype(f32)
     for i in range(ctx_size - 1):
-        total = total + recv[i].astype(f32)
+        total = total + got[i].astype(f32)
     summed[c] = total.astype(bf16)
-    spreads = []
-    for i in range(ctx_size - 1):
-        j = lax.rem(c + 1 + i, ctx_size)
-        spreads.append(
-            remote(
-                summed.at[c],
-                summed.at[c],
-                part_send.at[1, i],
-                part_recv.at[1, ctx_size - 2 - i],
-                {"ctx": j},
-            )
-        )
     for copy in spreads:
         copy.start()
+    cube2.relay()
     for copy in spreads:
         copy.wait_recv()
     for j in range(ctx_size):
-        outs[0][:, j * part : (j + 1) * part] = summed[j].astype(f32)
+        packed_ref[:, j * piece : (j + 1) * piece] = summed[j].astype(f32)
+    cube2.done()
+    grad_store = pltpu.make_async_copy(out_ref, input_grad_hbm, store_sem.at[1])
+    grad_store.start()
+    swap.wait_send()
     for copy in sends + spreads:
         copy.wait_send()
+    tail.done()
+    tail2.done()
+    grad_store.wait()
 
 
 def deal_kernel(strips, packed_ref, *outs):
-    at = 0
-    for out, strip in zip(outs, strips):
-        out[...] = packed_ref[:, at : at + strip[4]]
-        at += strip[4]
+    for out, (at, wide) in zip(outs, strips):
+        out[...] = packed_ref[:, at : at + wide]
 
 
 def local(ctx_size, tp_size, *arguments):
@@ -1296,13 +1476,37 @@
     tall = (pairs, length, width)
     block = rows // tp_size
     smem = pl.BlockSpec(memory_space=pltpu.SMEM)
+    mixer_sizes = (seqs, length, heads, width, ctx_size, tp_size)
+    kept_shapes = (
+        shape((rows, model), bf16),
+        shape((2, 8, 8, model), bf16),
+        shape((2, 8, slim_wide), bf16),
+        shape((LANES, model), bf16),
+        shape((LANES, 3 * cols + LANES), bf16),
+        shape((seqs, ext, 3 * cols), f32),
+        shape((rows, LANES), bf16),
+        shape((rows, LANES), f32),
+        shape((pairs, length, length), bf16),
+        shape(tall, bf16),
+        shape(tall, f32),
+        shape(tall, bf16),
+        shape(tall, f32),
+        shape(square, bf16),
+        shape((rows, cols), bf16),
+        shape(square, bf16),
+        shape((rows, units), f32),
+        shape((rows, LANES), bf16),
+    )
     (
-        n1,
-        wqkv,
+        second,
+        out_inner,
+        residual,
         wo,
         wg,
         wu,
         wd,
+        wqkv,
+        n1,
         wide_all,
         slim_all,
         into,
@@ -1316,53 +1520,59 @@
         reach,
         local_out,
         step_map,
-        end_state,
+        heads_low,
+        start,
+        active,
+        down_grad,
     ) = pl.pallas_call(
-        functools.partial(mixer_kernel, (seqs, length, heads, width, ctx_size)),
+        functools.partial(mixer_kernel, mixer_sizes),
         out_shape=(
             shape((rows, model), bf16),
-            shape((3, model, cols), bf16),
+            shape((rows, LANES), bf16),
+            shape((block, model), f32),
             shape(output_weight.shape, bf16),
             shape(gate_weight.shape, bf16),
             shape(up_weight.shape, bf16),
             shape(down_weight.shape, bf16),
-            shape((2, 8, 8, model), bf16),
-            shape((2, 8, slim_wide), bf16),
-            shape((LANES, model), bf16),
-            shape((LANES, 3 * cols + LANES), bf16),
-            shape((seqs, ext, 3 * cols), f32),
-            shape((rows, LANES), bf16),
-            shape((rows, LANES), f32),
-            shape((pairs, length, length), bf16),
-            shape(tall, bf16),
-            shape(tall, f32),
-            shape(tall, bf16),
-            shape(tall, f32),
-            shape(square, bf16),
-            shape(square, f32),
-        ),
-        in_specs=[smem] + [VMEM] * 5 + [ANY] * 24,
-        out_specs=(VMEM,) + (ANY,) * 5 + (VMEM,) * 14,
-        scratch_shapes=[
+            shape((3, model, cols), bf16),
+        )
+        + kept_shapes,
+        in_specs=[smem] + [VMEM] * 7 + [ANY] * 25,
+        out_specs=(VMEM,) * 3 + (ANY,) * (5 + len(kept_shapes)),
+        scratch_shapes=[pltpu.VMEM(item.shape, item.dtype) for item in kept_shapes]
+        + [
+            pltpu.VMEM(square, f32),
             pltpu.VMEM((3, model, cols), bf16),
             pltpu.VMEM((8, model), bf16),
             pltpu.VMEM((seqs, HALO, 3 * cols), bf16),
             pltpu.VMEM((seqs, HALO, 3 * cols), bf16),
             pltpu.VMEM((LANES, 3 * cols + LANES), f32),
             pltpu.VMEM((LANES, model), f32),
+            pltpu.VMEM((seqs, heads, width, width), bf16),
+            pltpu.VMEM((2,) + output_weight.shape, bf16),
+            pltpu.VMEM((2,) + down_weight.shape, bf16),
+            pltpu.VMEM((rows, model), bf16),
             DMA((24,)),
             DMA((24,)),
             DMA((20,)),
-            DMA((3,)),
+            DMA((19,)),
             DMA,
             DMA,
-        ],
+            DMA((4,)),
+            DMA,
+            DMA((seqs,)),
+            DMA((seqs,)),
+        ]
+        + cube_scratch(rows, model)
+        + tail_scratch(rows, tp_size),
         compiler_params=params(0),
         name="mixer",
     )(
         seq_lengths,
         x,
         gain1,
+        gain2,
+        gain3,
         query_conv,
         key_conv,
         value_conv,
@@ -1376,49 +1586,7 @@
         gate_weight,
         up_weight,
         down_weight,
-    )
-    mixer_sizes = (seqs, length, heads, width, ctx_size, tp_size)
-    second, out_inner, residual, heads_low, start, active, down_grad = pl.pallas_call(
-        functools.partial(attend_kernel, mixer_sizes),
-        out_shape=(
-            shape((rows, model), bf16),
-            shape((rows, LANES), bf16),
-            shape((block, model), f32),
-            shape((rows, cols), bf16),
-            shape(square, bf16),
-            shape((rows, units), f32),
-            shape((rows, LANES), bf16),
-        ),
-        in_specs=[smem] + [VMEM] * 10 + [ANY] * 4,
-        out_specs=(VMEM,) * 7,
-        scratch_shapes=[
-            pltpu.VMEM((seqs, heads, width, width), bf16),
-            pltpu.VMEM((2,) + output_weight.shape, bf16),
-            pltpu.VMEM((2,) + down_weight.shape, bf16),
-            DMA((2, 2)),
-            DMA((seqs,)),
-            DMA((seqs,)),
-        ]
-        + cube_scratch(rows, model)
-        + tail_scratch(rows, tp_size),
-        compiler_params=params(1),
-        name="attend",
-    )(
-        seq_lengths,
-        x,
-        gain2,
-        gain3,
-        step_map,
-        end_state,
-        reach,
-        local_out,
-        wide_all,
-        slim_all,
         grad_rows,
-        output_weight,
-        wo,
-        down_weight,
-        wd,
     )
     (
         resid_low,
@@ -1437,9 +1605,9 @@
             shape((block, model), f32),
             shape((rows, model), bf16),
             shape((rows, LANES), bf16),
-            shape((LANES, units), f32),
-            shape((LANES, units), f32),
-            shape((LANES, units), f32),
+            shape((32, units), f32),
+            shape((32, units), f32),
+            shape((32, units), f32),
         ),
         in_specs=[smem] + [VMEM] * 7 + [ANY] * 7,
         out_specs=(VMEM,) * 8,
@@ -1478,21 +1646,42 @@
         down_weight,
         wd,
     )
-    grad_pre, block_out, out_left, out_right, down_right_grad, feed_left = pl.pallas_call(
+    plan, used = strip_plan(cols, model, units)
+    grain = LANES * ctx_size
+    total_wide = -(-used // grain) * grain
+    piece = total_wide // ctx_size
+    block_out, input_grad, packed = pl.pallas_call(
         functools.partial(back_kernel, mixer_sizes),
         out_shape=(
-            shape((rows, 3 * cols + LANES), bf16),
             shape((rows, model), bf16),
-            shape((LANES, cols), f32),
-            shape((LANES, model), f32),
-            shape((LANES, model), f32),
-            shape((LANES, model), f32),
+            shape((rows, model), bf16),
+            shape((8, total_wide), f32),
         ),
-        in_specs=[smem] + [VMEM] * 16 + [ANY] * 2 + [VMEM] * 8,
-        out_specs=(VMEM,) * 6,
+        in_specs=[smem] + [VMEM] * 15 + [ANY] * 22,
+        out_specs=(ANY, ANY, VMEM),
         scratch_shapes=[
+            pltpu.VMEM(square, bf16),
+            pltpu.VMEM(square, bf16),
+            pltpu.VMEM(tall, bf16),
+            pltpu.VMEM(tall, f32),
+            pltpu.VMEM((pairs, length, length), bf16),
+            pltpu.VMEM(tall, bf16),
+            pltpu.VMEM(tall, f32),
+            pltpu.VMEM((seqs, ext, 3 * cols), f32),
+            pltpu.VMEM((rows, LANES), f32),
+            pltpu.VMEM((rows, cols), bf16),
+            pltpu.VMEM((rows, model), bf16),
+            pltpu.VMEM((block, model), f32),
+            pltpu.VMEM((rows, model), bf16),
+            pltpu.VMEM((rows, model), bf16),
+            pltpu.VMEM((block, model), bf16),
+            pltpu.VMEM((block, model), f32),
+            pltpu.VMEM((3, model, cols), bf16),
+            pltpu.VMEM((LANES, 3 * cols + LANES), bf16),
+            pltpu.VMEM((LANES, model), bf16),
             pltpu.VMEM((2,) + output_weight.shape, bf16),
-            pltpu.VMEM((rows, cols), f32),
+            pltpu.VMEM((rows, model), bf16),
+            pltpu.VMEM((rows, 3 * cols + LANES), bf16),
             pltpu.VMEM(tall, f32),
             pltpu.VMEM(square, bf16),
             pltpu.VMEM((seqs, heads, width, width), bf16),
@@ -1500,20 +1689,53 @@
             pltpu.VMEM((2, seqs, HALO, 3 * cols), f32),
             pltpu.VMEM((2, seqs, HALO, 3 * cols), bf16),
             pltpu.VMEM((rows, LANES), bf16),
-            DMA((1, 2)),
+            pltpu.VMEM(tall, f32),
+            pltpu.VMEM(tall, f32),
+            pltpu.VMEM(tall, f32),
+            pltpu.VMEM(tall, f32),
+            pltpu.VMEM(tall, f32),
+            pltpu.VMEM(tall, f32),
+            pltpu.VMEM(tall, bf16),
+            pltpu.VMEM((rows, LANES), bf16),
+            pltpu.VMEM((rows, LANES), bf16),
+            pltpu.VMEM((2, 8, total_wide), bf16),
+            pltpu.VMEM((8, total_wide), bf16),
+            pltpu.VMEM((ctx_size, 8, piece), bf16),
+            pltpu.VMEM((ctx_size - 1, 8, piece), bf16),
+            pltpu.VMEM((ctx_size, 8, piece), bf16),
+            DMA((BACK_LOADS,)),
+            DMA((2,)),
             DMA((seqs,)),
             DMA((seqs,)),
             DMA,
             DMA,
+            DMA,
+            DMA,
+            DMA((2, ctx_size - 1)),
+            DMA((2, ctx_size - 1)),
         ]
         + cube_scratch(rows, model)[1:]
-        + tail_scratch(rows, tp_size)[1:],
+        + [DMA((4, 2, CHUNKS, 2)), DMA((4, 2, CHUNKS, 2))]
+        + tail_scratch(rows, tp_size)[1:] * 2,
         compiler_params=params(3),
         name="back",
     )(
         seq_lengths,
         resid_low,
         gain3,
+        gain1,
+        query_conv,
+        key_conv,
+        value_conv,
+        wide_all,
+        slim_all,
+        down_tail,
+        feed_grad,
+        out_inner,
+        inner,
+        gate_right_grad,
+        up_right_grad,
+        down_left_grad,
         start,
         step_map,
         reach,
@@ -1522,90 +1744,26 @@
         wkey,
         wval,
         pre_ext,
-        query_conv,
-        key_conv,
-        value_conv,
         rates,
-        wide_all,
-        slim_all,
-        output_weight,
-        wo,
         heads_low,
-        out_inner,
         down_part,
-        down_tail,
         residual,
         grad_rows,
         second,
-        feed_grad,
-    )
-    input_grad, mixer_left, mixer_right = pl.pallas_call(
-        functools.partial(first_kernel, (tp_size,)),
-        out_shape=(
-            shape((rows, model), bf16),
-            shape((LANES, model), f32),
-            shape((LANES, 3 * cols + LANES), f32),
-        ),
-        in_specs=[VMEM] * 9,
-        out_specs=(VMEM,) * 3,
-        scratch_shapes=[pltpu.VMEM((rows, LANES), bf16)]
-        + cube_scratch(rows, model)
-        + tail_scratch(rows, tp_size),
-        compiler_params=params(4),
-        name="first",
-    )(grad_pre, wqkv, back, into, x, gain1, grad_residual, n1, inner)
-    sources = [
-        mixer_left,
-        mixer_right,
-        feed_left,
-        gate_right_grad,
-        up_right_grad,
-        out_left,
-        out_right,
-        down_left_grad,
-        down_right_grad,
-    ]
-    strips = []
-    for kind in range(4):
-        strips.append((0, kind * 8, 32, 0, model))
-        strips.append((1, kind * 8, 32, kind * cols, cols if kind < 3 else LANES))
-    strips += [
-        (5, 0, 8, 0, cols),
-        (6, 0, 8, 0, model),
-        (2, 0, 16, 0, model),
-        (3, 0, 16, 0, units),
-        (2, 8, 16, 0, model),
-        (4, 8, 16, 0, units),
-        (7, 0, 8, 0, units),
-        (8, 0, 8, 0, model),
-    ]
-    strips = tuple(strips)
-    used = sum(item[4] for item in strips)
-    grain = LANES * ctx_size
-    total_wide = -(-used // grain) * grain
-    packed = pl.pallas_call(
-        functools.partial(share_kernel, (ctx_size, total_wide), strips),
-        out_shape=(shape((8, total_wide), f32),),
-        in_specs=[VMEM] * len(sources),
-        out_specs=(VMEM,),
-        scratch_shapes=[
-            pltpu.VMEM((2, 8, total_wide), bf16),
-            pltpu.VMEM((8, total_wide), bf16),
-            pltpu.VMEM((ctx_size, 8, total_wide // ctx_size), bf16),
-            pltpu.VMEM((ctx_size - 1, 8, total_wide // ctx_size), bf16),
-            pltpu.VMEM((ctx_size, 8, total_wide // ctx_size), bf16),
-            DMA,
-            DMA,
-            DMA((2, ctx_size - 1)),
-            DMA((2, ctx_size - 1)),
-        ],
-        compiler_params=params(5),
-        name="share",
-    )(*sources)[0]
+        n1,
+        x,
+        grad_residual,
+        wqkv,
+        back,
+        into,
+        output_weight,
+        wo,
+    )
+    strips = tuple(plan.values())
     shares = list(
         pl.pallas_call(
             functools.partial(deal_kernel, strips),
-            out_shape=tuple(shape((8, item[4]), f32) for item in strips),
+            out_shape=tuple(shape((8, wide), f32) for _, wide in strips),
             in_specs=[VMEM],
             out_specs=(VMEM,) * len(strips),
             name="deal",

time: 318 us -> 259 us (0.81)
  Pallas kernels: 309 us -> 249 us
    pallas_call x4 -> x1, Pallas kernels: 165 us -> 81.4 us  [local(): pl.pallas_call(functools.partial(mixer_kernel, mixer_sizes), out_shape=(s...]
    pallas_call x1, Pallas kernels: 81 us -> 104 us  [local(): pl.pallas_call(functools.partial(back_kernel, mixer_sizes), out_shape=(sh...]
where the time goes in v2:
time: 259 us; the launch traced here: 258 us
  Pallas kernels  249 us (96%)
  local copies, waits for them, and re-layouts  8.77 us (3%)
    pallas_call x1, Pallas kernels, local(): pl.pallas_call(functools.partial(back_kernel, mixer_sizes), out_shape=(sh...  104 us
    pallas_call x1, Pallas kernels, local(): pl.pallas_call(functools.partial(mixer_kernel, mixer_sizes), out_shape=(s...  81.4 us
    pallas_call x1, Pallas kernels, local(): pl.pallas_call(functools.partial(feed_kernel, (seqs, length, cols, ctx_si...  61 us
    unnamed x6, local copies, waits for them, and re-layouts  6.05 us

profile of v2, /device:TPU:0, one launch (start us, length us, event | category | flops | bytes accessed | tf_op | source)
XLA Modules:
  0.0 258.3 jit_solution(8245183789629948574)
XLA Ops:
  0.7 0.8 copy.51
  1.4 0.7 pad.9.slim3
  2.1 1.3 pad.8.wr_ref
  3.4 81.4 %mixer.1 = (bf16[512,2048]{1,0:T(8,128)(2,1)}, bf16[512,128]{1,0:T(8,128)(2,1)}, f32[128,2048]{1,0:T(8,128)}, bf16[512,1024]{1,0:T(8,128)(2,1)}, bf16[1024,1408]...) custom-call(s32[4]{0:T(128)} %lens_ref.5, ...), custom_call_target="tpu_custom_call" | custom-call | tf_op jit(solution)/shard_map/mixer/pallas_call | solution.py:1527
  84.8 61.0 %feed.1 = (bf16[512,2048]{1,0:T(8,128)(2,1)}, bf16[512,128]{1,0:T(8,128)(2,1)}, f32[128,2048]{1,0:T(8,128)}, bf16[512,2048]{1,0:T(8,128)(2,1)}, bf16[512,128]{1,...) custom-call(s32[4]{0:T(128)} %lens_ref.5, ...), custom_call_target="tpu_custom_call" | custom-call | tf_op jit(solution)/shard_map/feed/pallas_call | solution.py:1600
  145.8 104.4 %back.1 = (bf16[512,2048]{1,0:T(8,128)(2,1)}, bf16[512,2048]{1,0:T(8,128)(2,1)}, f32[8,23040]{1,0:T(8,128)}) custom-call(s32[4]{0:T(128)} %lens_ref.5, bf16[512,2048]{1,0:T(8,128)(2,1)} %get-tuple-element.80.low_ref, f32[1,128]{1,0:T(1,128)} %bitcast.45, f32[1,2048]{1,0:T(1,128)} %bitcast.40, f32[4,512]{1,0:T(4,128)} %qtaps_ref.3, f32[4,512]{1,0:T(4,128)} %ktaps_ref.3, ...), custom_call_target="tpu_custom_call" | custom-call | tf_op jit(solution)/shard_map/back/pallas_call | solution.py:1653
  250.3 2.0 deal.1
  252.3 0.8 slice.3
  253.0 0.7 copy.52
  253.7 0.0 copy-start
  253.7 3.3 %copy.55 = bf16[4,128,2048]{2,1,0:T(8,128)(2,1)} copy(bf16[4,128,2048]{2,1,0:T(8,128)(2,1)} %bitcast.30) | data formatting | bytes 4194304
  257.0 0.0 copy-done
  257.0 1.3 copy.56
Async XLA Ops:
  253.7 3.3 %copy-start = (bf16[512,2048]{1,0:T(8,128)(2,1)S(1)}, bf16[512,2048]{1,0:T(8,128)(2,1)}, u32[]{:S(2)}) copy-start(bf16[512,2048]{1,0:T(8,128)(2,1)} %get-tuple-element.106) | copy-start | bytes 6291460

commit v3 on v2

--- a/solution.py
+++ b/solution.py
@@ -201,28 +201,56 @@
         self.copy(0, half, chunk, 0).start()
         self.copy(0, half, chunk, 1).start()
 
+    def block_at(self, i):
+        flip_x, flip_y = (3 - i) // 2, lax.rem(i + 1, 2)
+        y = self.y + flip_y * (1 - 2 * self.y)
+        return y * 2 + self.x + flip_x * (1 - 2 * self.x)
+
+    def send_block(self, i):
+        def go(half, j):
+            for chunk in range(self.chunks):
+                self.copy(0, half, chunk, j).start()
+
+        @pl.when(i == 0)
+        def _():
+            go(0, 1 - self.y)
+            go(1, 1 - self.x)
+
+        @pl.when(i == 1)
+        def _():
+            go(0, self.y)
+
+        @pl.when(i == 2)
+        def _():
+            go(1, self.x)
+
+    def pass_on(self, half, chunk):
+        wide = self.columns(half, chunk)
+        slim = part_of(chunk, self.width)
+        across = self.above * (1 - half) + self.beside * half
+        other = (1 - half) * (1 - self.y) + half * (1 - self.x)
+        self.copy(0, half, chunk, other).wait_recv()
+        self.held[half, :, slim] = (
+            self.src[part_of(across, self.block), wide].astype(f32)
+            + self.first[half, other, :, slim].astype(f32)
+        ).astype(bf16)
+        self.copy(1, half, chunk, 0).start()
+
     def middle(self):
-        def body(half, chunk):
-            wide = self.columns(half, chunk)
-            slim = part_of(chunk, self.width)
-            for j in range(2):
-                self.copy(0, half, chunk, j).wait_recv()
-            across = self.above * (1 - half) + self.beside * half
-            other = (1 - half) * (1 - self.y) + half * (1 - self.x)
-            self.held[half, :, slim] = (
-                self.src[part_of(across, self.block), wide].astype(f32)
-                + self.first[half, other, :, slim].astype(f32)
-            ).astype(bf16)
-            self.copy(1, half, chunk, 0).start()
-
-        self.each(body)
+        self.each(self.pass_on)
+
+    def middle_half(self, half):
+        @pl.loop(0, self.chunks)
+        def _(chunk):
+            self.pass_on(half, chunk)
 
     def finish(self, total_ref):
         def body(half, chunk):
             wide = self.columns(half, chunk)
             slim = part_of(chunk, self.width)
+            mine = (1 - half) * self.y + half * self.x
+            self.copy(0, half, chunk, mine).wait_recv()
             self.copy(1, half, chunk, 0).wait_recv()
-            mine = (1 - half) * self.y + half * self.x
             total_ref[:, wide] = (
                 self.src[part_of(self.t, self.block), wide].astype(f32)
                 + self.first[half, mine, :, slim].astype(f32)
@@ -284,6 +312,17 @@
     def start(self, stage):
         for copy in self.copies(stage):
             copy.start()
+
+    def send_block(self, g):
+        i = lax.rem(g - self.t - 1 + self.size, self.size)
+        back = self.size - 2 - i
+        remote(
+            self.src.at[part_of(g, self.block)],
+            self.got.at[back],
+            self.send_sem.at[0, i],
+            self.recv_sem.at[0, back],
+            {"tp": g},
+        ).start()
 
     def wait(self, stage):
         for copy in self.copies(stage):
@@ -506,7 +545,7 @@
     ]
     near = [pltpu.make_async_copy(src, dst, local_sem.at[i]) for i, (src, dst) in enumerate(moves)]
     local_count = len(moves)
-    moves += [(wo_own, wo_other), (wg_own, wg_other), (wu_own, wu_other), (wd_own, wd_other)]
+    moves += [(wo_own, wo_ref.at[f]), (wg_own, wg_other), (wu_own, wu_other), (wd_own, wd_other)]
     across = [
         remote(src, dst, send_sem.at[i], recv_sem.at[i], mate) for i, (src, dst) in enumerate(moves)
     ]
@@ -541,14 +580,20 @@
             back_f32[core * 32 + kind * 8 : core * 32 + kind * 8 + 8, at : at + wide] = slim_out[
                 core, :, at : at + wide
             ].astype(f32)
-    into_f32[RATE_AT : RATE_AT + 8, :] = wr_all[...].astype(f32)
+    into_f32[RATE_AT : RATE_AT + heads, :] = wr_all[...].astype(f32)
     into_ref[...] = into_f32[...].astype(bf16)
     back_ref[...] = back_f32[...].astype(bf16)
     store([(w_ref, wqkv_out), (n1_ref, n1_out), (wide_out, wide_hbm), (slim_out, slim_hbm)])
     store([(into_ref, into_out), (back_ref, back_out)])
 
+    def halo_of(s):
+        return remote(
+            halo_out.at[s], halo_in.at[s], halo_send.at[s], halo_recv.at[s], {"ctx": c + 1}
+        )
+
     @pl.loop(0, seqs)
-    def _(s):
+    def _(k):
+        s = cube.block_at(k)
         here = pl.ds(pl.multiple_of(s * length, length), length)
         block = n1_ref[here, :]
         tail = mt(block, into_ref[...])
@@ -561,25 +606,23 @@
         pre_rate = tail + SCALE * mm(inner, back_ref[:, 3 * cols :])
         rates_ref[here, :] = jax.nn.sigmoid(pre_rate) * kept(lens_ref, s, c, length)
 
-    halo = remote(halo_out, halo_in, halo_send, halo_recv, {"ctx": c + 1})
-
-    @pl.when(c < ctx_size - 1)
-    def _():
-        halo.start()
-
-    @pl.when(c > 0)
-    def _():
-        halo.wait_recv()
-        ext_ref[:, 0:HALO, :] = halo_in[...].astype(f32)
-
-    @pl.when(c == 0)
-    def _():
-        ext_ref[:, 0:HALO, :] = jnp.zeros((seqs, HALO, 3 * cols), f32)
+        @pl.when(c < ctx_size - 1)
+        def _():
+            halo_of(s).start()
 
     taps = jnp.concatenate([qtaps_ref[...], ktaps_ref[...], vtaps_ref[...]], axis=1)
     row_at, col_at = grid_of(length)
 
     def solve(s):
+        @pl.when(c > 0)
+        def _():
+            halo_of(s).wait_recv()
+            ext_ref[s, 0:HALO, :] = halo_in[s].astype(f32)
+
+        @pl.when(c == 0)
+        def _():
+            ext_ref[s, 0:HALO, :] = jnp.zeros((HALO, 3 * cols), f32)
+
         here = pl.ds(pl.multiple_of(s * length, length), length)
         rate_block = rates_ref[here, :]
         queries, keys, values, rates, stricts = [], [], [], [], []
@@ -617,26 +660,31 @@
 
     gain = head_gain_ref[...]
 
+    def hop_of(pair):
+        return remote(
+            chain_out.at[pair],
+            start_ref.at[pair],
+            chain_send.at[pair],
+            chain_recv.at[pair],
+            {"ctx": c + 1},
+        )
+
     def link(s):
-        pairs = pl.ds(s * heads, heads)
-        hop = remote(
-            chain_out.at[s], start_ref.at[pairs], chain_send.at[s], chain_recv.at[s], {"ctx": c + 1}
-        )
-
-        @pl.when(c > 0)
-        def _():
-            hop.wait_recv()
-
-        @pl.when(c == 0)
-        def _():
-            start_ref[pairs] = jnp.zeros((heads, width, width), bf16)
-
-        @pl.when(c < ctx_size - 1)
-        def _():
-            for h in range(heads):
-                pair = s * heads + h
-                chain_out[s, h] = (mm(map_ref[pair], start_ref[pair]) + end_ref[pair]).astype(bf16)
-            hop.start()
+        for h in range(heads):
+            pair = s * heads + h
+
+            @pl.when(c > 0)
+            def _(pair=pair):
+                hop_of(pair).wait_recv()
+
+            @pl.when(c == 0)
+            def _(pair=pair):
+                start_ref[pair] = jnp.zeros((width, width), bf16)
+
+            @pl.when(c < ctx_size - 1)
+            def _(pair=pair):
+                chain_out[pair] = (mm(map_ref[pair], start_ref[pair]) + end_ref[pair]).astype(bf16)
+                hop_of(pair).start()
 
         here = part_of(s, length)
         for h in range(heads):
@@ -644,15 +692,41 @@
             mixed = mm(reach_ref[pair], start_ref[pair]) + local_ref[pair]
             heads_ref[here, h * width : (h + 1) * width] = normed(mixed, gain).astype(bf16)
 
+    into = stacked([slim_out[core, :, left_at : left_at + cols] for core in range(2)])
+    across[local_count].wait_recv()
+    own_loads[0].wait()
+    store([(wo_ref.at[1 - f], wo_other)])
+
+    def project(i):
+        here = part_of(cube.block_at(i), length)
+        low = heads_ref[here, :]
+        for side in range(2):
+            src[here, side * half_model : (side + 1) * half_model] = mm(low, wo_ref[side]).astype(bf16)
+        tail_src[here, :] = mt(low, into).astype(bf16)
+        cube.send_block(i)
+
+        @pl.when(i < 3)
+        def _():
+            tail.send_block(cube.block_at(i))
+
+        @pl.when(i == 2)
+        def _():
+            cube.middle_half(1)
+
+        @pl.when(i == 3)
+        def _():
+            cube.middle_half(0)
+
     @pl.loop(0, seqs + ctx_size - 1)
     def _(k):
         @pl.when(k < seqs)
         def _():
-            solve(k)
+            solve(cube.block_at(k))
 
         @pl.when((k >= c) & (k < c + seqs))
         def _():
-            link(k - c)
+            link(cube.block_at(k - c))
+            project(k - c)
 
     store(
         [
@@ -669,23 +743,16 @@
             (start_ref, start_out),
         ]
     )
-    into = stacked([slim_out[core, :, left_at : left_at + cols] for core in range(2)])
-    low = heads_ref[...]
-    tail_src[...] = mt(low, into).astype(bf16)
-    tail.start(0)
-    across[local_count].wait_recv()
-    wo_load = pltpu.make_async_copy(wo_other, wo_ref.at[1 - f], load_sem.at[1])
-    wo_load.start()
-    own_loads[0].wait()
-    wo_load.wait()
-
-    def project(half, chunk):
-        src[:, cube.columns(half, chunk)] = mm(
-            heads_ref[...], wo_ref[half, :, part_of(chunk, cube.width)]
-        ).astype(bf16)
-        cube.start(half, chunk)
-
-    cube.each(project)
+    cube.finish(total_ref)
+    inner = tail.total().astype(bf16)
+    here = part_of(t, length)
+    right = stacked([wide_out[core, 6] for core in range(2)])
+    resid = x_ref[here, :].astype(f32) + total_ref[...] + SCALE * mm(inner, right)
+    resid_ref[...] = resid
+    out_inner_ref[here, :] = inner
+    n2_ref[here, :] = normed(resid, gain2_ref[...]).astype(bf16)
+    cube.spread()
+    tail.start(1)
     for copy in across[local_count + 1 :]:
         copy.wait_recv()
     wd_load = pltpu.make_async_copy(wd_other, wd_ref.at[1 - f], load_sem.at[3])
@@ -710,20 +777,9 @@
                 kept(lens_ref, s, c, length) * part[s * length : (s + 1) * length]
             )
 
+    cube.relay()
     unit_steps(units, activate)
     store([(active_ref, active_out), (down_inner_ref, down_inner_out)])
-    cube.middle()
-    cube.finish(total_ref)
-    inner = tail.total().astype(bf16)
-    here = part_of(t, length)
-    right = stacked([wide_out[core, 6] for core in range(2)])
-    resid = x_ref[here, :].astype(f32) + total_ref[...] + SCALE * mm(inner, right)
-    resid_ref[...] = resid
-    out_inner_ref[here, :] = inner
-    n2_ref[here, :] = normed(resid, gain2_ref[...]).astype(bf16)
-    cube.spread()
-    tail.start(1)
-    cube.relay()
     tail.wait(1)
     cube.done()
     tail.done()
@@ -734,25 +790,19 @@
 
     @pl.when(c < ctx_size - 1)
     def _():
-        halo.wait_send()
-
         @pl.loop(0, seqs)
         def _(s):
-            remote(
-                chain_out.at[s],
-                start_ref.at[pl.ds(0, heads)],
-                chain_send.at[s],
-                chain_recv.at[s],
-                {"ctx": c + 1},
-            ).wait_send()
+            halo_of(s).wait_send()
+
+        @pl.loop(0, seqs * heads)
+        def _(pair):
+            hop_of(pair).wait_send()
 
 
 def feed_kernel(
     sizes,
     lens_ref,
     n2_ref,
-    active_ref,
-    resid_ref,
     gain_ref,
     wide_ref,
     slim_ref,
@@ -764,10 +814,12 @@
     wu_other,
     wd_own,
     wd_other,
+    active_hbm,
+    resid_hbm,
     low_ref,
     inner_grad_ref,
-    gresid_ref,
-    down_ref,
+    gresid_hbm,
+    down_hbm,
     down_tail_ref,
     gate_right_ref,
     up_right_ref,
@@ -782,7 +834,13 @@
     back_gate,
     back_up,
     own_grad,
+    active_ref,
+    resid_ref,
+    gresid_ref,
+    down_ref,
     load_sem,
+    piece_sem,
+    store_sem,
     grad_sem,
     *scratch,
 ):
@@ -796,11 +854,33 @@
     f = lax.axis_index("fsdp")
     c = lax.axis_index("ctx")
     t = lax.axis_index("tp")
-    loads = slot_loads(
-        [(wg_own, wg_other, wg_ref), (wu_own, wu_other, wu_ref), (wd_own, wd_other, wd_ref)],
-        f,
-        load_sem,
-    )
+    step = 2 * LANES
+    spans = [pl.ds(at, min(step, units - at)) for at in range(0, units, step)]
+    whole = [
+        pltpu.make_async_copy(wd_own, wd_ref.at[f], load_sem.at[0]),
+        pltpu.make_async_copy(wd_other, wd_ref.at[1 - f], load_sem.at[1]),
+        pltpu.make_async_copy(resid_hbm, resid_ref, load_sem.at[2]),
+    ]
+
+    def piece_loads(at, k):
+        return [
+            pltpu.make_async_copy(source.at[:, at], target.at[:, at], piece_sem.at[k, i])
+            for i, (source, target) in enumerate(
+                (
+                    (wg_own, wg_ref.at[f]),
+                    (wg_other, wg_ref.at[1 - f]),
+                    (wu_own, wu_ref.at[f]),
+                    (wu_other, wu_ref.at[1 - f]),
+                    (active_hbm, active_ref),
+                )
+            )
+        ]
+
+    for k, at in enumerate(spans):
+        for load in piece_loads(at, k):
+            load.start()
+    for load in whole:
+        load.start()
     here = part_of(t, length)
     own_load = pltpu.make_async_copy(grad_ref.at[here], own_grad, grad_sem)
     own_load.start()
@@ -816,10 +896,9 @@
     back_gate[...] = stacked([gates[0], blank, gates[1], blank])
     back_up[...] = stacked([blank, ups[0], blank, ups[1]])
     inner_ref[...] = mt(n2_ref[...], into).astype(bf16)
-    for load in loads[:4]:
-        load.wait()
-
-    def forward(at):
+    def forward(at, k):
+        for load in piece_loads(at, k):
+            load.wait()
         pre = []
         for weight, back in ((wg_ref, back_gate), (wu_ref, back_up)):
             part = mm(n2_ref[:, :half_model], weight[0, :, at])
@@ -833,7 +912,14 @@
         dgate_ref[:, at] = (active * up * (sigma * (1.0 + gate * (1.0 - sigma)))).astype(bf16)
         dup_ref[:, at] = (active * silu).astype(bf16)
 
-    unit_steps(units, forward)
+    full = units // step
+
+    @pl.loop(0, full)
+    def _(k):
+        forward(part_of(k, step), k)
+
+    if units % step:
+        forward(spans[-1], full)
     tail_src[...] = (
         SCALE * (mt(dgate_ref[...], back_gate[...]) + mt(dup_ref[...], back_up[...]))
     ).astype(bf16)
@@ -848,7 +934,7 @@
 
     cube.each(project)
     cube.middle()
-    for load in loads[4:]:
+    for load in whole:
         load.wait()
 
     def descend(half, chunk):
@@ -857,6 +943,8 @@
         ).astype(bf16)
 
     cube.each(descend)
+    down_store = pltpu.make_async_copy(down_ref, down_hbm, store_sem.at[0])
+    down_store.start()
     cube.finish(total_ref)
     own_load.wait()
     inner = tail.total().astype(bf16)
@@ -865,6 +953,8 @@
         resid_ref[...], gain_ref[...], grad_second
     )
     gresid_ref[...] = grad
+    grad_store = pltpu.make_async_copy(gresid_ref, gresid_hbm, store_sem.at[1])
+    grad_store.start()
     low_ref[here, :] = grad.astype(bf16)
     inner_grad_ref[here, :] = inner
     cube.spread()
@@ -878,6 +968,8 @@
     tail.wait(1)
     cube.done()
     tail.done()
+    down_store.wait()
+    grad_store.wait()
 
 
 def strip_plan(cols, model, units):
@@ -1000,6 +1092,10 @@
     cube_recv,
     cube2_send,
     cube2_recv,
+    src2,
+    first2,
+    second2,
+    held2,
     tail_got,
     tail_send,
     tail_recv,
@@ -1013,6 +1109,7 @@
     half_model = model // 2
     units = gate_right_ref.shape[1]
     left_at = 3 * cols + LANES
+    pairs = seqs * heads
     plan, used = strip_plan(cols, model, units)
     f = lax.axis_index("fsdp")
     c = lax.axis_index("ctx")
@@ -1049,7 +1146,7 @@
     )
     cube = Cube(t, src, out_ref, first, second, held, cube_send, cube_recv, CHUNKS)
     tail = Tail(t, tail_src, down_inner_ref, tail_got, tail_send, tail_recv, tp_size)
-    cube2 = Cube(t, src, out_ref, first, second, held, cube2_send, cube2_recv, CHUNKS)
+    cube2 = Cube(t, src2, out_ref, first2, second2, held2, cube2_send, cube2_recv, CHUNKS)
     tail2 = Tail(t, tail2_src, inner_grad_ref, tail2_got, tail2_send, tail2_recv, tp_size)
 
     def put(name, core, rows):
@@ -1096,31 +1193,33 @@
     fetch("x", x_hbm.at[mine], x_ref)
     fetch("gresid", gresid_hbm, gresid_ref)
 
-    def hop_of(s):
-        pairs = pl.ds(s * heads, heads)
+    def hop_of(pair):
         return remote(
-            chain_out.at[s], after_ref.at[pairs], chain_send.at[s], chain_recv.at[s], {"ctx": c - 1}
+            chain_out.at[pair],
+            after_ref.at[pair],
+            chain_send.at[pair],
+            chain_recv.at[pair],
+            {"ctx": c - 1},
         )
 
     def link(s):
-        pairs = pl.ds(s * heads, heads)
-
-        @pl.when(c < ctx_size - 1)
-        def _():
-            hop_of(s).wait_recv()
-
-        @pl.when(c == ctx_size - 1)
-        def _():
-            after_ref[pairs] = jnp.zeros((heads, width, width), bf16)
-
-        @pl.when(c > 0)
-        def _():
-            for h in range(heads):
-                pair = s * heads + h
-                chain_out[s, h] = (
+        for h in range(heads):
+            pair = s * heads + h
+
+            @pl.when(c == ctx_size - 1)
+            def _(pair=pair):
+                after_ref[pair] = jnp.zeros((width, width), bf16)
+
+            @pl.when(c < ctx_size - 1)
+            def _(pair=pair):
+                hop_of(pair).wait_recv()
+
+            @pl.when(c > 0)
+            def _(pair=pair):
+                chain_out[pair] = (
                     tm(map_ref[pair], after_ref[pair]) + tm(reach_ref[pair], dmix_ref[pair])
                 ).astype(bf16)
-            hop_of(s).start()
+                hop_of(pair).start()
 
     def unconvolve(s, kind):
         here = part_of(s, length)
@@ -1139,65 +1238,104 @@
             halo_out[1, s, :, at : at + width] = spill
 
     def early(s):
-        for h in range(heads):
+        every = range(heads)
+        at = [h * width for h in every]
+        convs = [
+            [convolved(ext_ref, taps, s, length, i * cols + at[h], width) for i in range(3)]
+            for h in every
+        ]
+        starts_in = [start_ref[s * heads + h] for h in every]
+        grads_in = [dmix_ref[s * heads + h] for h in every]
+        wkeys = [wkey_ref[s * heads + h] for h in every]
+        wvals = [wval_ref[s * heads + h] for h in every]
+        fresh = [wval - mm(wkey, start) for wval, wkey, start in zip(wvals, wkeys, starts_in)]
+        sigmas = [[jax.nn.sigmoid(a) for a in row] for row in convs]
+        slopes = [
+            [b * (1.0 + a * (1.0 - b)) for a, b in zip(row, sig)] for row, sig in zip(convs, sigmas)
+        ]
+        acts = [[a * b for a, b in zip(row, sig)] for row, sig in zip(convs, sigmas)]
+        scales = [
+            [lax.rsqrt(jnp.sum(a * a, axis=-1, keepdims=True) + EPS) for a in row[:2]] for row in acts
+        ]
+        query = [acts[h][0] * scales[h][0] for h in every]
+        key = [acts[h][1] * scales[h][1] for h in every]
+        lower = row_at >= col_at
+        scores = [jnp.where(lower, finer(q, k, ((1,), (1,))), 0.0) for q, k in zip(query, key)]
+        dscores = [
+            jnp.where(lower, finer(g, v, ((1,), (1,))), 0.0) for g, v in zip(grads_in, fresh)
+        ]
+        dquery = [
+            mt(g, start) + mm(d, k) for g, start, d, k in zip(grads_in, starts_in, dscores, key)
+        ]
+        dfresh = [tm(p, g) for p, g in zip(scores, grads_in)]
+        dkeys = [tm(d, q) for d, q in zip(dscores, query)]
+        along = [jnp.sum(q * g, axis=-1, keepdims=True) for q, g in zip(query, dquery)]
+        for h in every:
             pair = s * heads + h
-            at = h * width
-            convs = [convolved(ext_ref, taps, s, length, i * cols + at, width) for i in range(3)]
-            sigmas = [jax.nn.sigmoid(a) for a in convs]
-            slopes = [b * (1.0 + a * (1.0 - b)) for a, b in zip(convs, sigmas)]
-            acts = [a * b for a, b in zip(convs, sigmas)]
-            scales = [lax.rsqrt(jnp.sum(a * a, axis=-1, keepdims=True) + EPS) for a in acts[:2]]
-            query, key = [a * b for a, b in zip(acts, scales)]
-            start, dmix = start_ref[pair], dmix_ref[pair]
-            fresh = wval_ref[pair] - mm(wkey_ref[pair], start)
-            scores = jnp.where(row_at >= col_at, finer(query, key, ((1,), (1,))), 0.0)
-            dscores = jnp.where(row_at >= col_at, finer(dmix, fresh, ((1,), (1,))), 0.0)
-            dquery = mt(dmix, start) + mm(dscores, key)
-            keys_ref[pair] = key
-            slopes_ref[pair] = slopes[1] * scales[1]
-            values_ref[pair] = acts[2]
-            vslopes_ref[pair] = slopes[2]
-            dfresh_ref[pair] = tm(scores, dmix)
-            dkeys_ref[pair] = tm(dscores, query)
-            fresh_ref[pair] = fresh.astype(bf16)
-            along = jnp.sum(query * dquery, axis=-1, keepdims=True)
-            gconv_ref[pl.ds(HALO, length), pl.ds(at, width)] = (
-                slopes[0] * scales[0] * (dquery - query * along)
+            keys_ref[pair] = key[h]
+            slopes_ref[pair] = slopes[h][1] * scales[h][1]
+            values_ref[pair] = acts[h][2]
+            vslopes_ref[pair] = slopes[h][2]
+            dfresh_ref[pair] = dfresh[h]
+            dkeys_ref[pair] = dkeys[h]
+            fresh_ref[pair] = fresh[h].astype(bf16)
+            gconv_ref[pl.ds(HALO, length), pl.ds(at[h], width)] = (
+                slopes[h][0] * scales[h][0] * (dquery[h] - query[h] * along[h])
             )
         unconvolve(s, 0)
 
     def late(s):
+        every = range(heads)
         here = part_of(s, length)
         rate_block = rates_ref[here, :]
-        rate_grads = jnp.zeros((length, LANES), f32)
         lane = lax.broadcasted_iota(jnp.int32, (length, LANES), 1)
-        for h in range(heads):
-            pair = s * heads + h
-            at = h * width
-            rate = column(rate_block, RATE_AT + h)
-            start, after, key, fresh = start_ref[pair], after_ref[pair], keys_ref[pair], fresh_ref[pair]
-            dfresh = dfresh_ref[pair] + mm(key, after)
-            dvalue = tm(inv_ref[pair], dfresh)
-            dkey_in = -mt(dvalue, start)
-            dstrict = jnp.where(row_at > col_at, -mt(dvalue, fresh), 0.0)
-            dprod = rate * dstrict
-            dkey = (
-                dkeys_ref[pair] + mt(fresh, after) + rate * dkey_in + mm(dprod, key) + tm(dprod, key)
-            )
-            drate = jnp.sum(
-                dstrict * mt(key, key) + dvalue * values_ref[pair] + dkey_in * key,
+        rate = [column(rate_block, RATE_AT + h) for h in every]
+        start = [start_ref[s * heads + h] for h in every]
+        after = [after_ref[s * heads + h] for h in every]
+        key = [keys_ref[s * heads + h] for h in every]
+        fresh = [fresh_ref[s * heads + h] for h in every]
+        before = [dfresh_ref[s * heads + h] for h in every]
+        inverse = [inv_ref[s * heads + h] for h in every]
+        dkeys = [dkeys_ref[s * heads + h] for h in every]
+        values = [values_ref[s * heads + h] for h in every]
+        keyed = [slopes_ref[s * heads + h] for h in every]
+        valued = [vslopes_ref[s * heads + h] for h in every]
+        low = [item.astype(bf16) for item in key]
+        dfresh = [b + mm(k, a) for b, k, a in zip(before, low, after)]
+        dvalue = [tm(inv, d) for inv, d in zip(inverse, dfresh)]
+        dvalue_low = [item.astype(bf16) for item in dvalue]
+        products = [mt(k, k) for k in low]
+        outer = [mt(v, a) for v, a in zip(fresh, after)]
+        dkey_in = [-mt(d, st) for d, st in zip(dvalue_low, start)]
+        dstrict = [
+            jnp.where(row_at > col_at, -mt(d, v), 0.0) for d, v in zip(dvalue_low, fresh)
+        ]
+        dprod = [(r * d).astype(bf16) for r, d in zip(rate, dstrict)]
+        forth = [mm(d, k) for d, k in zip(dprod, low)]
+        back = [tm(d, k) for d, k in zip(dprod, low)]
+        dkey = [
+            dkeys[h] + outer[h] + rate[h] * dkey_in[h] + forth[h] + back[h] for h in every
+        ]
+        drate = [
+            jnp.sum(
+                dstrict[h] * products[h] + dvalue[h] * values[h] + dkey_in[h] * key[h],
                 axis=-1,
                 keepdims=True,
             )
-            along = jnp.sum(key * dkey, axis=-1, keepdims=True)
-            gconv_ref[pl.ds(HALO, length), pl.ds(cols + at, width)] = slopes_ref[pair] * (
-                dkey - key * along
+            for h in every
+        ]
+        along = [jnp.sum(k * d, axis=-1, keepdims=True) for k, d in zip(key, dkey)]
+        rate_grads = jnp.zeros((length, LANES), f32)
+        for h in every:
+            at = h * width
+            gconv_ref[pl.ds(HALO, length), pl.ds(cols + at, width)] = keyed[h] * (
+                dkey[h] - key[h] * along[h]
             )
             gconv_ref[pl.ds(HALO, length), pl.ds(2 * cols + at, width)] = (
-                rate * dvalue * vslopes_ref[pair]
+                rate[h] * dvalue[h] * valued[h]
             )
             rate_grads = rate_grads + jnp.where(
-                lane == RATE_AT + h, drate * rate * (1.0 - rate), 0.0
+                lane == RATE_AT + h, drate[h] * rate[h] * (1.0 - rate[h]), 0.0
             )
         unconvolve(s, 1)
         unconvolve(s, 2)
@@ -1209,19 +1347,70 @@
     begins = (ctx_size - 1 - c) // (ctx_size - 1)
 
     final = c // (ctx_size - 1)
-
-    @pl.loop(0, 3 * seqs)
+    block_store = pltpu.make_async_copy(out_ref, block_hbm, store_sem.at[0])
+
+    def halo_of(s):
+        return remote(
+            halo_in.at[1, s], halo_in.at[0, s], halo_send.at[s], halo_recv.at[s], {"ctx": c - 1}
+        )
+
+    def project(i):
+        s = cube2.block_at(i)
+        here = part_of(s, length)
+
+        @pl.when(c < ctx_size - 1)
+        def _():
+            halo_of(s).wait_recv()
+            last = pl.ds(pl.multiple_of(s * length + length - 16, 16), 16)
+            rows = pre_ref[last, : 3 * cols].astype(f32)
+            edge = halo_out[0, s] + halo_in[0, s].astype(f32)
+            pre_ref[last, : 3 * cols] = jnp.concatenate([rows[:HALO], edge], axis=0).astype(bf16)
+
+        @pl.when(i == 0)
+        def _():
+            for name in ("w", "back", "into"):
+                loads[name].wait()
+
+        part = mm(pre_ref[here, 3 * cols :], into_ref[...])
+        for kind in range(3):
+            part = part + mt(pre_ref[here, kind * cols : (kind + 1) * cols], w_ref[kind])
+        src2[here, :] = part.astype(bf16)
+        tail2_src[here, :] = (SCALE * mt(pre_ref[here, :], back_ref[...])).astype(bf16)
+        cube2.send_block(i)
+
+        @pl.when(i < 3)
+        def _():
+            tail2.send_block(s)
+
+        @pl.when(i == 1)
+        def _():
+            cube.done()
+            block_store.start()
+
+        @pl.when(i == 2)
+        def _():
+            block_store.wait()
+            cube2.middle_half(1)
+
+        @pl.when(i == 3)
+        def _():
+            cube2.middle_half(0)
+
+    @pl.loop(0, 3 * seqs + 2)
     def _(k):
         part = k // seqs
-        s = lax.rem(k, seqs)
         odd = lax.rem(k, 2) == seqs % 2
-        later = (1 - begins) * s + begins * lax.rem((k + seqs) // 2, seqs)
+        s = cube2.block_at(lax.rem(k, seqs))
+        later = cube2.block_at(
+            (1 - begins) * lax.rem(k, seqs) + begins * lax.rem((k + seqs) // 2, seqs)
+        )
+        ready = (1 - begins) * (k - 2 * seqs - 1) + begins * ((k + seqs - 3) // 2 - seqs)
 
         @pl.when(k == 2 + 3 * final)
         def _():
             cube.middle()
 
-        @pl.when(k == 4 + 4 * final)
+        @pl.when(k == 4 + 3 * final)
         def _():
             cube.finish(total_ref)
             loads["resid"].wait()
@@ -1233,7 +1422,7 @@
             cube.spread()
             tail.start(1)
 
-        @pl.when(k == 6 + 4 * final)
+        @pl.when(k == 6 + 2 * final)
         def _():
             cube.relay()
 
@@ -1241,60 +1430,42 @@
         def _():
             early(s)
 
-        @pl.when((ends & (part == 0)) | (inside & (part == 1)) | (starts & (part > 0) & odd))
+        @pl.when(
+            (ends & (part == 0)) | (inside & (part == 1)) | (starts & (part > 0) & (part < 3) & odd)
+        )
         def _():
             link(later)
 
-        @pl.when(((ends | inside) & (part == 2)) | (starts & (part > 0) & jnp.logical_not(odd)))
+        @pl.when(
+            ((ends | inside) & (part == 2))
+            | (starts & (part > 0) & (part < 3) & jnp.logical_not(odd))
+        )
         def _():
             late(later)
-
-    halo_in[1] = halo_out[1].astype(bf16)
-    halo = remote(halo_in.at[1], halo_in.at[0], halo_send, halo_recv, {"ctx": c - 1})
+            halo_in[1, later] = halo_out[1, later].astype(bf16)
+
+            @pl.when(c > 0)
+            def _():
+                halo_of(later).start()
+
+        @pl.when(
+            ((ends | inside) & (k > 2 * seqs) & (k < 3 * seqs + 1))
+            | (starts & (k > seqs + 2) & jnp.logical_not(odd))
+        )
+        def _():
+            project(ready)
+
 
     @pl.when(c > 0)
     def _():
-        halo.start()
-
-    @pl.when(c < ctx_size - 1)
-    def _():
-        halo.wait_recv()
-        for s in range(seqs):
-            last = s * length + length - 16
-            block = pre_ref[last : last + 16, : 3 * cols].astype(f32)
-            edge = (halo_out[0, s] + halo_in[0, s].astype(f32))
-            pre_ref[last : last + 16, : 3 * cols] = jnp.concatenate(
-                [block[:HALO], edge], axis=0
-            ).astype(bf16)
-
-    @pl.when(c > 0)
-    def _():
-        halo.wait_send()
-
         @pl.loop(0, seqs)
         def _(s):
-            remote(
-                chain_out.at[s], after_ref.at[pl.ds(0, heads)], chain_send.at[s], chain_recv.at[s],
-                {"ctx": c - 1},
-            ).wait_send()
-
-    for name in ("w", "back", "into"):
-        loads[name].wait()
-    cube.done()
-    block_store = pltpu.make_async_copy(out_ref, block_hbm, store_sem.at[0])
-    block_store.start()
-    tail2_src[...] = (SCALE * mt(pre_ref[...], back_ref[...])).astype(bf16)
-    tail2.start(0)
-
-    def project(half, chunk):
-        rows = cube2.columns(half, chunk)
-        part = mm(pre_ref[:, 3 * cols :], into_ref[:, rows])
-        for i in range(3):
-            part = part + mt(pre_ref[:, i * cols : (i + 1) * cols], w_ref[i, rows, :])
-        src[:, rows] = part.astype(bf16)
-        cube2.start(half, chunk)
-
-    cube2.each(project)
+            halo_of(s).wait_send()
+
+        @pl.loop(0, pairs)
+        def _(pair):
+            hop_of(pair).wait_send()
+
     inner = tail2.total().astype(bf16)
     inner_grad_ref[mine, :] = inner
     tail2.start(1)
@@ -1330,8 +1501,6 @@
         for kind, name in enumerate(("qr", "kr", "vr", "rr")):
             at = core * 32 + kind * 8
             put(name, core, right[at : at + 8, kind * cols : kind * cols + plan[name][1]])
-    block_store.wait()
-    cube2.middle()
     loads["n1"].wait()
     tail2.wait(1)
     left = tm(inner_grad_ref[...], normed_ref[...])
@@ -1342,6 +1511,12 @@
     swap = remote(pack.at[1 - f], mate_in, swap_send, swap_recv, mate)
     swap.start()
     cube2.finish(total_ref)
+    loads["x"].wait()
+    loads["gresid"].wait()
+    grad_first = total_ref[...] + mm(inner, into_ref[...])
+    grad = gresid_ref[...] + norm_back(x_ref[...].astype(f32), gain_ref[...], grad_first)
+    out_ref[mine, :] = grad.astype(bf16)
+    cube2.spread()
     swap.wait_recv()
     both = (pack[f].astype(f32) + mate_in[...].astype(f32)).astype(bf16)
     piece = both.shape[1] // ctx_size
@@ -1366,12 +1541,7 @@
         )
     for copy in sends:
         copy.start()
-    loads["x"].wait()
-    loads["gresid"].wait()
-    grad_first = total_ref[...] + mm(inner, into_ref[...])
-    grad = gresid_ref[...] + norm_back(x_ref[...].astype(f32), gain_ref[...], grad_first)
-    out_ref[mine, :] = grad.astype(bf16)
-    cube2.spread()
+    cube2.relay()
     for copy in sends:
         copy.wait_recv()
     total = mine_ref[c].astype(f32)
@@ -1380,7 +1550,6 @@
     summed[c] = total.astype(bf16)
     for copy in spreads:
         copy.start()
-    cube2.relay()
     for copy in spreads:
         copy.wait_recv()
     for j in range(ctx_size):
@@ -1396,9 +1565,34 @@
     grad_store.wait()
 
 
-def deal_kernel(strips, packed_ref, *outs):
-    for out, (at, wide) in zip(outs, strips):
-        out[...] = packed_ref[:, at : at + wide]
+def deal_kernel(strips, heads, packed_ref, block_in, grad_in, block_out, grad_out, *refs):
+    outs, (block_ref, grad_ref, load_sem, store_sem) = refs[:-4], refs[-4:]
+    count = load_sem.shape[1]
+    size = block_ref.shape[0] // count
+    moves = []
+    for i, (source, middle, target) in enumerate(
+        ((block_in, block_ref, block_out), (grad_in, grad_ref, grad_out))
+    ):
+        for k in range(count):
+            here = pl.ds(k * size, size)
+            load = pltpu.make_async_copy(source.at[here], middle.at[here], load_sem.at[i, k])
+            load.start()
+            moves.append(
+                (load, pltpu.make_async_copy(middle.at[here], target.at[here], store_sem.at[i, k]))
+            )
+    for load, store in moves:
+        load.wait()
+        store.start()
+    for index, (out, (at, wide)) in enumerate(zip(outs, strips)):
+        if index == 7:
+            lanes = lax.broadcasted_iota(jnp.int32, (heads, LANES), 1)
+            rows = lax.broadcasted_iota(jnp.int32, (heads, LANES), 0)
+            pick = jnp.where(lanes == rows + RATE_AT, 1.0, 0.0)
+            out[...] = mt(pick, packed_ref[:, at : at + wide])
+        else:
+            out[...] = packed_ref[:, at : at + wide]
+    for _, store in moves:
+        store.wait()
 
 
 def local(ctx_size, tp_size, *arguments):
@@ -1448,7 +1642,7 @@
     x = hidden_in.reshape(rows, model)
     grad_rows = output_grad.reshape(rows, model)
     rate_from = jnp.pad(rate_right, ((0, 0), (RATE_AT, LANES - RATE_AT - heads)))
-    rate_rows = jnp.pad(rate_weight.T, ((0, 8 - heads), (0, 0)))
+    rate_rows = rate_weight.T
     wides = (
         query_left.T,
         key_left.T,
@@ -1543,25 +1737,25 @@
         + [
             pltpu.VMEM(square, f32),
             pltpu.VMEM((3, model, cols), bf16),
-            pltpu.VMEM((8, model), bf16),
+            pltpu.VMEM((heads, model), bf16),
             pltpu.VMEM((seqs, HALO, 3 * cols), bf16),
             pltpu.VMEM((seqs, HALO, 3 * cols), bf16),
             pltpu.VMEM((LANES, 3 * cols + LANES), f32),
             pltpu.VMEM((LANES, model), f32),
-            pltpu.VMEM((seqs, heads, width, width), bf16),
+            pltpu.VMEM(square, bf16),
             pltpu.VMEM((2,) + output_weight.shape, bf16),
             pltpu.VMEM((2,) + down_weight.shape, bf16),
             pltpu.VMEM((rows, model), bf16),
             DMA((24,)),
             DMA((24,)),
             DMA((20,)),
-            DMA((19,)),
-            DMA,
-            DMA,
+            DMA((20,)),
+            DMA((seqs,)),
+            DMA((seqs,)),
             DMA((4,)),
             DMA,
-            DMA((seqs,)),
-            DMA((seqs,)),
+            DMA((pairs,)),
+            DMA((pairs,)),
         ]
         + cube_scratch(rows, model)
         + tail_scratch(rows, tp_size),
@@ -1609,8 +1803,8 @@
             shape((32, units), f32),
             shape((32, units), f32),
         ),
-        in_specs=[smem] + [VMEM] * 7 + [ANY] * 7,
-        out_specs=(VMEM,) * 8,
+        in_specs=[smem] + [VMEM] * 5 + [ANY] * 9,
+        out_specs=(VMEM, VMEM, ANY, ANY) + (VMEM,) * 4,
         scratch_shapes=[
             pltpu.VMEM((2,) + gate_weight.shape, bf16),
             pltpu.VMEM((2,) + up_weight.shape, bf16),
@@ -1622,7 +1816,13 @@
             pltpu.VMEM((LANES, units), bf16),
             pltpu.VMEM((LANES, units), bf16),
             pltpu.VMEM((block, model), bf16),
-            DMA((3, 2)),
+            pltpu.VMEM((rows, units), f32),
+            pltpu.VMEM((block, model), f32),
+            pltpu.VMEM((block, model), f32),
+            pltpu.VMEM((rows, model), bf16),
+            DMA((3,)),
+            DMA((-(-units // (2 * LANES)), 5)),
+            DMA((2,)),
             DMA,
         ]
         + cube_scratch(rows, model)
@@ -1632,8 +1832,6 @@
     )(
         seq_lengths,
         second,
-        active,
-        residual,
         gain2,
         wide_all,
         slim_all,
@@ -1645,6 +1843,8 @@
         wu,
         down_weight,
         wd,
+        active,
+        residual,
     )
     plan, used = strip_plan(cols, model, units)
     grain = LANES * ctx_size
@@ -1684,7 +1884,7 @@
             pltpu.VMEM((rows, 3 * cols + LANES), bf16),
             pltpu.VMEM(tall, f32),
             pltpu.VMEM(square, bf16),
-            pltpu.VMEM((seqs, heads, width, width), bf16),
+            pltpu.VMEM(square, bf16),
             pltpu.VMEM((HALO + length + HALO, 3 * cols), f32),
             pltpu.VMEM((2, seqs, HALO, 3 * cols), f32),
             pltpu.VMEM((2, seqs, HALO, 3 * cols), bf16),
@@ -1705,10 +1905,10 @@
             pltpu.VMEM((ctx_size, 8, piece), bf16),
             DMA((BACK_LOADS,)),
             DMA((2,)),
+            DMA((pairs,)),
+            DMA((pairs,)),
             DMA((seqs,)),
             DMA((seqs,)),
-            DMA,
-            DMA,
             DMA,
             DMA,
             DMA((2, ctx_size - 1)),
@@ -1716,8 +1916,9 @@
         ]
         + cube_scratch(rows, model)[1:]
         + [DMA((4, 2, CHUNKS, 2)), DMA((4, 2, CHUNKS, 2))]
+        + cube_scratch(rows, model)[:4]
         + tail_scratch(rows, tp_size)[1:] * 2,
-        compiler_params=params(3),
+        compiler_params=params(3, 60 << 20),
         name="back",
     )(
         seq_lengths,
@@ -1760,17 +1961,25 @@
         wo,
     )
     strips = tuple(plan.values())
-    shares = list(
-        pl.pallas_call(
-            functools.partial(deal_kernel, strips),
-            out_shape=tuple(shape((8, wide), f32) for _, wide in strips),
-            in_specs=[VMEM],
-            out_specs=(VMEM,) * len(strips),
-            name="deal",
-        )(packed)
-    )
-    shares[7] = shares[7][:, RATE_AT : RATE_AT + heads]
-    lefts = (0, 2, 4, 6, 8, 10, 12, 14)
+    dealt = pl.pallas_call(
+        functools.partial(deal_kernel, strips, heads),
+        out_shape=(shape((rows, model), bf16),) * 2
+        + tuple(
+            shape((heads, 8) if i == 7 else (8, wide), f32) for i, (_, wide) in enumerate(strips)
+        ),
+        in_specs=[VMEM, ANY, ANY],
+        out_specs=(ANY, ANY) + (VMEM,) * len(strips),
+        scratch_shapes=[
+            pltpu.VMEM((rows, model), bf16),
+            pltpu.VMEM((rows, model), bf16),
+            DMA((2, 4)),
+            DMA((2, 4)),
+        ],
+        name="deal",
+    )(packed, block_out, input_grad)
+    block_out, input_grad = dealt[:2]
+    shares = list(dealt[2:])
+    lefts = (0, 2, 4, 6, 7, 8, 10, 12, 14)
     shares = [item.T if i in lefts else item for i, item in enumerate(shares)]
     return (
         block_out.reshape(seqs, length, model),

time: 259 us -> 239 us (0.923)
  Pallas kernels: 249 us -> 236 us
  local copies, waits for them, and re-layouts: 8.77 us -> 1.42 us
    pallas_call x1, Pallas kernels: 81.4 us -> 72.4 us  [local(): pl.pallas_call(functools.partial(mixer_kernel, mixer_sizes), out_shape=(s...]
    unnamed x6 -> x1, local copies, waits for them, and re-layouts: 6.05 us -> 0.77 us
    pallas_call x1, Pallas kernels: 61 us -> 56.8 us  [local(): pl.pallas_call(functools.partial(feed_kernel, (seqs, length, cols, ctx_si...]
    pallas_call x1, Pallas kernels: 1.98 us -> 5.56 us  [local(): pl.pallas_call(functools.partial(deal_kernel, strips, heads), out_shape=(...]
    pallas_call x1, Pallas kernels: 104 us -> 101 us  [local(): pl.pallas_call(functools.partial(back_kernel, mixer_sizes), out_shape=(sh...]
where the time goes in v3:
time: 239 us; the launch traced here: 238 us
  Pallas kernels  236 us (99%)
    pallas_call x1, Pallas kernels, local(): pl.pallas_call(functools.partial(back_kernel, mixer_sizes), out_shape=(sh...  101 us
    pallas_call x1, Pallas kernels, local(): pl.pallas_call(functools.partial(mixer_kernel, mixer_sizes), out_shape=(s...  72.4 us
    pallas_call x1, Pallas kernels, local(): pl.pallas_call(functools.partial(feed_kernel, (seqs, length, cols, ctx_si...  56.8 us
    pallas_call x1, Pallas kernels, local(): pl.pallas_call(functools.partial(deal_kernel, strips, heads), out_shape=(...  5.56 us

profile of v3, /device:TPU:0, one launch (start us, length us, event | category | flops | bytes accessed | tf_op | source)
XLA Modules:
  0.0 238.2 jit_solution(12670684771100375062)
XLA Ops:
  0.7 0.8 copy.51
  1.4 0.7 pad.4.slim3
  2.1 72.4 %mixer.1 = (bf16[512,2048]{1,0:T(8,128)(2,1)}, bf16[512,128]{1,0:T(8,128)(2,1)}, f32[128,2048]{1,0:T(8,128)}, bf16[512,1024]{1,0:T(8,128)(2,1)}, bf16[1024,1408]...) custom-call(s32[4]{0:T(128)} %lens_ref.5, ...), custom_call_target="tpu_custom_call" | custom-call | tf_op jit(solution)/shard_map/mixer/pallas_call | solution.py:1721
  74.5 56.8 %feed.1 = (bf16[512,2048]{1,0:T(8,128)(2,1)}, bf16[512,128]{1,0:T(8,128)(2,1)}, f32[128,2048]{1,0:T(8,128)}, bf16[512,2048]{1,0:T(8,128)(2,1)}, bf16[512,128]{1,...) custom-call(s32[4]{0:T(128)} %lens_ref.5, ...), custom_call_target="tpu_custom_call" | custom-call | tf_op jit(solution)/shard_map/feed/pallas_call | solution.py:1794
  131.4 101.1 %back.1 = (bf16[512,2048]{1,0:T(8,128)(2,1)}, bf16[512,2048]{1,0:T(8,128)(2,1)}, f32[8,23040]{1,0:T(8,128)}) custom-call(s32[4]{0:T(128)} %lens_ref.5, bf16[512,2048]{1,0:T(8,128)(2,1)} %get-tuple-element.82.low_ref, f32[1,128]{1,0:T(1,128)} %bitcast.44, f32[1,2048]{1,0:T(1,128)} %bitcast.39, f32[4,512]{1,0:T(4,128)} %qtaps_ref.3, f32[4,512]{1,0:T(4,128)} %ktaps_ref.3, ...), custom_call_target="tpu_custom_call" | custom-call | tf_op jit(solution)/shard_map/back/pallas_call | solution.py:1853
  232.5 5.6 %deal.1 = (bf16[512,2048]{1,0:T(8,128)(2,1)}, bf16[512,2048]{1,0:T(8,128)(2,1)}, f32[8,2048]{1,0:T(8,128)}, f32[8,512]{1,0:T(8,128)}, f32[8,2048]{1,0:T(8,128)},...) custom-call(f32[8,23040]{1,0:T(8,128)} %get-tuple-element.107.packed, ...), custom_call_target="tpu_custom_call" | custom-call | tf_op jit(solution)/shard_map/deal/pallas_call | solution.py:1964

commit v4 on v3

--- a/solution.py
+++ b/solution.py
@@ -104,19 +104,19 @@
     )
 
 
-def greet(barrier, peers):
-    count = 0
-    for peer, condition in peers:
+def greet(barrier, peers, later=(), expected=0):
+    count = expected
+    for peer, condition in list(peers) + list(later):
 
         def tell(peer=peer):
             pl.semaphore_signal(barrier, inc=1, device_id=peer, device_id_type=MESH)
 
         if condition is None:
             tell()
-            count = count + 1
         else:
             pl.when(condition)(tell)
-            count = count + jnp.where(condition, 1, 0)
+    for peer, condition in peers:
+        count = count + (1 if condition is None else jnp.where(condition, 1, 0))
     pl.semaphore_wait(barrier, count)
 
 
@@ -273,11 +273,18 @@
 
         self.each(body)
 
-    def done(self):
+    def first_sent(self):
+        def body(half, chunk):
+            for j in range(2):
+                self.copy(0, half, chunk, j).wait_send()
+
+        self.each(body)
+
+    def done(self, since=0):
         def body(half, chunk):
             for j in range(2):
                 self.copy(3, half, chunk, j).wait_recv()
-            for stage in range(4):
+            for stage in range(since, 4):
                 for j in range(2 if stage in (0, 3) else 1):
                     self.copy(stage, half, chunk, j).wait_send()
 
@@ -408,6 +415,7 @@
     qtaps_ref,
     ktaps_ref,
     vtaps_ref,
+    rate_from_ref,
     wq_ref,
     wk_ref,
     wv_ref,
@@ -423,7 +431,6 @@
     slim0,
     slim1,
     slim2,
-    slim3,
     slim4,
     slim5,
     slim6,
@@ -488,6 +495,7 @@
     wo_ref,
     wd_ref,
     grad_ref,
+    slim3,
     send_sem,
     recv_sem,
     local_sem,
@@ -530,6 +538,14 @@
             stores.append(copy)
 
     top = pl.ds(pl.multiple_of(f * half, half), half)
+    rows, lanes = grid_of(8)
+    wide_lanes = lax.broadcasted_iota(jnp.int32, (8, LANES), 1)
+    spread = jnp.zeros((8, LANES), f32)
+    for h in range(heads):
+        row = jnp.broadcast_to(rate_from_ref[h : h + 1, :].astype(f32), (8, 8))
+        turned = jnp.sum(jnp.where(rows == lanes, row, 0.0), axis=1, keepdims=True)
+        spread = spread + jnp.where(wide_lanes == RATE_AT + h, turned, 0.0)
+    slim3[...] = spread.astype(bf16)
     moves = []
     for i, ref in enumerate((wide0, wide1, wide2, wide3, wide4, wide5, wide6, wide7)):
         moves.append((ref, wide_out.at[f, i]))
@@ -1140,13 +1156,13 @@
     fetch("grad", grad_hbm, grad_ref)
     greet(
         pltpu.get_barrier_semaphore(),
-        [(mate, None)]
-        + [({"ctx": lax.rem(c + 1 + i, ctx_size)}, None) for i in range(ctx_size - 1)]
-        + tp_peers(t, tp_size),
+        [(mate, None)] + tp_peers(t, tp_size),
+        [({"ctx": c + 1 + i}, c + 1 + i < ctx_size) for i in range(ctx_size - 1)],
+        c,
     )
     cube = Cube(t, src, out_ref, first, second, held, cube_send, cube_recv, CHUNKS)
     tail = Tail(t, tail_src, down_inner_ref, tail_got, tail_send, tail_recv, tp_size)
-    cube2 = Cube(t, src2, out_ref, first2, second2, held2, cube2_send, cube2_recv, CHUNKS)
+    cube2 = Cube(t, src2, src, first2, second2, held2, cube2_send, cube2_recv, CHUNKS)
     tail2 = Tail(t, tail2_src, inner_grad_ref, tail2_got, tail2_send, tail2_recv, tp_size)
 
     def put(name, core, rows):
@@ -1382,14 +1398,8 @@
         def _():
             tail2.send_block(s)
 
-        @pl.when(i == 1)
-        def _():
-            cube.done()
-            block_store.start()
-
         @pl.when(i == 2)
         def _():
-            block_store.wait()
             cube2.middle_half(1)
 
         @pl.when(i == 3)
@@ -1406,13 +1416,14 @@
         )
         ready = (1 - begins) * (k - 2 * seqs - 1) + begins * ((k + seqs - 3) // 2 - seqs)
 
-        @pl.when(k == 2 + 3 * final)
+        @pl.when(k == 4 + 4 * final)
         def _():
             cube.middle()
 
-        @pl.when(k == 4 + 3 * final)
+        @pl.when(k == 7 + 3 * final)
         def _():
             cube.finish(total_ref)
+            cube.first_sent()
             loads["resid"].wait()
             inner = tail.total().astype(bf16)
             right = stacked([wide_ref[core, 7] for core in range(2)])
@@ -1422,7 +1433,7 @@
             cube.spread()
             tail.start(1)
 
-        @pl.when(k == 6 + 2 * final)
+        @pl.when(k == 9 + 3 * final)
         def _():
             cube.relay()
 
@@ -1515,8 +1526,10 @@
     loads["gresid"].wait()
     grad_first = total_ref[...] + mm(inner, into_ref[...])
     grad = gresid_ref[...] + norm_back(x_ref[...].astype(f32), gain_ref[...], grad_first)
-    out_ref[mine, :] = grad.astype(bf16)
+    src[mine, :] = grad.astype(bf16)
     cube2.spread()
+    cube.done(1)
+    block_store.start()
     swap.wait_recv()
     both = (pack[f].astype(f32) + mate_in[...].astype(f32)).astype(bf16)
     piece = both.shape[1] // ctx_size
@@ -1555,18 +1568,19 @@
     for j in range(ctx_size):
         packed_ref[:, j * piece : (j + 1) * piece] = summed[j].astype(f32)
     cube2.done()
-    grad_store = pltpu.make_async_copy(out_ref, input_grad_hbm, store_sem.at[1])
+    grad_store = pltpu.make_async_copy(src, input_grad_hbm, store_sem.at[1])
     grad_store.start()
     swap.wait_send()
     for copy in sends + spreads:
         copy.wait_send()
     tail.done()
     tail2.done()
+    block_store.wait()
     grad_store.wait()
 
 
-def deal_kernel(strips, heads, packed_ref, block_in, grad_in, block_out, grad_out, *refs):
-    outs, (block_ref, grad_ref, load_sem, store_sem) = refs[:-4], refs[-4:]
+def deal_kernel(strips, heads, packed_hbm, block_in, grad_in, block_out, grad_out, *refs):
+    outs, (block_ref, grad_ref, packed_ref, load_sem, store_sem, packed_sem) = refs[:-6], refs[-6:]
     count = load_sem.shape[1]
     size = block_ref.shape[0] // count
     moves = []
@@ -1580,9 +1594,12 @@
             moves.append(
                 (load, pltpu.make_async_copy(middle.at[here], target.at[here], store_sem.at[i, k]))
             )
+    packed_load = pltpu.make_async_copy(packed_hbm, packed_ref, packed_sem)
+    packed_load.start()
     for load, store in moves:
         load.wait()
         store.start()
+    packed_load.wait()
     for index, (out, (at, wide)) in enumerate(zip(outs, strips)):
         if index == 7:
             lanes = lax.broadcasted_iota(jnp.int32, (heads, LANES), 1)
@@ -1641,7 +1658,6 @@
     pairs = seqs * heads
     x = hidden_in.reshape(rows, model)
     grad_rows = output_grad.reshape(rows, model)
-    rate_from = jnp.pad(rate_right, ((0, 0), (RATE_AT, LANES - RATE_AT - heads)))
     rate_rows = rate_weight.T
     wides = (
         query_left.T,
@@ -1657,13 +1673,12 @@
         query_right,
         key_right,
         value_right,
-        rate_from,
         output_left.T,
         gate_right,
         up_right,
         down_left.T,
     )
-    slim_wide = sum(item.shape[1] for item in slims)
+    slim_wide = LANES + sum(item.shape[1] for item in slims)
     gain1, gain2, gain3 = mixer_gain[None, :], feed_gain[None, :], head_gain[None, :]
     ext = length + HALO
     square = (pairs, width, width)
@@ -1731,7 +1746,7 @@
             shape((3, model, cols), bf16),
         )
         + kept_shapes,
-        in_specs=[smem] + [VMEM] * 7 + [ANY] * 25,
+        in_specs=[smem] + [VMEM] * 8 + [ANY] * 24,
         out_specs=(VMEM,) * 3 + (ANY,) * (5 + len(kept_shapes)),
         scratch_shapes=[pltpu.VMEM(item.shape, item.dtype) for item in kept_shapes]
         + [
@@ -1746,6 +1761,7 @@
             pltpu.VMEM((2,) + output_weight.shape, bf16),
             pltpu.VMEM((2,) + down_weight.shape, bf16),
             pltpu.VMEM((rows, model), bf16),
+            pltpu.VMEM((8, LANES), bf16),
             DMA((24,)),
             DMA((24,)),
             DMA((20,)),
@@ -1770,6 +1786,7 @@
         query_conv,
         key_conv,
         value_conv,
+        rate_right.T,
         query_weight,
         key_weight,
         value_weight,
@@ -1967,13 +1984,15 @@
         + tuple(
             shape((heads, 8) if i == 7 else (8, wide), f32) for i, (_, wide) in enumerate(strips)
         ),
-        in_specs=[VMEM, ANY, ANY],
+        in_specs=[ANY, ANY, ANY],
         out_specs=(ANY, ANY) + (VMEM,) * len(strips),
         scratch_shapes=[
             pltpu.VMEM((rows, model), bf16),
             pltpu.VMEM((rows, model), bf16),
+            pltpu.VMEM((8, total_wide), f32),
             DMA((2, 4)),
             DMA((2, 4)),
+            DMA,
         ],
         name="deal",
     )(packed, block_out, input_grad)

time: 239 us -> 235 us (0.983)
  no operation moved by 1% of the time
where the time goes in v4:
time: 235 us
  Pallas kernels  234 us (100%)
    pallas_call x1, Pallas kernels, local(): pl.pallas_call(functools.partial(back_kernel, mixer_sizes), out_shape=(sh...  100 us
    pallas_call x1, Pallas kernels, local(): pl.pallas_call(functools.partial(mixer_kernel, mixer_sizes), out_shape=(s...  72.6 us
    pallas_call x1, Pallas kernels, local(): pl.pallas_call(functools.partial(feed_kernel, (seqs, length, cols, ctx_si...  56.9 us

profile of v4, /device:TPU:0, one launch (start us, length us, event | category | flops | bytes accessed | tf_op | source)
XLA Modules:
  0.0 235.2 jit_solution(993535545918339759)
XLA Ops:
  0.7 72.6 %mixer.1 = (bf16[512,2048]{1,0:T(8,128)(2,1)}, bf16[512,128]{1,0:T(8,128)(2,1)}, f32[128,2048]{1,0:T(8,128)}, bf16[512,1024]{1,0:T(8,128)(2,1)}, bf16[1024,1408]...) custom-call(s32[4]{0:T(128)} %lens_ref.5, ...), custom_call_target="tpu_custom_call" | custom-call | tf_op jit(solution)/shard_map/mixer/pallas_call | solution.py:1736
  73.3 56.9 %feed.1 = (bf16[512,2048]{1,0:T(8,128)(2,1)}, bf16[512,128]{1,0:T(8,128)(2,1)}, f32[128,2048]{1,0:T(8,128)}, bf16[512,2048]{1,0:T(8,128)(2,1)}, bf16[512,128]{1,...) custom-call(s32[4]{0:T(128)} %lens_ref.5, ...), custom_call_target="tpu_custom_call" | custom-call | tf_op jit(solution)/shard_map/feed/pallas_call | solution.py:1811
  130.2 100.2 %back.1 = (bf16[512,2048]{1,0:T(8,128)(2,1)}, bf16[512,2048]{1,0:T(8,128)(2,1)}, f32[8,23040]{1,0:T(8,128)}) custom-call(s32[4]{0:T(128)} %lens_ref.5, bf16[512,2048]{1,0:T(8,128)(2,1)} %get-tuple-element.82.low_ref, f32[1,128]{1,0:T(1,128)} %bitcast.45, f32[1,2048]{1,0:T(1,128)} %bitcast.40, f32[4,512]{1,0:T(4,128)} %qtaps_ref.3, f32[4,512]{1,0:T(4,128)} %ktaps_ref.3, ...), custom_call_target="tpu_custom_call" | custom-call | tf_op jit(solution)/shard_map/back/pallas_call | solution.py:1870
  230.4 4.6 %deal.1 = (bf16[512,2048]{1,0:T(8,128)(2,1)}, bf16[512,2048]{1,0:T(8,128)(2,1)}, f32[8,2048]{1,0:T(8,128)}, f32[8,512]{1,0:T(8,128)}, f32[8,2048]{1,0:T(8,128)},...) custom-call(f32[8,23040]{1,0:T(8,128)} %get-tuple-element.107.packed, ...), custom_call_target="tpu_custom_call" | custom-call | tf_op jit(solution)/shard_map/deal/pallas_call | solution.py:1981

commit v5 on v4

--- a/solution.py
+++ b/solution.py
@@ -348,7 +348,7 @@
                 copy.wait_send()
 
 
-CHUNKS = 4
+CHUNKS = 2
 
 
 def cube_scratch(rows, model):
@@ -733,8 +733,12 @@
         def _():
             cube.middle_half(0)
 
-    @pl.loop(0, seqs + ctx_size - 1)
+    @pl.loop(0, seqs + ctx_size)
     def _(k):
+        @pl.when((k > c) & (k < c + seqs + 1))
+        def _():
+            project(k - c - 1)
+
         @pl.when(k < seqs)
         def _():
             solve(cube.block_at(k))
@@ -742,7 +746,6 @@
         @pl.when((k >= c) & (k < c + seqs))
         def _():
             link(cube.block_at(k - c))
-            project(k - c)
 
     store(
         [

time: 235 us -> 235 us (level)
  no operation moved by 1% of the time
where the time goes in v5:
time: 235 us; the launch traced here: 234 us
  Pallas kernels  233 us (99%)
    pallas_call x1, Pallas kernels, local(): pl.pallas_call(functools.partial(back_kernel, mixer_sizes), out_shape=(sh...  98.8 us
    pallas_call x1, Pallas kernels, local(): pl.pallas_call(functools.partial(mixer_kernel, mixer_sizes), out_shape=(s...  72.3 us
    pallas_call x1, Pallas kernels, local(): pl.pallas_call(functools.partial(feed_kernel, (seqs, length, cols, ctx_si...  57.3 us

profile of v5, /device:TPU:0, one launch (start us, length us, event | category | flops | bytes accessed | tf_op | source)
XLA Modules:
  0.0 233.9 jit_solution(1623567666290379260)
XLA Ops:
  0.7 72.3 %mixer.1 = (bf16[512,2048]{1,0:T(8,128)(2,1)}, bf16[512,128]{1,0:T(8,128)(2,1)}, f32[128,2048]{1,0:T(8,128)}, bf16[512,1024]{1,0:T(8,128)(2,1)}, bf16[1024,1408]...) custom-call(s32[4]{0:T(128)} %lens_ref.5, ...), custom_call_target="tpu_custom_call" | custom-call | tf_op jit(solution)/shard_map/mixer/pallas_call | solution.py:1739
  73.0 57.3 %feed.1 = (bf16[512,2048]{1,0:T(8,128)(2,1)}, bf16[512,128]{1,0:T(8,128)(2,1)}, f32[128,2048]{1,0:T(8,128)}, bf16[512,2048]{1,0:T(8,128)(2,1)}, bf16[512,128]{1,...) custom-call(s32[4]{0:T(128)} %lens_ref.5, ...), custom_call_target="tpu_custom_call" | custom-call | tf_op jit(solution)/shard_map/feed/pallas_call | solution.py:1814
  130.3 98.8 %back.1 = (bf16[512,2048]{1,0:T(8,128)(2,1)}, bf16[512,2048]{1,0:T(8,128)(2,1)}, f32[8,23040]{1,0:T(8,128)}) custom-call(s32[4]{0:T(128)} %lens_ref.5, bf16[512,2048]{1,0:T(8,128)(2,1)} %get-tuple-element.82.low_ref, f32[1,128]{1,0:T(1,128)} %bitcast.45, f32[1,2048]{1,0:T(1,128)} %bitcast.40, f32[4,512]{1,0:T(4,128)} %qtaps_ref.3, f32[4,512]{1,0:T(4,128)} %ktaps_ref.3, ...), custom_call_target="tpu_custom_call" | custom-call | tf_op jit(solution)/shard_map/back/pallas_call | solution.py:1873
  229.1 4.6 %deal.1 = (bf16[512,2048]{1,0:T(8,128)(2,1)}, bf16[512,2048]{1,0:T(8,128)(2,1)}, f32[8,2048]{1,0:T(8,128)}, f32[8,512]{1,0:T(8,128)}, f32[8,2048]{1,0:T(8,128)},...) custom-call(f32[8,23040]{1,0:T(8,128)} %get-tuple-element.107.packed, ...), custom_call_target="tpu_custom_call" | custom-call | tf_op jit(solution)/shard_map/deal/pallas_call | solution.py:1984
